TPU v7x, 256 devices: a whole 4x4x8 slice. The times are simulated.
256 devices in a mesh: dap: 128 (over y, x_lo, z, core), ch: 2 (over x_hi).
Axes of the slice: x: 4 (x_hi: 2, x_lo: 2; x = x_hi * 2 + x_lo), y: 4, z: 8, core: 2. Of those that a mesh axis runs over, the one named last changes fastest.
Arguments:
- alignment_embedding: bfloat16 [128, 512, 256], P(None, 'dap'), may hold values from -6 to 6
- couple_embedding: bfloat16 [512, 512, 128], P('dap', 'ch'), may hold values from -6 to 6
- tensor_first_matrix: bfloat16 [256, 32], P(None, 'ch'), may hold values from -0.375 to 0.375
- tensor_second_matrix: bfloat16 [256, 32], replicated, may hold values from -0.375 to 0.375
- tensor_final_matrix: bfloat16 [1024, 128], P('ch'), may hold values from -1 to 1
- trimul_entry_matrix: bfloat16 [4, 128, 128], replicated, may hold values from -0.5 to 0.5
- trimul_sigmoid_matrix: bfloat16 [128, 128], replicated, may hold values from -0.5 to 0.5
- trimul_final_matrix: bfloat16 [128, 128], replicated, may hold values from -0.5 to 0.5
Outputs:
- pair_out: bfloat16 [512, 512, 128], P('dap', 'ch')
All inputs are finite; a program needn't handle non-finite values.
Results may differ from a plain program's by a relative error of at most 0.014.
Values may be sent and summed in bfloat16 or wider, within the bound.
No kernel may reach another device: no remote copies, remote signals or barrier semaphores. Data moves between devices by JAX's collectives and lax.ppermute only.
A program may use at most 64 MiB of HBM per device.

v0:
```python
import jax
import jax.numpy as jnp
from jax import lax
from jax.sharding import Mesh
from jax.sharding import PartitionSpec as P

DAP = ("dap_0", "dap_1", "dap_2", "dap_3")


def from_everyone(x, axis):
    copies = jnp.broadcast_to(x, (lax.axis_size(axis), *x.shape))
    return lax.all_to_all(copies, axis, split_axis=0, concat_axis=0, tiled=True)


def in_order(pieces, dim):
    dims = list(pieces.shape[1:])
    dims[dim] *= pieces.shape[0]
    return jnp.moveaxis(pieces, 0, dim).reshape(dims)


def gathered_by_axis(x, axes, dim):
    far, near = axes
    initial = from_everyone(x, far)
    pieces = jnp.swapaxes(from_everyone(initial, near), 0, 1)
    return in_order(pieces.reshape(-1, *x.shape), dim)


def one_gather(arrays, axis, dims):
    vector = jnp.concatenate([a.reshape(-1) for a in arrays])
    lines, at, gathered = (lax.all_gather(vector, axis), 0, [])
    for a, dim in zip(arrays, dims):
        pieces = lines[:, at : at + a.size].reshape(-1, *a.shape)
        gathered.append(in_order(pieces, dim))
        at += a.size
    return tuple(gathered)


def side_by_side(arrays, axis, split_dim, concat_dim, along):
    both = jnp.concatenate(arrays, axis=along)
    whole, at, gathered = (
        lax.all_to_all(both, axis, split_axis=split_dim, concat_axis=concat_dim, tiled=True),
        0,
        [],
    )
    for a in arrays:
        gathered.append(lax.slice_in_dim(whole, at, at + a.shape[along], axis=along))
        at += a.shape[along]
    return tuple(gathered)


def split_up(x, dim, count):
    dims = x.shape
    pieces = x.reshape(*dims[:dim], count, dims[dim] // count, *dims[dim + 1 :])
    return jnp.moveaxis(pieces, dim, 0)


def summed_on_arrival(x, axis, dim):
    count = lax.axis_size(axis)
    pieces = lax.all_to_all(split_up(x, dim, count), axis, 0, 0, tiled=True)
    return jnp.sum(pieces.astype(jnp.float32), axis=0)


def standardize_fn(value, axis):
    mean = jnp.mean(value, axis=axis, keepdims=True)
    centred = value - mean
    var = jnp.mean(centred * centred, axis=axis, keepdims=True)
    return centred * lax.rsqrt(var + 1e-05)


def outer_update(first_operand, right_rows, w_out, alignment_height):
    rows = first_operand.shape[1]
    outer = jnp.einsum(
        "sic,sje->ijce", first_operand, right_rows, preferred_element_type=jnp.float32
    )
    outer = (outer * (1.0 / alignment_height)).astype(jnp.bfloat16)
    outer = outer.reshape(rows, right_rows.shape[1], first_operand.shape[2] * right_rows.shape[2])
    return jnp.einsum("ijf,fz->ijz", outer, w_out, preferred_element_type=jnp.float32)


def per_device(
    alignment_embedding,
    couple_embedding,
    tensor_first_matrix,
    tensor_second_matrix,
    tensor_final_matrix,
    trimul_entry_matrix,
    trimul_sigmoid_matrix,
    trimul_final_matrix,
):
    alignment_height = alignment_embedding.shape[0]
    columns = couple_embedding.shape[1]
    alignment_standardized = standardize_fn(alignment_embedding.astype(jnp.float32), -1).astype(
        jnp.bfloat16
    )
    second_operand = jnp.einsum(
        "ziv,vl->zil",
        alignment_standardized,
        tensor_second_matrix,
        preferred_element_type=jnp.float32,
    ).astype(jnp.bfloat16)
    right_all = gathered_by_axis(second_operand, (("dap_0", "dap_1", "dap_2"), "dap_3"), 1)
    full_a, full_out = one_gather((tensor_first_matrix, tensor_final_matrix), "ch", (1, 0))
    first_operand = jnp.einsum(
        "ziv,vl->zil", alignment_standardized, full_a, preferred_element_type=jnp.float32
    ).astype(jnp.bfloat16)
    own_right = lax.dynamic_slice_in_dim(right_all, lax.axis_index("ch") * columns, columns, 1)
    update = outer_update(first_operand, own_right, full_out, alignment_height)
    lifted = (couple_embedding.astype(jnp.float32) + update).astype(jnp.bfloat16)
    normed = standardize_fn(lifted.astype(jnp.float32), -1).astype(jnp.bfloat16)
    projected = jnp.einsum(
        "rkz,qzc->qcrk", normed, trimul_entry_matrix, preferred_element_type=jnp.float32
    )
    left_t = (jax.nn.sigmoid(projected[0]) * projected[1]).astype(jnp.bfloat16)
    right_t = (jax.nn.sigmoid(projected[2]) * projected[3]).astype(jnp.bfloat16)
    left_cols, right_cols = side_by_side((left_t, right_t), DAP, 0, 1, 2)
    product = jnp.einsum("cik,cjk->cij", left_cols, right_cols, preferred_element_type=jnp.float32)
    summed = summed_on_arrival(product.astype(jnp.bfloat16), "ch", 2)
    mixed = lax.all_to_all(
        summed.astype(jnp.bfloat16), DAP, split_axis=1, concat_axis=0, tiled=True
    )
    tri_n = standardize_fn(mixed.astype(jnp.float32), 0).astype(jnp.bfloat16)
    out = jnp.einsum("crj,cz->rjz", tri_n, trimul_final_matrix, preferred_element_type=jnp.float32)
    gate = jax.nn.sigmoid(
        jnp.einsum("rjz,zy->rjy", normed, trimul_sigmoid_matrix, preferred_element_type=jnp.float32)
    )
    return (lifted.astype(jnp.float32) + gate * out).astype(jnp.bfloat16)


def solution(mesh):
    torus = Mesh(
        mesh.devices.reshape(4, 2, 8, 2, mesh.shape["ch"]),
        ("dap_0", "dap_1", "dap_2", "dap_3", "ch"),
    )
    return jax.shard_map(
        per_device,
        mesh=torus,
        in_specs=(
            P(None, DAP, None),
            P(DAP, "ch", None),
            P(None, "ch"),
            P(),
            P("ch", None),
            P(),
            P(),
            P(),
        ),
        out_specs=P(DAP, "ch", None),
        check_vma=False,
    )
```

profile of v0, /device:TPU:8, one launch (start us, length us, event | category | flops | bytes accessed | tf_op | source)
XLA Modules:
  0.0 160.3 jit_solution(10743161168091681936)
XLA Ops:
  0.0 1.2 convert_reduce_fusion
  1.2 1.3 fusion.14
  2.6 1.3 fusion.15
  3.9 0.9 convolution_convert_fusion.2
  4.8 1.9 %broadcast_in_dim.4 = bf16[64,128,4,32]{1,3,2,0:T(8,128)(2,1)} broadcast(bf16[128,4,32]{0,2,1:T(8,128)(2,1)S(1)} %convolution_convert_fusion.2), dimensions={1,2,3} | broadcast | bytes 2129920 | tf_op jit(solution)/shard_map/broadcast_in_dim | solution.py:11
  6.7 13.2 %all-to-all-start = ((bf16[64,128,4,32]{1,3,2,0:T(8,128)(2,1)}), bf16[64,128,4,32]{1,3,2,0:T(8,128)(2,1)S(1)}, u32[]{:S(2)}, u32[]{:S(2)}) async-start(bf16[64,128,4,32]{1,3,2,0:T(8,128)(2,1)} %broadcast_in_dim.4), calls=%async_computation | async-start | bytes 4194304 | tf_op jit(solution)/shard_map/all_to_all | solution.py:12
  20.1 11.4 %all-gather = bf16[139264]{0:T(1024)(128)(2,1)S(1)} all-gather(bf16[69632]{0:T(1024)(128)(2,1)S(1)} %pad_maximum_fusion.1), channel_id=2, replica_groups=mesh['dap_0'=4,'dap_1'=2,'dap_2'=8,'dap_3'=2,'ch'=2] {'ch'}, dimensions={0}, use_global_device_ids=true | all-gather | bytes 417792 | tf_op jit(solution)/shard_map/all_gather | solution.py:30
  32.4 38.0 %all-to-all-done = bf16[64,128,4,32]{1,3,2,0:T(8,128)(2,1)S(1)} async-done(((bf16[64,128,4,32]{1,3,2,0:T(8,128)(2,1)}), bf16[64,128,4,32]{1,3,2,0:T(8,128)(2,1)S(1)}, u32[]{:S(2)}, u32[]{:S(2)}) %all-to-all-start) | async-done | bytes 2097184 | tf_op jit(solution)/shard_map/all_to_all | solution.py:12
  70.3 1.1 broadcast_in_dim.5
  71.4 7.1 %all_to_all.36 = bf16[2,64,128,4,32]{2,4,3,1,0:T(8,128)(2,1)S(1)} all-to-all(bf16[2,64,128,4,32]{2,4,3,1,0:T(8,128)(2,1)S(1)} %broadcast_in_dim.5), channel_id=1, replica_groups=mesh['dap_0'=4,'dap_1'=2,'dap_2'=8,'dap_3'=2,'ch'=2] {'dap_3'}, dimensions={0} | all-to-all | bytes 8388608 | tf_op jit(solution)/shard_map/all_to_all | solution.py:12
  78.5 1.6 copy.42
  80.1 1.7 %constant_dynamic-slice_fusion = bf16[128,256,32]{0,2,1:T(8,128)(2,1)} fusion(bf16[128,512,32]{0,2,1:T(8,128)(2,1)S(1)} %bitcast.117, s32[]{:T(128)S(6)} %select_n.3), kind=kLoop, calls=%fused_computation.67 | loop fusion | bytes 4194308 | tf_op jit(solution)/shard_map/dynamic_slice | solution.py:106
  81.8 3.0 %copy.75 = bf16[128,256,32]{1,0,2:T(8,128)(2,1)S(1)} copy(bf16[128,256,32]{0,2,1:T(8,128)(2,1)} %constant_dynamic-slice_fusion) | data formatting | bytes 4194304
  84.8 2.2 %fusion.1 = bf16[4,256,32,32]{1,2,0,3:T(8,128)(2,1)} fusion(bf16[128,256,32]{1,0,2:T(8,128)(2,1)S(1)} %copy.75, bf16[256,32,1]{0,1,2:T(8,128)(2,1)S(1)} %bitcast.124, bf16[128,4,256]{2,1,0:T(4,128)(2,1)S(1)} %fusion.15), kind=kOutput, calls=%fused_computation.2 | convolution fusion | flops 278937600 | bytes 4472832 | tf_op jit(solution)/shard_map/sic,sje->ijce/dot_general | solution.py:72
  87.0 2.8 %copy.47 = bf16[4,256,32,32]{1,3,2,0:T(8,128)(2,1)S(1)} copy(bf16[4,256,32,32]{1,2,0,3:T(8,128)(2,1)} %fusion.1) | data formatting | bytes 4194304 | tf_op jit(solution)/shard_map/convert_element_type | solution.py:75
  89.8 0.5 fusion.40
  91.7 25.8 %all_to_all.37 = bf16[128,4,512]{2,1,0:T(4,128)(2,1)S(1)} all-to-all(bf16[128,4,512]{2,1,0:T(4,128)(2,1)S(1)} %copy.57), channel_id=1, replica_groups=mesh['dap_0'=4,'dap_1'=2,'dap_2'=8,'dap_3'=2,'ch'=2] {'dap_0','dap_1','d..., dimensions={0} | all-to-all | bytes 1048576 | tf_op jit(solution)/shard_map/all_to_all | solution.py:41
  118.0 14.4 %all_to_all.38 = bf16[2,1,512,256]{2,3,1,0:T(8,128)(2,1)S(1)} all-to-all(bf16[2,1,512,256]{2,3,1,0:T(8,128)(2,1)S(1)} %bitcast.120), channel_id=1, replica_groups=mesh['dap_0'=4,'dap_1'=2,'dap_2'=8,'dap_3'=2,'ch'=2] {'ch'}, dimensions={0} | all-to-all | bytes 1048576 | tf_op jit(solution)/shard_map/all_to_all | solution.py:59
  133.4 2.2 %reduce.4 = bf16[512,256]{1,0:T(8,128)(2,1)S(1)} reduce(bf16[512,1,256]{2,1,0:T(2,128)(2,1)S(1)} %bitcast.119, bf16[]{:T(256)} %broadcast.96), dimensions={1}, to_apply=%bitcast.109.reduce_sub_computation | reduce | bytes 524290
  135.6 0.9 reshape.119
  136.4 6.6 %all-to-all-start.4 = ((bf16[128,2,512]{2,1,0:T(2,128)(2,1)}), bf16[128,2,512]{2,1,0:T(2,128)(2,1)S(1)}, u32[]{:S(2)}, u32[]{:S(2)}) async-start(bf16[128,2,512]{2,1,0:T(2,128)(2,1)} %reshape.119), calls=%async_computation.4 | async-start | bytes 524288 | tf_op jit(solution)/shard_map/all_to_all | solution.py:118
  143.4 13.3 %all-to-all-done.4 = bf16[128,2,512]{2,1,0:T(2,128)(2,1)S(1)} async-done(((bf16[128,2,512]{2,1,0:T(2,128)(2,1)}), bf16[128,2,512]{2,1,0:T(2,128)(2,1)S(1)}, u32[]{:S(2)}, u32[]{:S(2)}) %all-to-all-start.4) | async-done | bytes 262176 | tf_op jit(solution)/shard_map/all_to_all | solution.py:118
  157.0 1.5 convert_reduce_fusion.1
  159.4 0.8 copy.63
  (46 shorter events, 5.3 us)
Async XLA Ops:
  0.0 90.4 %copy-start = (bf16[4,128,128]{2,1,0:T(8,128)(2,1)S(1)}, bf16[4,128,128]{2,1,0:T(8,128)(2,1)}, u32[]{:S(2)}) copy-start(bf16[4,128,128]{2,1,0:T(8,128)(2,1)} %param.13) | copy-start | bytes 393220
  6.6 13.2 %copy-start.4 = (bf16[256,16]{0,1:T(8,128)(2,1)S(1)}, bf16[256,16]{0,1:T(8,128)(2,1)}, u32[]{:S(2)}) copy-start(bf16[256,16]{0,1:T(8,128)(2,1)} %param.10) | copy-start | bytes 24580
  6.7 13.4 %copy-start.2 = (bf16[512,128]{1,0:T(8,128)(2,1)S(1)}, bf16[512,128]{1,0:T(8,128)(2,1)}, u32[]{:S(2)}) copy-start(bf16[512,128]{1,0:T(8,128)(2,1)} %param.12) | copy-start | bytes 393220
  6.7 63.7 %all-to-all-start = ((bf16[64,128,4,32]{1,3,2,0:T(8,128)(2,1)}), bf16[64,128,4,32]{1,3,2,0:T(8,128)(2,1)S(1)}, u32[]{:S(2)}, u32[]{:S(2)}) async-start(bf16[64,128,4,32]{1,3,2,0:T(8,128)(2,1)} %broadcast_in_dim.4), calls=%async_computation | async-start | bytes 4194304 | tf_op jit(solution)/shard_map/all_to_all | solution.py:12
  19.8 12.4 %copy-start.1 = (bf16[4,256,128]{2,1,0:T(8,128)(2,1)S(1)}, bf16[4,256,128]{2,1,0:T(8,128)(2,1)}, u32[]{:S(2)}) copy-start(bf16[4,256,128]{2,1,0:T(8,128)(2,1)} %param.9) | copy-start | bytes 786436
  118.0 25.1 %copy-start.5 = (bf16[128,128]{1,0:T(8,128)(2,1)S(1)}, bf16[128,128]{1,0:T(8,128)(2,1)}, u32[]{:S(2)}) copy-start(bf16[128,128]{1,0:T(8,128)(2,1)} %param.14) | copy-start | bytes 98308
  136.4 20.3 %all-to-all-start.4 = ((bf16[128,2,512]{2,1,0:T(2,128)(2,1)}), bf16[128,2,512]{2,1,0:T(2,128)(2,1)S(1)}, u32[]{:S(2)}, u32[]{:S(2)}) async-start(bf16[128,2,512]{2,1,0:T(2,128)(2,1)} %reshape.119), calls=%async_computation.4 | async-start | bytes 524288 | tf_op jit(solution)/shard_map/all_to_all | solution.py:118
  157.0 2.2 %copy-start.3 = (bf16[128,128]{1,0:T(8,128)(2,1)S(1)}, bf16[128,128]{1,0:T(8,128)(2,1)}, u32[]{:S(2)}) copy-start(bf16[128,128]{1,0:T(8,128)(2,1)} %param.15) | copy-start | bytes 98308
where the time goes:
time: 163 us; the launch traced here: 160 us
  blocking collectives  58.7 us (36%)
  waiting for transfers between devices  51.3 us (31%)
  starting transfers between devices  19.8 us (12%)
  local copies, waits for them, and re-layouts  16.7 us (10%)
  other arithmetic  8.51 us (5%)
  matrix products  5.01 us (3%)
    all_to_all x1, waiting for transfers between devices, from_everyone(): return lax.all_to_all(copies, axis, split_axis=0, concat_axis=0, tiled=True)  38 us
    all_to_all x1, blocking collectives, side_by_side(): lax.all_to_all(both, axis, split_axis=split_dim, concat_axis=concat_dim,...  25.8 us
    all_to_all x1, blocking collectives, summed_on_arrival(): pieces = lax.all_to_all(split_up(x, dim, count), axis, 0, 0, tiled=True)  14.4 us
    all_to_all x1, waiting for transfers between devices, per_device(): lax.all_to_all(summed.astype(jnp.bfloat16), DAP, split_axis=1, concat_axi...  13.3 us
    all_to_all x1, starting transfers between devices, from_everyone(): return lax.all_to_all(copies, axis, split_axis=0, concat_axis=0, tiled=True)  13.2 us
    all_gather x1, blocking collectives, one_gather(): lines, at, gathered = (lax.all_gather(vector, axis), 0, [])  11.4 us
    all_to_all x1, blocking collectives, from_everyone(): return lax.all_to_all(copies, axis, split_axis=0, concat_axis=0, tiled=True)  7.1 us
    all_to_all x1, starting transfers between devices, per_device(): lax.all_to_all(summed.astype(jnp.bfloat16), DAP, split_axis=1, concat_axi...  6.62 us
  transfers between devices with their start and end apart: 2, of which 2 were waited for; matrix products, arithmetic and copies ran while one was open for 1% of the time, Pallas kernels for 0%

commit v1 on v0

v1 whole, which is shorter than its diff:
```python
import jax
import jax.numpy as jnp
from jax import lax
from jax.sharding import Mesh
from jax.sharding import PartitionSpec as P

DAP = ("yh", "yl", "xl", "z", "core")
PLANE = ("yl", "xl", "core")
CHIP = ("yh", "yl", "xl", "z", "xh")
F32 = jnp.float32
BF16 = jnp.bfloat16


def exchanged(x, axes):
    return lax.all_to_all(x, axes, split_axis=0, concat_axis=0, tiled=True)


def from_everyone(x, axes):
    copies = jnp.broadcast_to(x, (lax.axis_size(axes), *x.shape))
    return exchanged(copies, axes)


def partner(x, axis):
    return lax.ppermute(x, axis, [(0, 1), (1, 0)])


def standardize_fn(value, axis):
    mean = jnp.mean(value, axis=axis, keepdims=True)
    centred = value - mean
    var = jnp.mean(centred * centred, axis=axis, keepdims=True)
    return centred * lax.rsqrt(var + 1e-05)


def per_device(msa, couple, first, second, w_out, entry, w_gate, w_final):
    seqs = msa.shape[0]
    yh, xh, core = lax.axis_index("yh"), lax.axis_index("xh"), lax.axis_index("core")
    msa_n = standardize_fn(msa.astype(F32), -1).astype(BF16)
    right = jnp.einsum("siv,ve->eis", msa_n, second, preferred_element_type=F32).astype(BF16)
    right = jnp.where(yh == xh, right, partner(right, "yh"))
    right = from_everyone(right, "z")
    left = jnp.einsum("siv,vc->ics", msa_n, first, preferred_element_type=F32).astype(BF16)
    left = from_everyone(left.reshape(-1, seqs), PLANE + ("xh",))
    left = left.reshape(8, 2, 4, 16, seqs)
    w_other = partner(w_out, "xh")
    w_full = jnp.where(xh == 0, jnp.stack([w_out, w_other]), jnp.stack([w_other, w_out]))
    w_full = w_full.reshape(2, 16, 32, 128)

    block = couple.reshape(4, 2, 2, 8, 2, 4, 128).transpose(1, 2, 4, 0, 3, 5, 6)
    block = exchanged(block.reshape(8, 4, 32, 128), PLANE)
    outer = jnp.einsum("wejs,gxics->gijwexc", right, left, preferred_element_type=F32)
    outer = (outer * (1.0 / seqs)).astype(BF16)
    update = jnp.einsum("gijwexc,xcez->giwjz", outer, w_full, preferred_element_type=F32)
    lifted = (block.astype(F32) + update.reshape(8, 4, 32, 128)).astype(BF16)
    normed = standardize_fn(lifted.astype(F32), -1).astype(BF16)
    projected = jnp.einsum("gijz,qzc->qcgij", normed, entry, preferred_element_type=F32)
    left_t = (jax.nn.sigmoid(projected[0]) * projected[1]).astype(BF16).reshape(128, 8, 128)
    right_t = (jax.nn.sigmoid(projected[2]) * projected[3]).astype(BF16).reshape(128, 8, 128)
    cols = exchanged(jnp.concatenate([left_t, right_t], 1), CHIP)

    own = exchanged(lifted, PLANE)
    own = own.reshape(2, 2, 2, 4, 8, 4, 128).transpose(3, 0, 1, 4, 2, 5, 6).reshape(4, 256, 128)

    cols = cols.reshape(2, 2, 2, 8, 2, 2, 32, 32).transpose(5, 0, 3, 6, 1, 2, 4, 7)
    cols = cols.reshape(2, 512, 256)
    product = jnp.einsum("ik,jk->ij", cols[0], cols[1], preferred_element_type=F32)
    product = product.astype(BF16).reshape(2, 8, 2, 2, 2, 4, 512).transpose(4, 0, 2, 3, 1, 5, 6)
    product = product.reshape(2, 256, 512)
    mine = lax.dynamic_index_in_dim(product, core, 0, keepdims=False)
    theirs = partner(lax.dynamic_index_in_dim(product, 1 - core, 0, keepdims=False), "core")
    summed = (mine.astype(F32) + theirs.astype(F32)).astype(BF16)
    summed = summed.reshape(64, 4, 2, 256).transpose(0, 2, 1, 3).reshape(128, 8, 128)
    mixed = exchanged(summed, CHIP)
    mixed = mixed.reshape(128, 4, 8, 2, 2, 8).transpose(0, 1, 3, 4, 2, 5).reshape(128, 4, 256)
    tri_n = standardize_fn(mixed.astype(F32), 0).astype(BF16)
    out = jnp.einsum("crj,cz->rjz", tri_n, w_final, preferred_element_type=F32)
    own_n = standardize_fn(own.astype(F32), -1).astype(BF16)
    gate = jax.nn.sigmoid(jnp.einsum("rjz,zy->rjy", own_n, w_gate, preferred_element_type=F32))
    return (own.astype(F32) + gate * out).astype(BF16)


def solution(mesh):
    torus = Mesh(mesh.devices.reshape(2, 2, 2, 8, 2, 2), ("yh", "yl", "xl", "z", "core", "xh"))
    return jax.shard_map(
        per_device,
        mesh=torus,
        in_specs=(
            P(None, DAP, None),
            P(DAP, "xh", None),
            P(None, "xh"),
            P(),
            P("xh", None),
            P(),
            P(),
            P(),
        ),
        out_specs=P(DAP, "xh", None),
        check_vma=False,
    )
```

time: 163 us -> 128 us (0.79)
  blocking collectives: 58.7 us -> 0 us
  starting transfers between devices: 19.8 us -> 40.4 us
  matrix products: 5.01 us -> 14.1 us
  waiting for transfers between devices: 51.3 us -> 47.6 us
  local copies, waits for them, and re-layouts: 16.7 us -> 14.6 us
    all_to_all x3 -> x0, blocking collectives: 47.3 us -> none  [the longest x1 25.8 us: side_by_side(): lax.all_to_all(both, axis, split_axis=split_dim, concat_axis=concat_dim,...]
    all_to_all x2 -> x6, starting transfers between devices: 19.8 us -> 37.1 us  [exchanged(): return lax.all_to_all(x, axes, split_axis=0, concat_axis=0, tiled=True)]
    all_gather x1 -> x0, blocking collectives: 11.4 us -> none  [one_gather(): lines, at, gathered = (lax.all_gather(vector, axis), 0, [])]
    dot_general x7 -> x8, matrix products: 5.01 us -> 14.1 us  [the longest x1 7.69 us: per_device(): jnp.einsum('gijwexc,xcez->giwjz', outer, w_full, preferred_element_type=F32)]
    unnamed x18 -> x9, local copies, waits for them, and re-layouts: 4.89 us -> 0.06 us
    all_to_all x2 -> x6, waiting for transfers between devices: 51.3 us -> 46.7 us  [exchanged(): return lax.all_to_all(x, axes, split_axis=0, concat_axis=0, tiled=True)]
    slice x2 -> x3, local copies, waits for them, and re-layouts: 0.2 us -> 4.54 us  [the longest x2 2.6 us: per_device(): cols[1]]
    reshape x2 -> x7, local copies, waits for them, and re-layouts: 0.25 us -> 4.12 us  [the longest x1 1.75 us: per_device(): block = couple.reshape(4, 2, 2, 8, 2, 4, 128).transpose(1, 2, 4, 0, 3, 5, 6)]
  transfers between devices with their start and end apart: 2 -> 9, of which waited for: 2 -> 5; matrix products, arithmetic and copies ran while one was open for 1% -> 21% of each run, Pallas kernels for 0% -> 0%
where the time goes in v1:
time: 128 us; the launch traced here: 127 us
  waiting for transfers between devices  47.6 us (37%)
  starting transfers between devices  40.4 us (32%)
  local copies, waits for them, and re-layouts  14.6 us (11%)
  matrix products  14.1 us (11%)
  other arithmetic  9.77 us (8%)
    all_to_all x6, waiting for transfers between devices, exchanged(): return lax.all_to_all(x, axes, split_axis=0, concat_axis=0, tiled=True)  46.7 us
    all_to_all x6, starting transfers between devices, exchanged(): return lax.all_to_all(x, axes, split_axis=0, concat_axis=0, tiled=True)  37.1 us
    dot_general x1, matrix products, per_device(): jnp.einsum('gijwexc,xcez->giwjz', outer, w_full, preferred_element_type=F32)  7.69 us
    ppermute x3, starting transfers between devices, partner(): return lax.ppermute(x, axis, [(0, 1), (1, 0)])  3.26 us
    reduce_sum x4, other arithmetic, standardize_fn(): var = jnp.mean(centred * centred, axis=axis, keepdims=True)  2.94 us
    slice x2, local copies, waits for them, and re-layouts, per_device(): cols[1]  2.6 us
  transfers between devices with their start and end apart: 9, of which 5 were waited for; matrix products, arithmetic and copies ran while one was open for 21% of the time, Pallas kernels for 0%

profile of v1, /device:TPU:8, one launch (start us, length us, event | category | flops | bytes accessed | tf_op | source)
XLA Modules:
  0.0 126.8 jit_solution(11003527634752362422)
XLA Ops:
  0.0 1.2 convert_reduce_fusion.1
  1.2 1.3 %fusion.16 = f32[128,4]{1,0:T(8,128)S(1)} fusion(bf16[128,4,256]{2,1,0:T(4,128)(2,1)} %param.8, f32[128,4]{1,0:T(8,128)S(1)} %broadcast_multiply_fusion.2), kind=kLoop, calls=%fused_computation.25 | loop fusion | flops 523776 | bytes 266240 | tf_op jit(solution)/shard_map/reduce_sum | solution.py:30
  2.6 1.3 %fusion.17 = bf16[128,4,256]{2,1,0:T(4,128)(2,1)S(1)} fusion(bf16[128,4,256]{2,1,0:T(4,128)(2,1)} %param.8, f32[128,4]{1,0:T(8,128)S(1)} %add_rsqrt_fusion.2, f32[128,4]{1,0:T(8,128)S(1)} %broadcast_multiply_fusion.2), kind=kLoop, calls=%fused_computation.26 | loop fusion | flops 524288 | bytes 528384 | tf_op jit(solution)/shard_map/convert_element_type | solution.py:37
  4.8 2.3 %collective-permute-start.1 = (bf16[32,4,128]{2,0,1:T(8,128)(2,1)S(1)}, bf16[32,4,128]{2,0,1:T(8,128)(2,1)S(1)}, u32[]{:S(2)}, u32[]{:S(2)}) collective-permute-start(bf16[32,4,128]{2,0,1:T(8,128)(2,1)S(1)} %fusion.11), channel_id=1, source_target_pairs={{0,128},{128,0},{1,129},{129,1},{2,130},{130,2},{3,131},{131,3},{4... | collective-permute-start | bytes 98312 | tf_op jit(solution)/shard_map/ppermute | solution.py:24
  8.7 5.8 %all-to-all-start.1 = ((bf16[16,64,128]{2,1,0:T(8,128)(2,1)}), bf16[16,64,128]{2,1,0:T(8,128)(2,1)S(1)}, u32[]{:S(2)}, u32[]{:S(2)}) async-start(bf16[16,64,128]{2,1,0:T(8,128)(2,1)} %broadcast_in_dim.4), calls=%async_computation.1 | async-start | bytes 524288 | tf_op jit(solution)/shard_map/all_to_all | solution.py:15
  14.5 7.0 %all-to-all-done.1 = bf16[16,64,128]{2,1,0:T(8,128)(2,1)S(1)} async-done(((bf16[16,64,128]{2,1,0:T(8,128)(2,1)}), bf16[16,64,128]{2,1,0:T(8,128)(2,1)S(1)}, u32[]{:S(2)}, u32[]{:S(2)}) %all-to-all-start.1) | async-done | bytes 262176 | tf_op jit(solution)/shard_map/all_to_all | solution.py:15
  22.2 8.6 %all-to-all-start.2 = ((bf16[8,32,4,128]{3,1,2,0:T(8,128)(2,1)}), bf16[8,32,4,128]{3,1,2,0:T(8,128)(2,1)S(1)}, u32[]{:S(2)}, u32[]{:S(2)}) async-start(bf16[8,32,4,128]{3,1,2,0:T(8,128)(2,1)} %broadcast_in_dim.5), calls=%async_computation.2 | async-start | bytes 524288 | tf_op jit(solution)/shard_map/all_to_all | solution.py:15
  31.5 1.7 %copy.79 = bf16[4,2,2,8,2,4,128]{6,5,3,0,4,2,1:T(4,128)(2,1)} copy(bf16[4,2,2,8,2,4,128]{6,5,4,3,2,1,0:T(4,128)(2,1)} %bitcast.132) | data formatting | bytes 524288 | tf_op jit(solution)/shard_map/reshape | solution.py:48
  33.3 9.4 %all-to-all-done.2 = bf16[8,32,4,128]{3,1,2,0:T(8,128)(2,1)S(1)} async-done(((bf16[8,32,4,128]{3,1,2,0:T(8,128)(2,1)}), bf16[8,32,4,128]{3,1,2,0:T(8,128)(2,1)S(1)}, u32[]{:S(2)}, u32[]{:S(2)}) %all-to-all-start.2) | async-done | bytes 262176 | tf_op jit(solution)/shard_map/all_to_all | solution.py:15
  42.6 4.8 %all-to-all-start = ((bf16[8,4,32,128]{3,2,1,0:T(8,128)(2,1)}), bf16[8,4,32,128]{3,2,1,0:T(8,128)(2,1)S(1)}, u32[]{:S(2)}, u32[]{:S(2)}) async-start(bf16[8,4,32,128]{3,2,1,0:T(8,128)(2,1)} %bitcast.2), calls=%async_computation | async-start | bytes 524288 | tf_op jit(solution)/shard_map/all_to_all | solution.py:15
  47.4 2.4 %fusion.2 = bf16[8,4,4,8,32,2,16]{4,6,2,3,1,5,0:T(8,128)(2,1)S(1)} fusion(bf16[8,2,4,16,128,1,1]{4,3,6,5,2,1,0:T(8,128)(2,1)S(1)} %bitcast.127, bf16[8,32,4,128]{3,1,2,0:T(8,128)(2,1)S(1)} %all-to-all-done.2), kind=kOutput, calls=%fused_computation.3 | convolution fusion | flops 270532608 | bytes 2621440 | tf_op jit(solution)/shard_map/wejs,gxics->gijwexc/dot_general | solution.py:50
  49.8 7.7 %fusion.3 = f32[8,4,8,4,128]{4,2,3,1,0:T(8,128)S(1)} fusion(bf16[8,4,4,8,32,2,16]{4,6,2,3,1,5,0:T(8,128)(2,1)S(1)} %fusion.2, bf16[1,16,32,128]{3,2,0,1:T(8,128)(2,1)S(1)} %bitcast.135, bf16[1,16,32,128]{3,2,0,1:T(8,128)(2,1)S(1)} %bitcast.134, pred[]{:T(512)S(6)} %eq.6), kind=kOutput, calls=%fused_computation.6 | convolution fusion | flops 269615104 | bytes 2883585 | tf_op jit(solution)/shard_map/gijwexc,xcez->giwjz/dot_general | solution.py:52
  61.1 6.0 %all-to-all-start.4 = ((bf16[128,16,128]{2,1,0:T(8,128)(2,1)}), bf16[128,16,128]{2,1,0:T(8,128)(2,1)S(1)}, u32[]{:S(2)}, u32[]{:S(2)}) async-start(bf16[128,16,128]{2,1,0:T(8,128)(2,1)} %pad_maximum_fusion), calls=%async_computation.4 | async-start | bytes 1048576 | tf_op jit(solution)/shard_map/all_to_all | solution.py:15
  67.9 18.3 %all-to-all-done.4 = bf16[128,16,128]{2,1,0:T(8,128)(2,1)S(1)} async-done(((bf16[128,16,128]{2,1,0:T(8,128)(2,1)}), bf16[128,16,128]{2,1,0:T(8,128)(2,1)S(1)}, u32[]{:S(2)}, u32[]{:S(2)}) %all-to-all-start.4) | async-done | bytes 524320 | tf_op jit(solution)/shard_map/all_to_all | solution.py:15
  86.1 4.6 %all-to-all-start.3 = ((bf16[8,4,32,128]{3,2,1,0:T(8,128)(2,1)}), bf16[8,4,32,128]{3,2,1,0:T(8,128)(2,1)S(1)}, u32[]{:S(2)}, u32[]{:S(2)}) async-start(bf16[8,4,32,128]{3,2,1,0:T(8,128)(2,1)} %copy.89), calls=%async_computation.3 | async-start | bytes 524288 | tf_op jit(solution)/shard_map/all_to_all | solution.py:15
  91.6 1.6 %fusion.56 = (bf16[1,2,8,32,2,2,2,32]{7,3,0,6,2,5,4,1:T(8,128)(2,1)S(1)}, bf16[1,2,8,32,2,2,2,32]{7,3,0,6,2,5,4,1:T(8,128)(2,1)}) fusion(bf16[2,2,8,32,2,2,2,32]{7,3,0,6,2,5,4,1:T(8,128)(2,1)S(1)} %bitcast.116), kind=kLoop, calls=%fused_computation.90 | loop fusion | bytes 1048576 | tf_op jit(solution)/shard_map/slice | solution.py:65
  93.2 1.9 %copy.94 = bf16[1,2,8,32,2,2,2,32]{3,2,1,7,6,5,4,0:T(8,128)(2,1)S(1)} copy(bf16[1,2,8,32,2,2,2,32]{7,3,0,6,2,5,4,1:T(8,128)(2,1)} %get-tuple-element.8) | data formatting | bytes 524288 | tf_op jit(solution)/shard_map/slice | solution.py:65
  95.2 1.0 squeeze.21
  96.2 1.0 copy.95
  97.2 1.0 squeeze.22
  99.1 1.0 constant_dynamic-slice_fusion
  102.8 7.3 %all-to-all-start.5 = ((bf16[128,8,128]{2,1,0:T(8,128)(2,1)}), bf16[128,8,128]{2,1,0:T(8,128)(2,1)S(1)}, u32[]{:S(2)}, u32[]{:S(2)}) async-start(bf16[128,8,128]{2,1,0:T(8,128)(2,1)} %reshape.171), calls=%async_computation.5 | async-start | bytes 524288 | tf_op jit(solution)/shard_map/all_to_all | solution.py:15
  112.2 12.1 %all-to-all-done.5 = bf16[128,8,128]{2,1,0:T(8,128)(2,1)S(1)} async-done(((bf16[128,8,128]{2,1,0:T(8,128)(2,1)}), bf16[128,8,128]{2,1,0:T(8,128)(2,1)S(1)}, u32[]{:S(2)}, u32[]{:S(2)}) %all-to-all-start.5) | async-done | bytes 262176 | tf_op jit(solution)/shard_map/all_to_all | solution.py:15
  125.9 0.9 fusion.10
  (61 shorter events, 16.2 us)
Async XLA Ops:
  0.0 58.9 %copy-start = (bf16[4,128,128]{2,1,0:T(8,128)(2,1)S(1)}, bf16[4,128,128]{2,1,0:T(8,128)(2,1)}, u32[]{:S(2)}) copy-start(bf16[4,128,128]{2,1,0:T(8,128)(2,1)} %param.13) | copy-start | bytes 393220
  4.8 9.8 %collective-permute-start.1 = (bf16[32,4,128]{2,0,1:T(8,128)(2,1)S(1)}, bf16[32,4,128]{2,0,1:T(8,128)(2,1)S(1)}, u32[]{:S(2)}, u32[]{:S(2)}) collective-permute-start(bf16[32,4,128]{2,0,1:T(8,128)(2,1)S(1)} %fusion.11), channel_id=1, source_target_pairs={{0,128},{128,0},{1,129},{129,1},{2,130},{130,2},{3,131},{131,3},{4... | collective-permute-start | bytes 98312 | tf_op jit(solution)/shard_map/ppermute | solution.py:24
  8.7 12.8 %all-to-all-start.1 = ((bf16[16,64,128]{2,1,0:T(8,128)(2,1)}), bf16[16,64,128]{2,1,0:T(8,128)(2,1)S(1)}, u32[]{:S(2)}, u32[]{:S(2)}) async-start(bf16[16,64,128]{2,1,0:T(8,128)(2,1)} %broadcast_in_dim.4), calls=%async_computation.1 | async-start | bytes 524288 | tf_op jit(solution)/shard_map/all_to_all | solution.py:15
  22.2 27.6 %copy-start.2 = (bf16[512,128]{1,0:T(8,128)(2,1)S(1)}, bf16[512,128]{1,0:T(8,128)(2,1)}, u32[]{:S(2)}) copy-start(bf16[512,128]{1,0:T(8,128)(2,1)} %param.12) | copy-start | bytes 393220
  22.2 20.4 %all-to-all-start.2 = ((bf16[8,32,4,128]{3,1,2,0:T(8,128)(2,1)}), bf16[8,32,4,128]{3,1,2,0:T(8,128)(2,1)S(1)}, u32[]{:S(2)}, u32[]{:S(2)}) async-start(bf16[8,32,4,128]{3,1,2,0:T(8,128)(2,1)} %broadcast_in_dim.5), calls=%async_computation.2 | async-start | bytes 524288 | tf_op jit(solution)/shard_map/all_to_all | solution.py:15
  30.8 19.0 %collective-permute-start = (bf16[512,128]{1,0:T(8,128)(2,1)}, bf16[512,128]{1,0:T(8,128)(2,1)S(1)}, u32[]{:S(2)}, u32[]{:S(2)}) collective-permute-start(bf16[512,128]{1,0:T(8,128)(2,1)} %param.12), channel_id=1, source_target_pairs={{0,1},{1,0},{2,3},{3,2},{4,5},{5,4},{6,7},{7,6},{8,9},{9,8},{10,11... | collective-permute-start | bytes 393224 | tf_op jit(solution)/shard_map/ppermute | solution.py:24
  42.6 15.2 %all-to-all-start = ((bf16[8,4,32,128]{3,2,1,0:T(8,128)(2,1)}), bf16[8,4,32,128]{3,2,1,0:T(8,128)(2,1)S(1)}, u32[]{:S(2)}, u32[]{:S(2)}) async-start(bf16[8,4,32,128]{3,2,1,0:T(8,128)(2,1)} %bitcast.2), calls=%async_computation | async-start | bytes 524288 | tf_op jit(solution)/shard_map/all_to_all | solution.py:15
  61.1 25.1 %all-to-all-start.4 = ((bf16[128,16,128]{2,1,0:T(8,128)(2,1)}), bf16[128,16,128]{2,1,0:T(8,128)(2,1)S(1)}, u32[]{:S(2)}, u32[]{:S(2)}) async-start(bf16[128,16,128]{2,1,0:T(8,128)(2,1)} %pad_maximum_fusion), calls=%async_computation.4 | async-start | bytes 1048576 | tf_op jit(solution)/shard_map/all_to_all | solution.py:15
  86.1 14.2 %all-to-all-start.3 = ((bf16[8,4,32,128]{3,2,1,0:T(8,128)(2,1)}), bf16[8,4,32,128]{3,2,1,0:T(8,128)(2,1)S(1)}, u32[]{:S(2)}, u32[]{:S(2)}) async-start(bf16[8,4,32,128]{3,2,1,0:T(8,128)(2,1)} %copy.89), calls=%async_computation.3 | async-start | bytes 524288 | tf_op jit(solution)/shard_map/all_to_all | solution.py:15
  95.1 16.3 %copy-start.3 = (bf16[128,128]{1,0:T(8,128)(2,1)S(1)}, bf16[128,128]{1,0:T(8,128)(2,1)}, u32[]{:S(2)}) copy-start(bf16[128,128]{1,0:T(8,128)(2,1)} %param.14) | copy-start | bytes 98308
  98.6 27.3 %copy-start.1 = (bf16[128,128]{1,0:T(8,128)(2,1)S(1)}, bf16[128,128]{1,0:T(8,128)(2,1)}, u32[]{:S(2)}) copy-start(bf16[128,128]{1,0:T(8,128)(2,1)} %param.15) | copy-start | bytes 98308
  100.1 1.6 %collective-permute-start.2 = (bf16[256,512]{1,0:T(8,128)(2,1)S(1)}, bf16[256,512]{1,0:T(8,128)(2,1)S(1)}, u32[]{:S(2)}, u32[]{:S(2)}) collective-permute-start(bf16[256,512]{1,0:T(8,128)(2,1)S(1)} %bitcast.131), channel_id=1, source_target_pairs={{0,2},{2,0},{1,3},{3,1},{4,6},{6,4},{5,7},{7,5},{8,10},{10,8},{9,1... | collective-permute-start | bytes 786440 | tf_op jit(solution)/shard_map/ppermute | solution.py:24
  102.8 21.5 %all-to-all-start.5 = ((bf16[128,8,128]{2,1,0:T(8,128)(2,1)}), bf16[128,8,128]{2,1,0:T(8,128)(2,1)S(1)}, u32[]{:S(2)}, u32[]{:S(2)}) async-start(bf16[128,8,128]{2,1,0:T(8,128)(2,1)} %reshape.171), calls=%async_computation.5 | async-start | bytes 524288 | tf_op jit(solution)/shard_map/all_to_all | solution.py:15

commit v2 on v1

v2 whole, which is shorter than its diff:
```python
import jax
import jax.numpy as jnp
from jax import lax
from jax.experimental import pallas as pl
from jax.experimental.pallas import tpu as pltpu
from jax.sharding import Mesh
from jax.sharding import PartitionSpec as P

DAP = ("yh", "yl", "xl", "z", "core")
PLANE = ("yl", "xl", "core")
CHIP = ("yh", "yl", "xl", "z", "xh")
F32 = jnp.float32
BF16 = jnp.bfloat16
VMEM = pl.BlockSpec(memory_space=pltpu.VMEM)
ANY = pl.BlockSpec(memory_space=pl.ANY)
SMEM = pl.BlockSpec(memory_space=pltpu.SMEM)


def dot(a, b, dims):
    return lax.dot_general(a, b, (dims, ((), ())), preferred_element_type=F32)


def standardized(x, axis):
    mean = jnp.mean(x, axis=axis, keepdims=True)
    centred = x - mean
    var = jnp.mean(centred * centred, axis=axis, keepdims=True)
    return centred * lax.rsqrt(var + 1e-05)


def on_core(kernel, outs, n_in, scratch=(), scalars=0, elsewhere=(), cost=None, limit=12):
    return pl.pallas_call(
        kernel,
        out_shape=outs,
        in_specs=[SMEM if i < scalars else ANY if i in elsewhere else VMEM for i in range(n_in)],
        out_specs=jax.tree.map(lambda _: VMEM, outs),
        scratch_shapes=scratch,
        compiler_params=pltpu.CompilerParams(vmem_limit_bytes=limit << 20),
        cost_estimate=cost,
    )


def cost(us):
    return pl.CostEstimate(flops=int(us * 1e9), bytes_accessed=int(us * 3e6), transcendentals=0)


def first_kernel(msa_ref, second_ref, right_ref, norm_ref):
    x = [msa_ref[:, i, :].astype(F32) for i in range(4)]
    for i in range(4):
        normed = standardized(x[i], -1).astype(BF16)
        norm_ref[i] = normed
        right_ref[i * 32 : (i + 1) * 32, :] = dot(second_ref[...], normed, ((0,), (1,))).astype(BF16)


def firsts(msa, second):
    return on_core(
        first_kernel,
        (jax.ShapeDtypeStruct((128, 128), BF16), jax.ShapeDtypeStruct((4, 128, 256), BF16)),
        2,
        cost=cost(1),
    )(msa, second)


def pack_kernel(me_ref, norm_ref, own_ref, other_ref, couple_ref, packed_ref):
    mex = me_ref[1]
    for i in range(4):
        normed = norm_ref[i]
        lo = dot(own_ref[...], normed, ((0,), (1,))).astype(BF16)
        hi = dot(other_ref[...], normed, ((0,), (1,))).astype(BF16)
        for g in range(8):
            packed_ref[g, pl.ds(pl.multiple_of(128 + mex * 64 + i * 16, 16), 16), :] = lo
            packed_ref[g, pl.ds(pl.multiple_of(192 - mex * 64 + i * 16, 16), 16), :] = hi
    row = lax.broadcasted_iota(jnp.int32, (8, 128), 0)
    for i in range(4):
        for y in range(4):
            for zz in range(4):
                pair = couple_ref[i, (y * 8 + zz * 2) * 8 : (y * 8 + zz * 2 + 2) * 8, :].astype(F32)
                a, b = pair[:8], pair[8:]
                rows = slice(i * 32 + zz * 8, i * 32 + zz * 8 + 8)
                packed_ref[y * 2, rows, :] = jnp.where(row < 4, a, pltpu.roll(b, 4, 0)).astype(BF16)
                packed_ref[y * 2 + 1, rows, :] = jnp.where(row < 4, pltpu.roll(a, 4, 0), b).astype(BF16)


def packs(me, normed, own, other, couple):
    return on_core(
        pack_kernel, jax.ShapeDtypeStruct((8, 256, 128), BF16), 5, scalars=1, cost=cost(1)
    )(me, normed, own, other, couple)


def wide_kernel(me_ref, own_ref, other_ref, wide_ref, w_scr):
    mex = me_ref[1]
    w_scr[pl.ds(pl.multiple_of(mex * 512, 512), 512), :] = own_ref[...].astype(F32)
    w_scr[pl.ds(pl.multiple_of(512 - mex * 512, 512), 512), :] = other_ref[...].astype(F32)
    wide_ref[...] = jnp.zeros_like(wide_ref)
    for e in range(32):
        w = w_scr[pl.ds(e, 32, stride=32), :].astype(BF16)
        for x in range(2):
            for i in range(4):
                row = ((e * 2 + x) * 4 + i) * 16
                wide_ref[row : row + 16, i * 128 : (i + 1) * 128] = w[x * 16 : (x + 1) * 16]


def widened(me, own, other):
    return on_core(
        wide_kernel,
        jax.ShapeDtypeStruct((4096, 512), BF16),
        3,
        [pltpu.VMEM((1024, 128), F32)],
        scalars=1,
        cost=cost(2),
    )(me, own, other)


def pair_kernel(me_ref, right_ref, packed_ref, wide_ref, entry_ref, *rest):
    lifted_refs, cols_ref = rest[:8], rest[8]
    rows_scr, lhs_scr, cols_scr, norm_scr, up_scr, wide_scr, sem = rest[9:]
    me = me_ref[0]
    fetch = pltpu.make_async_copy(wide_ref, wide_scr, sem)
    fetch.start()
    for z in range(8):
        for j in range(4):
            rows_scr[pl.ds(z * 4 + j, 32, stride=32), :] = right_ref[z, j * 32 : (j + 1) * 32, :].astype(F32)
    lefts = jnp.concatenate([packed_ref[g, 128:256, :] for g in range(8)], axis=0)
    for part in range(4):
        rows = rows_scr[part * 256 : (part + 1) * 256, :].astype(BF16)
        outer = (dot(rows, lefts, ((1,), (1,))) * (1.0 / 128)).astype(BF16)
        for e in range(8):
            for g in range(8):
                lhs_scr[g * 32 : (g + 1) * 32, (part * 8 + e) * 128 : (part * 8 + e + 1) * 128] = outer[
                    e * 32 : (e + 1) * 32, g * 128 : (g + 1) * 128
                ]
    fetch.wait()
    for half in range(2):
        rows = slice(half * 128, (half + 1) * 128)
        up_scr[rows, :] = dot(lhs_scr[rows, :], wide_scr[...], ((1,), (0,)))
    for m in range(8):
        g = m ^ me
        for i in range(4):
            lifted = (
                packed_ref[g, i * 32 : (i + 1) * 32, :].astype(F32)
                + up_scr[pl.ds(pl.multiple_of(g * 32, 32), 32), i * 128 : (i + 1) * 128]
            ).astype(BF16)
            lifted_refs[m][i * 32 : (i + 1) * 32, :] = lifted
            norm_scr[pl.ds(pl.multiple_of(g * 128 + i * 32, 32), 32), :] = standardized(
                lifted.astype(F32), -1
            ).astype(BF16)
    for g in range(8):
        normed = norm_scr[g * 128 : (g + 1) * 128, :]
        p = [dot(entry_ref[q], normed, ((1,), (1,))) for q in range(4)]
        cols_scr[pl.ds(g, 128, stride=16), :] = jax.nn.sigmoid(p[0]) * p[1]
        cols_scr[pl.ds(8 + g, 128, stride=16), :] = jax.nn.sigmoid(p[2]) * p[3]
    for part in range(8):
        cols_ref[part * 16 : (part + 1) * 16] = (
            cols_scr[part * 256 : (part + 1) * 256, :].reshape(16, 16, 128).astype(BF16)
        )


def pairs(me, right, packed, wide, entry_t):
    out = on_core(
        pair_kernel,
        (jax.ShapeDtypeStruct((128, 128), BF16),) * 8 + (jax.ShapeDtypeStruct((128, 16, 128), BF16),),
        5,
        [
            pltpu.VMEM((1024, 128), F32),
            pltpu.VMEM((256, 4096), BF16),
            pltpu.VMEM((2048, 128), F32),
            pltpu.VMEM((1024, 128), BF16),
            pltpu.VMEM((256, 512), F32),
            pltpu.VMEM((4096, 512), BF16),
            pltpu.SemaphoreType.DMA(()),
        ],
        elsewhere=(3,),
        limit=20,
        scalars=1,
        cost=cost(5),
    )(me, right, packed, wide, entry_t)
    return out[:8], out[8]


def regrouped(v, lane):
    low, even = lane < 64, (lane // 32) % 2 == 0
    t0 = jnp.where(low, v[0], pltpu.roll(v[2], 64, 1))
    t2 = jnp.where(low, pltpu.roll(v[0], 64, 1), v[2])
    t1 = jnp.where(low, v[1], pltpu.roll(v[3], 64, 1))
    t3 = jnp.where(low, pltpu.roll(v[1], 64, 1), v[3])
    u0 = jnp.where(even, t0, pltpu.roll(t1, 32, 1))
    u1 = jnp.where(even, pltpu.roll(t0, 96, 1), t1)
    u2 = jnp.where(even, t2, pltpu.roll(t3, 32, 1))
    u3 = jnp.where(even, pltpu.roll(t2, 96, 1), t3)
    return u0, u1, u2, u3


def product_kernel(me_ref, cols_ref, mine_ref, theirs_ref, ops_scr, out_scr):
    core = me_ref[2]
    lane = lax.broadcasted_iota(jnp.int32, (8, 128), 1)
    for yh in range(2):
        for z in range(8):
            for part in range(2):
                pieces = []
                for xh in range(2):
                    for x in range(2):
                        src = (((yh * 2 + part) * 2 + x) * 8 + z) * 2 + xh
                        pieces.append(cols_ref[src].astype(F32))
                left = regrouped([p[0:8] for p in pieces], lane)
                right = regrouped([p[8:16] for p in pieces], lane)
                lanes = slice(part * 128, (part + 1) * 128)
                for q in range(4):
                    row = (q * 16 + yh * 8 + z) * 8
                    ops_scr[0, row : row + 8, lanes] = left[q]
                    row = (yh * 32 + q * 8 + z) * 8
                    ops_scr[1, row : row + 8, lanes] = right[q]
    rights = ops_scr[1].astype(BF16)
    for q in range(4):
        prod = dot(ops_scr[0, q * 128 : (q + 1) * 128, :].astype(BF16), rights, ((1,), (1,)))
        for yh in range(2):
            for z in range(8):
                for t in range(4):
                    start = yh * 1024 + (z * 2 + t // 2) * 8 + q * 2 + t % 2
                    out_scr[pl.ds(start, 8, stride=128), :] = prod[
                        (yh * 8 + z) * 8 : (yh * 8 + z + 1) * 8, t * 128 : (t + 1) * 128
                    ]
    for y in range(8):
        rows = slice(y * 16, (y + 1) * 16)
        mine_ref[rows] = out_scr[pl.ds(pl.multiple_of((y * 2 + core) * 128, 128), 128), :].reshape(16, 8, 128)
        theirs_ref[rows] = (
            out_scr[pl.ds(pl.multiple_of((y * 2 + 1 - core) * 128, 128), 128), :].reshape(16, 8, 128).astype(BF16)
        )


def products(me, cols):
    return on_core(
        product_kernel,
        (jax.ShapeDtypeStruct((128, 8, 128), F32), jax.ShapeDtypeStruct((128, 8, 128), BF16)),
        2,
        [pltpu.VMEM((2, 512, 256), F32), pltpu.VMEM((2048, 128), F32)],
        scalars=1,
        cost=cost(3),
    )(me, cols)


def crossed(scr, out_row):
    row = lax.broadcasted_iota(jnp.int32, (8, 128), 0)
    res = []
    for m in range(4):
        a, b = scr[out_row + m * 8 : out_row + m * 8 + 8, :], scr[out_row + 32 + m * 8 : out_row + 40 + m * 8, :]
        res.append(jnp.where(row < 4, a, pltpu.roll(b, 4, 0)))
        res.append(jnp.where(row < 4, pltpu.roll(a, 4, 0), b))
    return jnp.concatenate(res, axis=0)


def gate_kernel(me_ref, *rest):
    own_refs, w_ref, gate_ref, base_ref, gate_scr, base_scr = rest[:8], *rest[8:]
    me = me_ref[0]
    for m in range(8):
        x = own_refs[m][...].astype(F32)
        normed = standardized(x, -1).astype(BF16)
        gate = jax.nn.sigmoid(dot(normed, w_ref[...], ((1,), (0,))))
        for i in range(4):
            rows = pl.ds(pl.multiple_of(i * 256 + (m ^ me) * 32, 32), 32)
            gate_scr[rows, :] = gate[i * 32 : (i + 1) * 32]
            base_scr[rows, :] = x[i * 32 : (i + 1) * 32]
    for b in range(16):
        gate_ref[b * 64 : (b + 1) * 64, :] = crossed(gate_scr, b * 64)
        base_ref[b * 64 : (b + 1) * 64, :] = crossed(base_scr, b * 64)


def gates(me, own, w):
    return on_core(
        gate_kernel,
        (jax.ShapeDtypeStruct((1024, 128), F32), jax.ShapeDtypeStruct((1024, 128), F32)),
        10,
        [pltpu.VMEM((1024, 128), F32), pltpu.VMEM((1024, 128), F32)],
        scalars=1,
        cost=cost(2),
    )(me, *own, w)


def final_kernel(mixed_ref, gate_ref, base_ref, w_ref, out_ref, norm_scr, mm_scr):
    tri_n = standardized(mixed_ref[...].astype(F32), 0)
    norm_scr[...] = tri_n.reshape(1024, 128)
    for i in range(4):
        for t in range(2):
            x = norm_scr[pl.ds(i * 2 + t, 128, stride=8), :].astype(BF16)
            out = dot(x, w_ref[...], ((0,), (0,)))
            for j in range(2):
                for z in range(8):
                    row = (j * 8 + z) * 8
                    mm_scr[pl.ds(i * 256 + z * 4 + t * 2 + j, 8, stride=32), :] = out[row : row + 8]
    for b in range(16):
        rows = slice(b * 64, (b + 1) * 64)
        out_ref[rows, :] = (base_ref[rows, :] + gate_ref[rows, :] * crossed(mm_scr, b * 64)).astype(BF16)


def finals(mixed, gate, base, w):
    return on_core(
        final_kernel,
        jax.ShapeDtypeStruct((1024, 128), BF16),
        4,
        [pltpu.VMEM((1024, 128), F32), pltpu.VMEM((1024, 128), F32)],
        cost=cost(2),
    )(mixed, gate, base, w)


def exchanged(x, axes):
    return lax.all_to_all(x, axes, split_axis=0, concat_axis=0, tiled=True)


def partner(x, axis):
    return lax.ppermute(x, axis, [(0, 1), (1, 0)])


def per_device(msa, couple, first, second, w_out, entry, w_gate, w_final):
    at = {name: lax.axis_index(name) for name in ("yh", "yl", "xl", "core", "xh")}
    me = jnp.stack([at["yl"] * 4 + at["xl"] * 2 + at["core"], at["xh"], at["core"]]).astype(jnp.int32)
    first_other = partner(first, "xh")
    w_other = partner(w_out, "xh")
    right, normed = firsts(msa, second)
    right = jnp.where(at["yh"] == at["xh"], right, partner(right, "yh"))
    packed = exchanged(packs(me, normed, first, first_other, couple), PLANE)
    right = exchanged(jnp.broadcast_to(right, (8, 128, 128)), "z")
    wide = widened(me, w_out, w_other)
    lifted, cols = pairs(me, right, packed, wide, jnp.swapaxes(entry, 1, 2))
    cols = exchanged(cols, CHIP)
    own = [lifted[0]]
    own += [lax.ppermute(lifted[m], PLANE, [(i, i ^ m) for i in range(8)]) for m in range(1, 8)]
    gate, base = gates(me, own, w_gate)
    mine, theirs = products(me, cols)
    summed = (mine + partner(theirs, "core").astype(F32)).astype(BF16)
    mixed = exchanged(summed, CHIP)
    return finals(mixed, gate, base, w_final).reshape(4, 256, 128)


def solution(mesh):
    torus = Mesh(mesh.devices.reshape(2, 2, 2, 8, 2, 2), ("yh", "yl", "xl", "z", "core", "xh"))
    return jax.shard_map(
        per_device,
        mesh=torus,
        in_specs=(
            P(None, DAP, None),
            P(DAP, "xh", None),
            P(None, "xh"),
            P(),
            P("xh", None),
            P(),
            P(),
            P(),
        ),
        out_specs=P(DAP, "xh", None),
        check_vma=False,
    )
```

time: 128 us -> 107 us (0.84)
  blocking collectives: 0 us -> 29.4 us
  waiting for transfers between devices: 47.6 us -> 20.9 us
  matrix products: 14.1 us -> 0 us
  Pallas kernels: 0 us -> 12.4 us
  other arithmetic: 9.77 us -> 0.84 us
  local copies, waits for them, and re-layouts: 14.6 us -> 8.56 us
  starting transfers between devices: 40.4 us -> 34.4 us
    all_to_all x6 -> x3, waiting for transfers between devices: 46.7 us -> 6.2 us  [exchanged(): return lax.all_to_all(x, axes, split_axis=0, concat_axis=0, tiled=True)]
    all_to_all x0 -> x1, blocking collectives: none -> 29.4 us  [exchanged(): return lax.all_to_all(x, axes, split_axis=0, concat_axis=0, tiled=True)]
    all_to_all x6 -> x3, starting transfers between devices: 37.1 us -> 20.9 us  [exchanged(): return lax.all_to_all(x, axes, split_axis=0, concat_axis=0, tiled=True)]
    dot_general x8 -> x0, matrix products: 14.1 us -> none  [the longest x1 7.69 us: per_device(): jnp.einsum('gijwexc,xcez->giwjz', outer, w_full, preferred_element_type=F32)]
    pallas_call x0 -> x7, Pallas kernels: none -> 12.4 us  [the longest x1 4.55 us: pairs(): on_core(pair_kernel, (jax.ShapeDtypeStruct((128, 128), BF16),) * 8 + (jax...]
    ppermute x3 -> x4, waiting for transfers between devices: 0.86 us -> 11.6 us  [partner(): return lax.ppermute(x, axis, [(0, 1), (1, 0)])]
    unnamed x9 -> x19, local copies, waits for them, and re-layouts: 0.06 us -> 7.82 us
    ppermute x0 -> x7, starting transfers between devices: none -> 6.36 us  [per_device(): lax.ppermute(lifted[m], PLANE, [(i, i ^ m) for i in range(8)])]
  transfers between devices with their start and end apart: 9 -> 14, of which waited for: 5 -> 11; matrix products, arithmetic and copies ran while one was open for 21% -> 1% of each run, Pallas kernels for 0% -> 3%
where the time goes in v2:
time: 107 us
  starting transfers between devices  34.4 us (32%)
  blocking collectives  29.4 us (27%)
  waiting for transfers between devices  20.9 us (20%)
  Pallas kernels  12.4 us (12%)
  local copies, waits for them, and re-layouts  8.56 us (8%)
    all_to_all x1, blocking collectives, exchanged(): return lax.all_to_all(x, axes, split_axis=0, concat_axis=0, tiled=True)  29.4 us
    all_to_all x3, starting transfers between devices, exchanged(): return lax.all_to_all(x, axes, split_axis=0, concat_axis=0, tiled=True)  20.9 us
    ppermute x4, waiting for transfers between devices, partner(): return lax.ppermute(x, axis, [(0, 1), (1, 0)])  11.6 us
    unnamed x19, local copies, waits for them, and re-layouts  7.82 us
    ppermute x4, starting transfers between devices, partner(): return lax.ppermute(x, axis, [(0, 1), (1, 0)])  7.15 us
    ppermute x7, starting transfers between devices, per_device(): lax.ppermute(lifted[m], PLANE, [(i, i ^ m) for i in range(8)])  6.36 us
    all_to_all x3, waiting for transfers between devices, exchanged(): return lax.all_to_all(x, axes, split_axis=0, concat_axis=0, tiled=True)  6.2 us
    pallas_call x1, Pallas kernels, pairs(): on_core(pair_kernel, (jax.ShapeDtypeStruct((128, 128), BF16),) * 8 + (jax...  4.55 us
  transfers between devices with their start and end apart: 14, of which 11 were waited for; matrix products, arithmetic and copies ran while one was open for 1% of the time, Pallas kernels for 3%

profile of v2, /device:TPU:8, one launch (start us, length us, event | category | flops | bytes accessed | tf_op | source)
XLA Modules:
  0.0 106.7 jit_solution(18430503838379257116)
XLA Ops:
  0.8 3.1 %collective-permute-start.1 = (bf16[256,16]{1,0:T(8,128)(2,1)S(1)}, bf16[256,16]{1,0:T(8,128)(2,1)S(1)}, u32[]{:S(2)}, u32[]{:S(2)}) collective-permute-start(bf16[256,16]{1,0:T(8,128)(2,1)S(1)} %copy.11.own_ref), channel_id=1, source_target_pairs={{0,1},{1,0},{2,3},{3,2},{4,5},{5,4},{6,7},{7,6},{8,9},{9,8},{10,11... | collective-permute-start | bytes 24584 | tf_op jit(solution)/shard_map/ppermute | solution.py:308
  7.6 1.7 %shard_map.83 = bf16[8,256,128]{2,1,0:T(8,128)(2,1)} custom-call(s32[3]{0:T(128)S(1)} %pad_add_fusion.me_ref, bf16[4,128,256]{2,1,0:T(8,128)(2,1)S(1)} %get-tuple-element.21.norm_ref, bf16[256,16]{1,0:T(8,128)(2,1)S(1)} %copy.11.own_ref, bf16[256,16]{1,0:T(8,128)(2,1)S(1)} %collective-permute-done.1.other_ref, bf16[4,256,128]{2,1,0:T(8,128)(2,1)S(1)} %copy-done.1), custom_call_target="tpu_custom_call" | custom-call | flops 1000000000 | bytes 3000000 | tf_op jit(solution)/shard_map/pallas_call | solution.py:84
  9.3 5.6 %all-to-all-start.1 = ((bf16[8,256,128]{2,1,0:T(8,128)(2,1)}), bf16[8,256,128]{2,1,0:T(8,128)(2,1)S(1)}, u32[]{:S(2)}, u32[]{:S(2)}) async-start(bf16[8,256,128]{2,1,0:T(8,128)(2,1)} %shard_map.83), calls=%async_computation.1 | async-start | bytes 1048576 | tf_op jit(solution)/shard_map/all_to_all | solution.py:304
  15.8 6.4 %collective-permute-done = bf16[128,128]{1,0:T(8,128)(2,1)S(1)} collective-permute-done((bf16[128,128]{1,0:T(8,128)(2,1)S(1)}, bf16[128,128]{1,0:T(8,128)(2,1)S(1)}, u32[]{:S(2)}, u32[]{:S(2)}) %collective-permute-start) | collective-permute-done | bytes 32800 | tf_op jit(solution)/shard_map/ppermute | solution.py:308
  22.2 1.0 all-to-all-done.1.packed_ref
  23.9 7.5 %all-to-all-start = ((bf16[8,128,128]{2,1,0:T(8,128)(2,1)}), bf16[8,128,128]{2,1,0:T(8,128)(2,1)S(1)}, u32[]{:S(2)}, u32[]{:S(2)}) async-start(bf16[8,128,128]{2,1,0:T(8,128)(2,1)} %broadcast_in_dim.3), calls=%async_computation | async-start | bytes 524288 | tf_op jit(solution)/shard_map/all_to_all | solution.py:304
  31.4 3.0 %collective-permute-start.2 = (bf16[512,128]{1,0:T(8,128)(2,1)S(1)}, bf16[512,128]{1,0:T(8,128)(2,1)S(1)}, u32[]{:S(2)}, u32[]{:S(2)}) collective-permute-start(bf16[512,128]{1,0:T(8,128)(2,1)S(1)} %copy-done.2), channel_id=1, source_target_pairs={{0,1},{1,0},{2,3},{3,2},{4,5},{5,4},{6,7},{7,6},{8,9},{9,8},{10,11... | collective-permute-start | bytes 393224 | tf_op jit(solution)/shard_map/ppermute | solution.py:308
  34.6 3.4 %collective-permute-done.2.other_ref = bf16[512,128]{1,0:T(8,128)(2,1)S(1)} collective-permute-done((bf16[512,128]{1,0:T(8,128)(2,1)S(1)}, bf16[512,128]{1,0:T(8,128)(2,1)S(1)}, u32[]{:S(2)}, u32[]{:S(2)}) %collective-permute-start.2) | collective-permute-done | bytes 131104 | tf_op jit(solution)/shard_map/ppermute | solution.py:308
  38.0 1.3 %shard_map.84.wide_ref = bf16[4096,512]{1,0:T(8,128)(2,1)S(1)} custom-call(s32[3]{0:T(128)S(1)} %pad_add_fusion.me_ref, bf16[512,128]{1,0:T(8,128)(2,1)S(1)} %copy-done.2, bf16[512,128]{1,0:T(8,128)(2,1)S(1)} %collective-permute-done.2.other_ref), custom_call_target="tpu_custom_call" | custom-call | flops 2000000000 | bytes 6000000 | tf_op jit(solution)/shard_map/pallas_call | solution.py:103
  39.3 1.9 %copy-done.5 = bf16[4096,512]{1,0:T(8,128)(2,1)} copy-done((bf16[4096,512]{1,0:T(8,128)(2,1)}, bf16[4096,512]{1,0:T(8,128)(2,1)S(1)}, u32[]{:S(2)}) %copy-start.5) | copy-done | bytes 4194328
  41.2 1.6 %all-to-all-done.right_ref = bf16[8,128,128]{2,1,0:T(8,128)(2,1)S(1)} async-done(((bf16[8,128,128]{2,1,0:T(8,128)(2,1)}), bf16[8,128,128]{2,1,0:T(8,128)(2,1)S(1)}, u32[]{:S(2)}, u32[]{:S(2)}) %all-to-all-start) | async-done | bytes 262176 | tf_op jit(solution)/shard_map/all_to_all | solution.py:304
  42.8 2.2 %copy-done.6 = bf16[4096,512]{1,0:T(8,128)(2,1)S(1)} copy-done((bf16[4096,512]{1,0:T(8,128)(2,1)S(1)}, bf16[4096,512]{1,0:T(8,128)(2,1)}, u32[]{:S(2)}) %copy-start.6) | copy-done | bytes 4194328
  45.0 4.6 %shard_map.85 = (bf16[128,128]{1,0:T(8,128)(2,1)S(1)}, bf16[128,128]{1,0:T(8,128)(2,1)S(1)}, bf16[128,128]{1,0:T(8,128)(2,1)S(1)}, bf16[128,128]{1,0:T(8,128)(2,...) custom-call(s32[3]{0:T(128)S(1)} %pad_add_fusion.me_ref, ...), custom_call_target="tpu_custom_call" | custom-call | flops 5000000000 | bytes 15000000 | tf_op jit(solution)/shard_map/pallas_call | solution.py:158
  49.6 29.4 %all_to_all.20.cols_ref = bf16[128,16,128]{2,1,0:T(8,128)(2,1)S(1)} all-to-all(bf16[128,16,128]{2,1,0:T(8,128)(2,1)S(1)} %get-tuple-element.22), channel_id=1, replica_groups=mesh['yh'=2,'yl'=2,'xl'=2,'z'=8,'core'=2,'xh'=2] {'yh','yl','xl','z','xh'}, dimensions={0} | all-to-all | bytes 1048576 | tf_op jit(solution)/shard_map/all_to_all | solution.py:304
  79.0 1.8 %shard_map.86 = (f32[128,8,128]{2,1,0:T(8,128)S(1)}, bf16[128,8,128]{2,1,0:T(8,128)(2,1)S(1)}) custom-call(s32[3]{0:T(128)S(1)} %pad_add_fusion.me_ref, bf16[128,16,128]{2,1,0:T(8,128)(2,1)S(1)} %all_to_all.20.cols_ref), custom_call_target="tpu_custom_call" | custom-call | flops 3000000000 | bytes 9000000 | tf_op jit(solution)/shard_map/pallas_call | solution.py:230
  80.9 1.5 %collective-permute-done.3 = bf16[128,8,128]{2,1,0:T(8,128)(2,1)S(1)} collective-permute-done((bf16[128,8,128]{2,1,0:T(8,128)(2,1)S(1)}, bf16[128,8,128]{2,1,0:T(8,128)(2,1)S(1)}, u32[]{:S(2)}, u32[]{:S(2)}) %collective-permute-start.3) | collective-permute-done | bytes 262176 | tf_op jit(solution)/shard_map/ppermute | solution.py:308
  83.2 7.7 %all-to-all-start.3 = ((bf16[128,8,128]{2,1,0:T(8,128)(2,1)}), bf16[128,8,128]{2,1,0:T(8,128)(2,1)S(1)}, u32[]{:S(2)}, u32[]{:S(2)}) async-start(bf16[128,8,128]{2,1,0:T(8,128)(2,1)} %add_convert_fusion), calls=%async_computation.3 | async-start | bytes 524288 | tf_op jit(solution)/shard_map/all_to_all | solution.py:304
  91.0 1.7 %collective-permute-start.5 = (bf16[128,128]{1,0:T(8,128)(2,1)S(1)}, bf16[128,128]{1,0:T(8,128)(2,1)S(1)}, u32[]{:S(2)}, u32[]{:S(2)}) collective-permute-start(bf16[128,128]{1,0:T(8,128)(2,1)S(1)} %get-tuple-element.27), channel_id=1, source_target_pairs={{0,32},{2,34},{32,0},{34,2},{64,96},{66,98},{96,64},{98,66},{1,33}... | collective-permute-start | bytes 98312 | tf_op jit(solution)/shard_map/ppermute | solution.py:324
  94.6 1.4 %collective-permute-start.9 = (bf16[128,128]{1,0:T(8,128)(2,1)S(1)}, bf16[128,128]{1,0:T(8,128)(2,1)S(1)}, u32[]{:S(2)}, u32[]{:S(2)}) collective-permute-start(bf16[128,128]{1,0:T(8,128)(2,1)S(1)} %get-tuple-element.31), channel_id=1, source_target_pairs={{0,96},{2,98},{32,64},{34,66},{64,32},{66,34},{96,0},{98,2},{1,97}... | collective-permute-start | bytes 98312 | tf_op jit(solution)/shard_map/ppermute | solution.py:324
  96.0 1.3 %collective-permute-start.10 = (bf16[128,128]{1,0:T(8,128)(2,1)S(1)}, bf16[128,128]{1,0:T(8,128)(2,1)S(1)}, u32[]{:S(2)}, u32[]{:S(2)}) collective-permute-start(bf16[128,128]{1,0:T(8,128)(2,1)S(1)} %get-tuple-element.32), channel_id=1, source_target_pairs={{0,98},{2,96},{32,66},{34,64},{64,34},{66,32},{96,2},{98,0},{1,99}... | collective-permute-start | bytes 98312 | tf_op jit(solution)/shard_map/ppermute | solution.py:324
  97.9 1.7 %collective-permute-done.9.rest_6_ = bf16[128,128]{1,0:T(8,128)(2,1)S(1)} collective-permute-done((bf16[128,128]{1,0:T(8,128)(2,1)S(1)}, bf16[128,128]{1,0:T(8,128)(2,1)S(1)}, u32[]{:S(2)}, u32[]{:S(2)}) %collective-permute-start.9) | collective-permute-done | bytes 32800 | tf_op jit(solution)/shard_map/ppermute | solution.py:324
  100.4 1.1 shard_map.87
  101.5 3.6 %all-to-all-done.3.mixed_ref = bf16[128,8,128]{2,1,0:T(8,128)(2,1)S(1)} async-done(((bf16[128,8,128]{2,1,0:T(8,128)(2,1)}), bf16[128,8,128]{2,1,0:T(8,128)(2,1)S(1)}, u32[]{:S(2)}, u32[]{:S(2)}) %all-to-all-start.3) | async-done | bytes 262176 | tf_op jit(solution)/shard_map/all_to_all | solution.py:304
  105.1 1.6 %shard_map.88 = bf16[1024,128]{1,0:T(8,128)(2,1)} custom-call(bf16[128,8,128]{2,1,0:T(8,128)(2,1)S(1)} %all-to-all-done.3.mixed_ref, f32[1024,128]{1,0:T(8,128)S(1)} %get-tuple-element.33.gate_ref, f32[1024,128]{1,0:T(8,128)S(1)} %get-tuple-element.34.base_ref, bf16[128,128]{1,0:T(8,128)(2,1)S(1)} %copy-done.4), custom_call_target="tpu_custom_call" | custom-call | flops 2000000000 | bytes 6000000 | tf_op jit(solution)/shard_map/pallas_call | solution.py:294
  (35 shorter events, 10.6 us)
Async XLA Ops:
  0.8 5.9 %collective-permute-start.1 = (bf16[256,16]{1,0:T(8,128)(2,1)S(1)}, bf16[256,16]{1,0:T(8,128)(2,1)S(1)}, u32[]{:S(2)}, u32[]{:S(2)}) collective-permute-start(bf16[256,16]{1,0:T(8,128)(2,1)S(1)} %copy.11.own_ref), channel_id=1, source_target_pairs={{0,1},{1,0},{2,3},{3,2},{4,5},{5,4},{6,7},{7,6},{8,9},{9,8},{10,11... | collective-permute-start | bytes 24584 | tf_op jit(solution)/shard_map/ppermute | solution.py:308
  4.8 1.0 copy-start
  5.8 25.6 %copy-start.2 = (bf16[512,128]{1,0:T(8,128)(2,1)S(1)}, bf16[512,128]{1,0:T(8,128)(2,1)}, u32[]{:S(2)}) copy-start(bf16[512,128]{1,0:T(8,128)(2,1)} %own_ref.2) | copy-start | bytes 393220
  5.8 28.7 %copy-start.7 = (bf16[4,128,128]{2,1,0:T(8,128)(2,1)S(1)}, bf16[4,128,128]{2,1,0:T(8,128)(2,1)}, u32[]{:S(2)}) copy-start(bf16[4,128,128]{2,1,0:T(8,128)(2,1)} %param.13) | copy-start | bytes 393220
  6.7 1.0 copy-start.1
  9.3 13.9 %all-to-all-start.1 = ((bf16[8,256,128]{2,1,0:T(8,128)(2,1)}), bf16[8,256,128]{2,1,0:T(8,128)(2,1)S(1)}, u32[]{:S(2)}, u32[]{:S(2)}) async-start(bf16[8,256,128]{2,1,0:T(8,128)(2,1)} %shard_map.83), calls=%async_computation.1 | async-start | bytes 1048576 | tf_op jit(solution)/shard_map/all_to_all | solution.py:304
  14.9 7.3 %collective-permute-start = (bf16[128,128]{1,0:T(8,128)(2,1)S(1)}, bf16[128,128]{1,0:T(8,128)(2,1)S(1)}, u32[]{:S(2)}, u32[]{:S(2)}) collective-permute-start(bf16[128,128]{1,0:T(8,128)(2,1)S(1)} %get-tuple-element.20), channel_id=1, source_target_pairs={{0,128},{128,0},{1,129},{129,1},{2,130},{130,2},{3,131},{131,3},{4... | collective-permute-start | bytes 98312 | tf_op jit(solution)/shard_map/ppermute | solution.py:308
  23.9 18.9 %all-to-all-start = ((bf16[8,128,128]{2,1,0:T(8,128)(2,1)}), bf16[8,128,128]{2,1,0:T(8,128)(2,1)S(1)}, u32[]{:S(2)}, u32[]{:S(2)}) async-start(bf16[8,128,128]{2,1,0:T(8,128)(2,1)} %broadcast_in_dim.3), calls=%async_computation | async-start | bytes 524288 | tf_op jit(solution)/shard_map/all_to_all | solution.py:304
  31.4 6.6 %collective-permute-start.2 = (bf16[512,128]{1,0:T(8,128)(2,1)S(1)}, bf16[512,128]{1,0:T(8,128)(2,1)S(1)}, u32[]{:S(2)}, u32[]{:S(2)}) collective-permute-start(bf16[512,128]{1,0:T(8,128)(2,1)S(1)} %copy-done.2), channel_id=1, source_target_pairs={{0,1},{1,0},{2,3},{3,2},{4,5},{5,4},{6,7},{7,6},{8,9},{9,8},{10,11... | collective-permute-start | bytes 393224 | tf_op jit(solution)/shard_map/ppermute | solution.py:308
  39.3 1.9 %copy-start.5 = (bf16[4096,512]{1,0:T(8,128)(2,1)}, bf16[4096,512]{1,0:T(8,128)(2,1)S(1)}, u32[]{:S(2)}) copy-start(bf16[4096,512]{1,0:T(8,128)(2,1)S(1)} %shard_map.84.wide_ref) | copy-start | bytes 12582916
  42.8 2.2 %copy-start.6 = (bf16[4096,512]{1,0:T(8,128)(2,1)S(1)}, bf16[4096,512]{1,0:T(8,128)(2,1)}, u32[]{:S(2)}) copy-start(bf16[4096,512]{1,0:T(8,128)(2,1)} %copy-done.5) | copy-start | bytes 12582916
  79.0 21.4 %copy-start.3 = (bf16[128,128]{1,0:T(8,128)(2,1)S(1)}, bf16[128,128]{1,0:T(8,128)(2,1)}, u32[]{:S(2)}) copy-start(bf16[128,128]{1,0:T(8,128)(2,1)} %rest_8_.1) | copy-start | bytes 98308
  80.8 1.6 %collective-permute-start.3 = (bf16[128,8,128]{2,1,0:T(8,128)(2,1)S(1)}, bf16[128,8,128]{2,1,0:T(8,128)(2,1)S(1)}, u32[]{:S(2)}, u32[]{:S(2)}) collective-permute-start(bf16[128,8,128]{2,1,0:T(8,128)(2,1)S(1)} %get-tuple-element.24), channel_id=1, source_target_pairs={{0,2},{2,0},{1,3},{3,1},{4,6},{6,4},{5,7},{7,5},{8,10},{10,8},{9,1... | collective-permute-start | bytes 786440 | tf_op jit(solution)/shard_map/ppermute | solution.py:308
  83.2 21.9 %copy-start.4 = (bf16[128,128]{1,0:T(8,128)(2,1)S(1)}, bf16[128,128]{1,0:T(8,128)(2,1)}, u32[]{:S(2)}) copy-start(bf16[128,128]{1,0:T(8,128)(2,1)} %w_ref.1) | copy-start | bytes 98308
  83.2 21.9 %all-to-all-start.3 = ((bf16[128,8,128]{2,1,0:T(8,128)(2,1)}), bf16[128,8,128]{2,1,0:T(8,128)(2,1)S(1)}, u32[]{:S(2)}, u32[]{:S(2)}) async-start(bf16[128,8,128]{2,1,0:T(8,128)(2,1)} %add_convert_fusion), calls=%async_computation.3 | async-start | bytes 524288 | tf_op jit(solution)/shard_map/all_to_all | solution.py:304
  90.9 3.7 %collective-permute-start.4 = (bf16[128,128]{1,0:T(8,128)(2,1)S(1)}, bf16[128,128]{1,0:T(8,128)(2,1)S(1)}, u32[]{:S(2)}, u32[]{:S(2)}) collective-permute-start(bf16[128,128]{1,0:T(8,128)(2,1)S(1)} %get-tuple-element.26), channel_id=1, source_target_pairs={{0,2},{2,0},{32,34},{34,32},{64,66},{66,64},{96,98},{98,96},{1,3},... | collective-permute-start | bytes 98312 | tf_op jit(solution)/shard_map/ppermute | solution.py:324
  91.0 5.0 %collective-permute-start.5 = (bf16[128,128]{1,0:T(8,128)(2,1)S(1)}, bf16[128,128]{1,0:T(8,128)(2,1)S(1)}, u32[]{:S(2)}, u32[]{:S(2)}) collective-permute-start(bf16[128,128]{1,0:T(8,128)(2,1)S(1)} %get-tuple-element.27), channel_id=1, source_target_pairs={{0,32},{2,34},{32,0},{34,2},{64,96},{66,98},{96,64},{98,66},{1,33}... | collective-permute-start | bytes 98312 | tf_op jit(solution)/shard_map/ppermute | solution.py:324
  92.7 4.6 %collective-permute-start.6 = (bf16[128,128]{1,0:T(8,128)(2,1)S(1)}, bf16[128,128]{1,0:T(8,128)(2,1)S(1)}, u32[]{:S(2)}, u32[]{:S(2)}) collective-permute-start(bf16[128,128]{1,0:T(8,128)(2,1)S(1)} %get-tuple-element.28), channel_id=1, source_target_pairs={{0,34},{2,32},{32,2},{34,0},{64,98},{66,96},{96,66},{98,64},{1,35}... | collective-permute-start | bytes 98312 | tf_op jit(solution)/shard_map/ppermute | solution.py:324
  92.9 4.5 %collective-permute-start.7 = (bf16[128,128]{1,0:T(8,128)(2,1)S(1)}, bf16[128,128]{1,0:T(8,128)(2,1)S(1)}, u32[]{:S(2)}, u32[]{:S(2)}) collective-permute-start(bf16[128,128]{1,0:T(8,128)(2,1)S(1)} %get-tuple-element.29), channel_id=1, source_target_pairs={{0,64},{2,66},{32,96},{34,98},{64,0},{66,2},{96,32},{98,34},{1,65}... | collective-permute-start | bytes 98312 | tf_op jit(solution)/shard_map/ppermute | solution.py:324
  93.7 4.2 %collective-permute-start.8 = (bf16[128,128]{1,0:T(8,128)(2,1)S(1)}, bf16[128,128]{1,0:T(8,128)(2,1)S(1)}, u32[]{:S(2)}, u32[]{:S(2)}) collective-permute-start(bf16[128,128]{1,0:T(8,128)(2,1)S(1)} %get-tuple-element.30), channel_id=1, source_target_pairs={{0,66},{2,64},{32,98},{34,96},{64,2},{66,0},{96,34},{98,32},{1,67}... | collective-permute-start | bytes 98312 | tf_op jit(solution)/shard_map/ppermute | solution.py:324
  94.6 5.0 %collective-permute-start.9 = (bf16[128,128]{1,0:T(8,128)(2,1)S(1)}, bf16[128,128]{1,0:T(8,128)(2,1)S(1)}, u32[]{:S(2)}, u32[]{:S(2)}) collective-permute-start(bf16[128,128]{1,0:T(8,128)(2,1)S(1)} %get-tuple-element.31), channel_id=1, source_target_pairs={{0,96},{2,98},{32,64},{34,66},{64,32},{66,34},{96,0},{98,2},{1,97}... | collective-permute-start | bytes 98312 | tf_op jit(solution)/shard_map/ppermute | solution.py:324
  96.0 4.4 %collective-permute-start.10 = (bf16[128,128]{1,0:T(8,128)(2,1)S(1)}, bf16[128,128]{1,0:T(8,128)(2,1)S(1)}, u32[]{:S(2)}, u32[]{:S(2)}) collective-permute-start(bf16[128,128]{1,0:T(8,128)(2,1)S(1)} %get-tuple-element.32), channel_id=1, source_target_pairs={{0,98},{2,96},{32,66},{34,64},{64,34},{66,32},{96,2},{98,0},{1,99}... | collective-permute-start | bytes 98312 | tf_op jit(solution)/shard_map/ppermute | solution.py:324

commit v3 on v2

--- a/solution.py
+++ b/solution.py
@@ -12,7 +12,6 @@
 F32 = jnp.float32
 BF16 = jnp.bfloat16
 VMEM = pl.BlockSpec(memory_space=pltpu.VMEM)
-ANY = pl.BlockSpec(memory_space=pl.ANY)
 SMEM = pl.BlockSpec(memory_space=pltpu.SMEM)
 
 
@@ -27,11 +26,11 @@
     return centred * lax.rsqrt(var + 1e-05)
 
 
-def on_core(kernel, outs, n_in, scratch=(), scalars=0, elsewhere=(), cost=None, limit=12):
+def on_core(kernel, outs, n_in, scratch=(), scalars=0, cost=None, limit=12):
     return pl.pallas_call(
         kernel,
         out_shape=outs,
-        in_specs=[SMEM if i < scalars else ANY if i in elsewhere else VMEM for i in range(n_in)],
+        in_specs=[SMEM if i < scalars else VMEM for i in range(n_in)],
         out_specs=jax.tree.map(lambda _: VMEM, outs),
         scratch_shapes=scratch,
         compiler_params=pltpu.CompilerParams(vmem_limit_bytes=limit << 20),
@@ -44,135 +43,152 @@
 
 
 def first_kernel(msa_ref, second_ref, right_ref, norm_ref):
-    x = [msa_ref[:, i, :].astype(F32) for i in range(4)]
     for i in range(4):
-        normed = standardized(x[i], -1).astype(BF16)
+        normed = standardized(msa_ref[:, i, :].astype(F32), -1).astype(BF16)
         norm_ref[i] = normed
-        right_ref[i * 32 : (i + 1) * 32, :] = dot(second_ref[...], normed, ((0,), (1,))).astype(BF16)
-
-
-def firsts(msa, second):
+        right_ref[i * 32 : (i + 1) * 32, :] = dot(second_ref[...], normed, ((1,), (1,))).astype(BF16)
+
+
+def firsts(msa, second_t):
     return on_core(
         first_kernel,
         (jax.ShapeDtypeStruct((128, 128), BF16), jax.ShapeDtypeStruct((4, 128, 256), BF16)),
         2,
         cost=cost(1),
-    )(msa, second)
-
-
-def pack_kernel(me_ref, norm_ref, own_ref, other_ref, couple_ref, packed_ref):
-    mex = me_ref[1]
+    )(msa, second_t)
+
+
+def spread_kernel(me_ref, own_ref, other_ref, all_ref):
+    @pl.when(me_ref[3] == 1)
+    def _():
+        for z in range(8):
+            all_ref[z] = own_ref[...]
+
+    @pl.when(me_ref[3] == 0)
+    def _():
+        for z in range(8):
+            all_ref[z] = other_ref[...]
+
+
+def spreads(me, own, other):
+    return on_core(
+        spread_kernel, jax.ShapeDtypeStruct((8, 128, 128), BF16), 3, scalars=1, cost=cost(1)
+    )(me, own, other)
+
+
+def pack_kernel(me_ref, norm_ref, own_ref, other_ref, couple_ref, *packed_refs):
+    me, mex = me_ref[0], me_ref[1]
     for i in range(4):
         normed = norm_ref[i]
-        lo = dot(own_ref[...], normed, ((0,), (1,))).astype(BF16)
-        hi = dot(other_ref[...], normed, ((0,), (1,))).astype(BF16)
-        for g in range(8):
-            packed_ref[g, pl.ds(pl.multiple_of(128 + mex * 64 + i * 16, 16), 16), :] = lo
-            packed_ref[g, pl.ds(pl.multiple_of(192 - mex * 64 + i * 16, 16), 16), :] = hi
+        lo = dot(own_ref[...], normed, ((1,), (1,))).astype(BF16)
+        hi = dot(other_ref[...], normed, ((1,), (1,))).astype(BF16)
+        for m in range(8):
+            packed_refs[m][pl.ds(pl.multiple_of(128 + mex * 64 + i * 16, 16), 16), :] = lo
+            packed_refs[m][pl.ds(pl.multiple_of(192 - mex * 64 + i * 16, 16), 16), :] = hi
     row = lax.broadcasted_iota(jnp.int32, (8, 128), 0)
-    for i in range(4):
-        for y in range(4):
+    for m in range(8):
+        g = m ^ me
+        keep = (row < 4) == (g % 2 == 0)
+        for i in range(4):
             for zz in range(4):
-                pair = couple_ref[i, (y * 8 + zz * 2) * 8 : (y * 8 + zz * 2 + 2) * 8, :].astype(F32)
+                start = pl.multiple_of((g // 2) * 64 + zz * 16, 16)
+                pair = couple_ref[i, pl.ds(start, 16), :].astype(F32)
                 a, b = pair[:8], pair[8:]
+                low = jnp.where(keep, a, pltpu.roll(a, 4, 0))
+                high = jnp.where(keep, b, pltpu.roll(b, 4, 0))
                 rows = slice(i * 32 + zz * 8, i * 32 + zz * 8 + 8)
-                packed_ref[y * 2, rows, :] = jnp.where(row < 4, a, pltpu.roll(b, 4, 0)).astype(BF16)
-                packed_ref[y * 2 + 1, rows, :] = jnp.where(row < 4, pltpu.roll(a, 4, 0), b).astype(BF16)
-
-
-def packs(me, normed, own, other, couple):
-    return on_core(
-        pack_kernel, jax.ShapeDtypeStruct((8, 256, 128), BF16), 5, scalars=1, cost=cost(1)
-    )(me, normed, own, other, couple)
-
-
-def wide_kernel(me_ref, own_ref, other_ref, wide_ref, w_scr):
+                packed_refs[m][rows, :] = jnp.where(row < 4, low, high).astype(BF16)
+
+
+def packs(me, normed, own_t, other_t, couple):
+    return on_core(
+        pack_kernel, (jax.ShapeDtypeStruct((256, 128), BF16),) * 8, 5, scalars=1, cost=cost(1)
+    )(me, normed, own_t, other_t, couple)
+
+
+def weight_kernel(me_ref, own_ref, other_ref, by_e_ref, w_scr):
     mex = me_ref[1]
     w_scr[pl.ds(pl.multiple_of(mex * 512, 512), 512), :] = own_ref[...].astype(F32)
     w_scr[pl.ds(pl.multiple_of(512 - mex * 512, 512), 512), :] = other_ref[...].astype(F32)
-    wide_ref[...] = jnp.zeros_like(wide_ref)
     for e in range(32):
-        w = w_scr[pl.ds(e, 32, stride=32), :].astype(BF16)
-        for x in range(2):
-            for i in range(4):
-                row = ((e * 2 + x) * 4 + i) * 16
-                wide_ref[row : row + 16, i * 128 : (i + 1) * 128] = w[x * 16 : (x + 1) * 16]
-
-
-def widened(me, own, other):
-    return on_core(
-        wide_kernel,
-        jax.ShapeDtypeStruct((4096, 512), BF16),
+        by_e_ref[e] = w_scr[pl.ds(e, 32, stride=32), :].astype(BF16)
+
+
+def weights(me, own, other):
+    return on_core(
+        weight_kernel,
+        jax.ShapeDtypeStruct((32, 32, 128), BF16),
         3,
         [pltpu.VMEM((1024, 128), F32)],
         scalars=1,
-        cost=cost(2),
+        cost=cost(1),
     )(me, own, other)
 
 
-def pair_kernel(me_ref, right_ref, packed_ref, wide_ref, entry_ref, *rest):
-    lifted_refs, cols_ref = rest[:8], rest[8]
-    rows_scr, lhs_scr, cols_scr, norm_scr, up_scr, wide_scr, sem = rest[9:]
+def pair_kernel(me_ref, right_ref, *rest):
+    packed_refs, by_e_ref, entry_ref = rest[:8], rest[8], rest[9]
+    lifted_refs, cols_ref = rest[10:18], rest[18]
+    rows_scr, lhs_scr, cols_scr, wide_scr = rest[19:]
     me = me_ref[0]
-    fetch = pltpu.make_async_copy(wide_ref, wide_scr, sem)
-    fetch.start()
     for z in range(8):
         for j in range(4):
             rows_scr[pl.ds(z * 4 + j, 32, stride=32), :] = right_ref[z, j * 32 : (j + 1) * 32, :].astype(F32)
-    lefts = jnp.concatenate([packed_ref[g, 128:256, :] for g in range(8)], axis=0)
+    lefts = jnp.concatenate([packed_refs[m][128:256, :] for m in range(8)], axis=0)
+    blank = jnp.zeros((16, 128), BF16)
     for part in range(4):
+        for e in range(part * 8, part * 8 + 8):
+            for x in range(2):
+                for i in range(4):
+                    for j in range(4):
+                        row = ((e * 2 + x) * 4 + i) * 16
+                        wide_scr[row : row + 16, j * 128 : (j + 1) * 128] = (
+                            by_e_ref[e, x * 16 : (x + 1) * 16, :] if i == j else blank
+                        )
         rows = rows_scr[part * 256 : (part + 1) * 256, :].astype(BF16)
         outer = (dot(rows, lefts, ((1,), (1,))) * (1.0 / 128)).astype(BF16)
         for e in range(8):
-            for g in range(8):
-                lhs_scr[g * 32 : (g + 1) * 32, (part * 8 + e) * 128 : (part * 8 + e + 1) * 128] = outer[
-                    e * 32 : (e + 1) * 32, g * 128 : (g + 1) * 128
+            for m in range(8):
+                lhs_scr[m * 32 : (m + 1) * 32, (part * 8 + e) * 128 : (part * 8 + e + 1) * 128] = outer[
+                    e * 32 : (e + 1) * 32, m * 128 : (m + 1) * 128
                 ]
-    fetch.wait()
     for half in range(2):
-        rows = slice(half * 128, (half + 1) * 128)
-        up_scr[rows, :] = dot(lhs_scr[rows, :], wide_scr[...], ((1,), (0,)))
-    for m in range(8):
-        g = m ^ me
-        for i in range(4):
-            lifted = (
-                packed_ref[g, i * 32 : (i + 1) * 32, :].astype(F32)
-                + up_scr[pl.ds(pl.multiple_of(g * 32, 32), 32), i * 128 : (i + 1) * 128]
-            ).astype(BF16)
-            lifted_refs[m][i * 32 : (i + 1) * 32, :] = lifted
-            norm_scr[pl.ds(pl.multiple_of(g * 128 + i * 32, 32), 32), :] = standardized(
-                lifted.astype(F32), -1
-            ).astype(BF16)
-    for g in range(8):
-        normed = norm_scr[g * 128 : (g + 1) * 128, :]
-        p = [dot(entry_ref[q], normed, ((1,), (1,))) for q in range(4)]
-        cols_scr[pl.ds(g, 128, stride=16), :] = jax.nn.sigmoid(p[0]) * p[1]
-        cols_scr[pl.ds(8 + g, 128, stride=16), :] = jax.nn.sigmoid(p[2]) * p[3]
+        update = dot(lhs_scr[half * 128 : (half + 1) * 128, :], wide_scr[...], ((1,), (0,)))
+        for mm in range(4):
+            m = half * 4 + mm
+            normed = []
+            for i in range(4):
+                rows = slice(i * 32, (i + 1) * 32)
+                lifted = (
+                    packed_refs[m][rows, :].astype(F32)
+                    + update[mm * 32 : (mm + 1) * 32, i * 128 : (i + 1) * 128]
+                ).astype(BF16)
+                lifted_refs[m][rows, :] = lifted
+                normed.append(standardized(lifted.astype(F32), -1).astype(BF16))
+            normed = jnp.concatenate(normed, axis=0)
+            p = [dot(entry_ref[q], normed, ((1,), (1,))) for q in range(4)]
+            cols_scr[pl.ds(m ^ me, 128, stride=16), :] = jax.nn.sigmoid(p[0]) * p[1]
+            cols_scr[pl.ds(8 + (m ^ me), 128, stride=16), :] = jax.nn.sigmoid(p[2]) * p[3]
     for part in range(8):
         cols_ref[part * 16 : (part + 1) * 16] = (
             cols_scr[part * 256 : (part + 1) * 256, :].reshape(16, 16, 128).astype(BF16)
         )
 
 
-def pairs(me, right, packed, wide, entry_t):
+def pairs(me, right, packed, by_e, entry_t):
     out = on_core(
         pair_kernel,
         (jax.ShapeDtypeStruct((128, 128), BF16),) * 8 + (jax.ShapeDtypeStruct((128, 16, 128), BF16),),
-        5,
+        12,
         [
             pltpu.VMEM((1024, 128), F32),
             pltpu.VMEM((256, 4096), BF16),
             pltpu.VMEM((2048, 128), F32),
-            pltpu.VMEM((1024, 128), BF16),
-            pltpu.VMEM((256, 512), F32),
             pltpu.VMEM((4096, 512), BF16),
-            pltpu.SemaphoreType.DMA(()),
         ],
-        elsewhere=(3,),
+        scalars=1,
         limit=20,
-        scalars=1,
         cost=cost(5),
-    )(me, right, packed, wide, entry_t)
+    )(me, right, *packed, by_e, entry_t)
     return out[:8], out[8]
 
 
@@ -308,21 +324,29 @@
     return lax.ppermute(x, axis, [(0, 1), (1, 0)])
 
 
+def to_peers(pieces):
+    sent = [lax.ppermute(pieces[m], PLANE, [(i, i ^ m) for i in range(8)]) for m in range(1, 8)]
+    return [pieces[0], *sent]
+
+
 def per_device(msa, couple, first, second, w_out, entry, w_gate, w_final):
     at = {name: lax.axis_index(name) for name in ("yh", "yl", "xl", "core", "xh")}
-    me = jnp.stack([at["yl"] * 4 + at["xl"] * 2 + at["core"], at["xh"], at["core"]]).astype(jnp.int32)
-    first_other = partner(first, "xh")
+    me = jnp.stack(
+        [at["yl"] * 4 + at["xl"] * 2 + at["core"], at["xh"], at["core"], (at["yh"] == at["xh"]).astype(jnp.int32)]
+    ).astype(jnp.int32)
+    right, normed = firsts(msa, second.T)
+    first_t, w_out, right = lax.optimization_barrier((first.T, w_out, right))
+    right = spreads(me, right, partner(right, "yh"))
+    first_other = partner(first_t, "xh")
     w_other = partner(w_out, "xh")
-    right, normed = firsts(msa, second)
-    right = jnp.where(at["yh"] == at["xh"], right, partner(right, "yh"))
-    packed = exchanged(packs(me, normed, first, first_other, couple), PLANE)
-    right = exchanged(jnp.broadcast_to(right, (8, 128, 128)), "z")
-    wide = widened(me, w_out, w_other)
-    lifted, cols = pairs(me, right, packed, wide, jnp.swapaxes(entry, 1, 2))
+    right, normed = lax.optimization_barrier((right, normed))
+    right = exchanged(right, "z")
+    packed = to_peers(packs(me, normed, first_t, first_other, couple))
+    by_e = weights(me, w_out, w_other)
+    lifted, cols = pairs(me, right, packed, by_e, jnp.swapaxes(entry, 1, 2))
     cols = exchanged(cols, CHIP)
-    own = [lifted[0]]
-    own += [lax.ppermute(lifted[m], PLANE, [(i, i ^ m) for i in range(8)]) for m in range(1, 8)]
-    gate, base = gates(me, own, w_gate)
+    gate, base = gates(me, to_peers(lifted), w_gate)
+    me, gate, base = lax.optimization_barrier((me, gate, base))
     mine, theirs = products(me, cols)
     summed = (mine + partner(theirs, "core").astype(F32)).astype(BF16)
     mixed = exchanged(summed, CHIP)

time: 107 us -> 101 us (0.944)
  blocking collectives: 29.4 us -> 21.5 us
  starting transfers between devices: 34.4 us -> 41.4 us
  local copies, waits for them, and re-layouts: 8.56 us -> 1.82 us
  Pallas kernels: 12.4 us -> 13.6 us
    all_to_all x1, blocking collectives: 29.4 us -> 21.5 us  [exchanged(): return lax.all_to_all(x, axes, split_axis=0, concat_axis=0, tiled=True)]
    unnamed x19 -> x17, local copies, waits for them, and re-layouts: 7.82 us -> 1.82 us
    ppermute x7 -> x14, starting transfers between devices: 6.36 us -> 12.1 us  [to_peers(): lax.ppermute(pieces[m], PLANE, [(i, i ^ m) for i in range(8)])]
    ppermute x4, waiting for transfers between devices: 11.6 us -> 6.19 us  [partner(): return lax.ppermute(x, axis, [(0, 1), (1, 0)])]
    ppermute x7 -> x14, waiting for transfers between devices: 3.12 us -> 7.73 us  [to_peers(): lax.ppermute(pieces[m], PLANE, [(i, i ^ m) for i in range(8)])]
    all_to_all x3 -> x2, starting transfers between devices: 20.9 us -> 23.2 us  [exchanged(): return lax.all_to_all(x, axes, split_axis=0, concat_axis=0, tiled=True)]
    all_to_all x3 -> x2, waiting for transfers between devices: 6.2 us -> 7.96 us  [exchanged(): return lax.all_to_all(x, axes, split_axis=0, concat_axis=0, tiled=True)]
    pallas_call x1, Pallas kernels: 4.55 us -> 5.65 us  [pairs(): on_core(pair_kernel, (jax.ShapeDtypeStruct((128, 128), BF16),) * 8 + (jax...]
  transfers between devices with their start and end apart: 14 -> 20, of which waited for: 11 -> 11; matrix products, arithmetic and copies ran while one was open for 1% -> 0% of each run, Pallas kernels for 3% -> 3%
where the time goes in v3:
time: 101 us
  starting transfers between devices  41.4 us (41%)
  waiting for transfers between devices  21.9 us (22%)
  blocking collectives  21.5 us (21%)
  Pallas kernels  13.6 us (13%)
  local copies, waits for them, and re-layouts  1.82 us (2%)
    all_to_all x2, starting transfers between devices, exchanged(): return lax.all_to_all(x, axes, split_axis=0, concat_axis=0, tiled=True)  23.2 us
    all_to_all x1, blocking collectives, exchanged(): return lax.all_to_all(x, axes, split_axis=0, concat_axis=0, tiled=True)  21.5 us
    ppermute x14, starting transfers between devices, to_peers(): lax.ppermute(pieces[m], PLANE, [(i, i ^ m) for i in range(8)])  12.1 us
    all_to_all x2, waiting for transfers between devices, exchanged(): return lax.all_to_all(x, axes, split_axis=0, concat_axis=0, tiled=True)  7.96 us
    ppermute x14, waiting for transfers between devices, to_peers(): lax.ppermute(pieces[m], PLANE, [(i, i ^ m) for i in range(8)])  7.73 us
    ppermute x4, waiting for transfers between devices, partner(): return lax.ppermute(x, axis, [(0, 1), (1, 0)])  6.19 us
    ppermute x4, starting transfers between devices, partner(): return lax.ppermute(x, axis, [(0, 1), (1, 0)])  6.09 us
    pallas_call x1, Pallas kernels, pairs(): on_core(pair_kernel, (jax.ShapeDtypeStruct((128, 128), BF16),) * 8 + (jax...  5.65 us
  transfers between devices with their start and end apart: 20, of which 11 were waited for; matrix products, arithmetic and copies ran while one was open for 0% of the time, Pallas kernels for 3%

profile of v3, /device:TPU:8, one launch (start us, length us, event | category | flops | bytes accessed | tf_op | source)
XLA Modules:
  0.0 100.6 jit_solution(17111293637956378886)
XLA Ops:
  0.0 0.9 copy-done
  2.2 2.4 %collective-permute-start = (bf16[128,128]{1,0:T(8,128)(2,1)S(1)}, bf16[128,128]{1,0:T(8,128)(2,1)S(1)}, u32[]{:S(2)}, u32[]{:S(2)}) collective-permute-start(bf16[128,128]{1,0:T(8,128)(2,1)S(1)} %get-tuple-element.37.own_ref), channel_id=1, source_target_pairs={{0,128},{128,0},{1,129},{129,1},{2,130},{130,2},{3,131},{131,3},{4... | collective-permute-start | bytes 98312 | tf_op jit(solution)/shard_map/ppermute | solution.py:324
  4.7 3.0 %collective-permute-done.other_ref = bf16[128,128]{1,0:T(8,128)(2,1)S(1)} collective-permute-done((bf16[128,128]{1,0:T(8,128)(2,1)S(1)}, bf16[128,128]{1,0:T(8,128)(2,1)S(1)}, u32[]{:S(2)}, u32[]{:S(2)}) %collective-permute-start) | collective-permute-done | bytes 32800 | tf_op jit(solution)/shard_map/ppermute | solution.py:324
  7.7 1.3 %shard_map.83 = bf16[8,128,128]{2,1,0:T(8,128)(2,1)} custom-call(s32[4]{0:T(128)S(1)} %pad_add_fusion.me_ref, bf16[128,128]{1,0:T(8,128)(2,1)S(1)} %get-tuple-element.37.own_ref, bf16[128,128]{1,0:T(8,128)(2,1)S(1)} %collective-permute-done.other_ref), custom_call_target="tpu_custom_call" | custom-call | flops 1000000000 | bytes 3000000 | tf_op jit(solution)/shard_map/pallas_call | solution.py:74
  9.0 8.6 %all-to-all-start = ((bf16[8,128,128]{2,1,0:T(8,128)(2,1)}), bf16[8,128,128]{2,1,0:T(8,128)(2,1)S(1)}, u32[]{:S(2)}, u32[]{:S(2)}) async-start(bf16[8,128,128]{2,1,0:T(8,128)(2,1)} %shard_map.83), calls=%async_computation | async-start | bytes 524288 | tf_op jit(solution)/shard_map/all_to_all | solution.py:320
  17.6 3.1 %collective-permute-start.1 = (bf16[16,256]{1,0:T(8,128)(2,1)S(1)}, bf16[16,256]{1,0:T(8,128)(2,1)S(1)}, u32[]{:S(2)}, u32[]{:S(2)}) collective-permute-start(bf16[16,256]{1,0:T(8,128)(2,1)S(1)} %bitcast.10), channel_id=1, source_target_pairs={{0,1},{1,0},{2,3},{3,2},{4,5},{5,4},{6,7},{7,6},{8,9},{9,8},{10,11... | collective-permute-start | bytes 24584 | tf_op jit(solution)/shard_map/ppermute | solution.py:324
  21.2 1.6 %collective-permute-done.1.other_ref = bf16[16,256]{1,0:T(8,128)(2,1)S(1)} collective-permute-done((bf16[16,256]{1,0:T(8,128)(2,1)S(1)}, bf16[16,256]{1,0:T(8,128)(2,1)S(1)}, u32[]{:S(2)}, u32[]{:S(2)}) %collective-permute-start.1) | collective-permute-done | bytes 8224 | tf_op jit(solution)/shard_map/ppermute | solution.py:324
  23.9 1.6 %collective-permute-start.3 = (bf16[256,128]{1,0:T(8,128)(2,1)S(1)}, bf16[256,128]{1,0:T(8,128)(2,1)S(1)}, u32[]{:S(2)}, u32[]{:S(2)}) collective-permute-start(bf16[256,128]{1,0:T(8,128)(2,1)S(1)} %get-tuple-element.44), channel_id=1, source_target_pairs={{0,32},{2,34},{32,0},{34,2},{64,96},{66,98},{96,64},{98,66},{1,33}... | collective-permute-start | bytes 196616 | tf_op jit(solution)/shard_map/ppermute | solution.py:328
  26.4 1.2 %collective-permute-start.6 = (bf16[256,128]{1,0:T(8,128)(2,1)S(1)}, bf16[256,128]{1,0:T(8,128)(2,1)S(1)}, u32[]{:S(2)}, u32[]{:S(2)}) collective-permute-start(bf16[256,128]{1,0:T(8,128)(2,1)S(1)} %get-tuple-element.47), channel_id=1, source_target_pairs={{0,66},{2,64},{32,98},{34,96},{64,2},{66,0},{96,34},{98,32},{1,67}... | collective-permute-start | bytes 196616 | tf_op jit(solution)/shard_map/ppermute | solution.py:328
  28.4 1.9 %collective-permute-start.7 = (bf16[256,128]{1,0:T(8,128)(2,1)S(1)}, bf16[256,128]{1,0:T(8,128)(2,1)S(1)}, u32[]{:S(2)}, u32[]{:S(2)}) collective-permute-start(bf16[256,128]{1,0:T(8,128)(2,1)S(1)} %get-tuple-element.48), channel_id=1, source_target_pairs={{0,96},{2,98},{32,64},{34,66},{64,32},{66,34},{96,0},{98,2},{1,97}... | collective-permute-start | bytes 196616 | tf_op jit(solution)/shard_map/ppermute | solution.py:328
  31.3 2.3 %collective-permute-done.7.rest_6_ = bf16[256,128]{1,0:T(8,128)(2,1)S(1)} collective-permute-done((bf16[256,128]{1,0:T(8,128)(2,1)S(1)}, bf16[256,128]{1,0:T(8,128)(2,1)S(1)}, u32[]{:S(2)}, u32[]{:S(2)}) %collective-permute-start.7) | collective-permute-done | bytes 65568 | tf_op jit(solution)/shard_map/ppermute | solution.py:328
  33.5 1.4 %collective-permute-done.8.rest_7_ = bf16[256,128]{1,0:T(8,128)(2,1)S(1)} collective-permute-done((bf16[256,128]{1,0:T(8,128)(2,1)S(1)}, bf16[256,128]{1,0:T(8,128)(2,1)S(1)}, u32[]{:S(2)}, u32[]{:S(2)}) %collective-permute-start.8) | collective-permute-done | bytes 65568 | tf_op jit(solution)/shard_map/ppermute | solution.py:328
  34.9 5.6 %shard_map.86 = (bf16[128,128]{1,0:T(8,128)(2,1)S(1)}, bf16[128,128]{1,0:T(8,128)(2,1)S(1)}, bf16[128,128]{1,0:T(8,128)(2,1)S(1)}, bf16[128,128]{1,0:T(8,128)(2,...) custom-call(s32[4]{0:T(128)S(1)} %pad_add_fusion.me_ref, ...), custom_call_target="tpu_custom_call" | custom-call | flops 5000000000 | bytes 15000000 | tf_op jit(solution)/shard_map/pallas_call | solution.py:178
  40.6 14.6 %all-to-all-start.1 = ((bf16[128,16,128]{2,1,0:T(8,128)(2,1)}), bf16[128,16,128]{2,1,0:T(8,128)(2,1)S(1)}, u32[]{:S(2)}, u32[]{:S(2)}) async-start(bf16[128,16,128]{2,1,0:T(8,128)(2,1)} %get-tuple-element.62), calls=%async_computation.1 | async-start | bytes 1048576 | tf_op jit(solution)/shard_map/all_to_all | solution.py:320
  55.3 1.7 %collective-permute-start.11 = (bf16[128,128]{1,0:T(8,128)(2,1)S(1)}, bf16[128,128]{1,0:T(8,128)(2,1)S(1)}, u32[]{:S(2)}, u32[]{:S(2)}) collective-permute-start(bf16[128,128]{1,0:T(8,128)(2,1)S(1)} %get-tuple-element.53), channel_id=1, source_target_pairs={{0,32},{2,34},{32,0},{34,2},{64,96},{66,98},{96,64},{98,66},{1,33}... | collective-permute-start | bytes 98312 | tf_op jit(solution)/shard_map/ppermute | solution.py:328
  58.9 1.4 %collective-permute-start.15 = (bf16[128,128]{1,0:T(8,128)(2,1)S(1)}, bf16[128,128]{1,0:T(8,128)(2,1)S(1)}, u32[]{:S(2)}, u32[]{:S(2)}) collective-permute-start(bf16[128,128]{1,0:T(8,128)(2,1)S(1)} %get-tuple-element.57), channel_id=1, source_target_pairs={{0,96},{2,98},{32,64},{34,66},{64,32},{66,34},{96,0},{98,2},{1,97}... | collective-permute-start | bytes 98312 | tf_op jit(solution)/shard_map/ppermute | solution.py:328
  60.3 1.3 %collective-permute-start.16 = (bf16[128,128]{1,0:T(8,128)(2,1)S(1)}, bf16[128,128]{1,0:T(8,128)(2,1)S(1)}, u32[]{:S(2)}, u32[]{:S(2)}) collective-permute-start(bf16[128,128]{1,0:T(8,128)(2,1)S(1)} %get-tuple-element.58), channel_id=1, source_target_pairs={{0,98},{2,96},{32,66},{34,64},{64,34},{66,32},{96,2},{98,0},{1,99}... | collective-permute-start | bytes 98312 | tf_op jit(solution)/shard_map/ppermute | solution.py:328
  62.2 2.1 %collective-permute-done.15.rest_6_ = bf16[128,128]{1,0:T(8,128)(2,1)S(1)} collective-permute-done((bf16[128,128]{1,0:T(8,128)(2,1)S(1)}, bf16[128,128]{1,0:T(8,128)(2,1)S(1)}, u32[]{:S(2)}, u32[]{:S(2)}) %collective-permute-start.15) | collective-permute-done | bytes 32800 | tf_op jit(solution)/shard_map/ppermute | solution.py:328
  65.0 1.1 %shard_map.87 = (f32[1024,128]{1,0:T(8,128)S(1)}, f32[1024,128]{1,0:T(8,128)S(1)}) custom-call(s32[4]{0:T(128)S(1)} %pad_add_fusion.me_ref, bf16[128,128]{1,0:T(8,128)(2,1)S(1)} %get-tuple-element.51.rest_0_, bf16[128,128]{1,0:T(8,128)(2,1)S(1)} %collective-permute-done.10.rest_1_, bf16[128,128]{1,0:T(8,128)(2,1)S(1)} %collective-permute-done.11.rest_2_, ...), custom_call_target="tpu_custom_call" | custom-call | flops 2000000000 | bytes 6000000 | tf_op jit(solution)/shard_map/pallas_call | solution.py:283
  66.0 8.0 %all-to-all-done.1.cols_ref = bf16[128,16,128]{2,1,0:T(8,128)(2,1)S(1)} async-done(((bf16[128,16,128]{2,1,0:T(8,128)(2,1)}), bf16[128,16,128]{2,1,0:T(8,128)(2,1)S(1)}, u32[]{:S(2)}, u32[]{:S(2)}) %all-to-all-start.1) | async-done | bytes 524320 | tf_op jit(solution)/shard_map/all_to_all | solution.py:320
  74.0 1.8 %shard_map.88 = (f32[128,8,128]{2,1,0:T(8,128)S(1)}, bf16[128,8,128]{2,1,0:T(8,128)(2,1)S(1)}) custom-call(s32[4]{0:T(128)S(1)} %pad_add_fusion.me_ref, bf16[128,16,128]{2,1,0:T(8,128)(2,1)S(1)} %all-to-all-done.1.cols_ref), custom_call_target="tpu_custom_call" | custom-call | flops 3000000000 | bytes 9000000 | tf_op jit(solution)/shard_map/pallas_call | solution.py:246
  75.8 1.5 %collective-permute-done.17 = bf16[128,8,128]{2,1,0:T(8,128)(2,1)S(1)} collective-permute-done((bf16[128,8,128]{2,1,0:T(8,128)(2,1)S(1)}, bf16[128,8,128]{2,1,0:T(8,128)(2,1)S(1)}, u32[]{:S(2)}, u32[]{:S(2)}) %collective-permute-start.17) | collective-permute-done | bytes 262176 | tf_op jit(solution)/shard_map/ppermute | solution.py:324
  77.4 21.5 %all_to_all.15.mixed_ref = bf16[128,8,128]{2,1,0:T(8,128)(2,1)S(1)} all-to-all(bf16[128,8,128]{2,1,0:T(8,128)(2,1)S(1)} %add_convert_fusion), channel_id=1, replica_groups=mesh['yh'=2,'yl'=2,'xl'=2,'z'=8,'core'=2,'xh'=2] {'yh','yl','xl','z','xh'}, dimensions={0} | all-to-all | bytes 524288 | tf_op jit(solution)/shard_map/all_to_all | solution.py:320
  99.0 1.6 %shard_map.89 = bf16[1024,128]{1,0:T(8,128)(2,1)} custom-call(bf16[128,8,128]{2,1,0:T(8,128)(2,1)S(1)} %all_to_all.15.mixed_ref, f32[1024,128]{1,0:T(8,128)S(1)} %get-tuple-element.65.gate_ref, f32[1024,128]{1,0:T(8,128)S(1)} %get-tuple-element.66.base_ref, bf16[128,128]{1,0:T(8,128)(2,1)S(1)} %copy-done.4), custom_call_target="tpu_custom_call" | custom-call | flops 2000000000 | bytes 6000000 | tf_op jit(solution)/shard_map/pallas_call | solution.py:310
  (44 shorter events, 8.9 us)
Async XLA Ops:
  2.2 5.5 %collective-permute-start = (bf16[128,128]{1,0:T(8,128)(2,1)S(1)}, bf16[128,128]{1,0:T(8,128)(2,1)S(1)}, u32[]{:S(2)}, u32[]{:S(2)}) collective-permute-start(bf16[128,128]{1,0:T(8,128)(2,1)S(1)} %get-tuple-element.37.own_ref), channel_id=1, source_target_pairs={{0,128},{128,0},{1,129},{129,1},{2,130},{130,2},{3,131},{131,3},{4... | collective-permute-start | bytes 98312 | tf_op jit(solution)/shard_map/ppermute | solution.py:324
  9.0 11.7 %copy-start.2 = (bf16[512,128]{1,0:T(8,128)(2,1)S(1)}, bf16[512,128]{1,0:T(8,128)(2,1)}, u32[]{:S(2)}) copy-start(bf16[512,128]{1,0:T(8,128)(2,1)} %own_ref) | copy-start | bytes 393220
  9.0 13.9 %copy-start.1 = (bf16[4,256,128]{2,1,0:T(8,128)(2,1)S(1)}, bf16[4,256,128]{2,1,0:T(8,128)(2,1)}, u32[]{:S(2)}) copy-start(bf16[4,256,128]{2,1,0:T(8,128)(2,1)} %couple_ref.1) | copy-start | bytes 786436
  9.0 25.9 %all-to-all-start = ((bf16[8,128,128]{2,1,0:T(8,128)(2,1)}), bf16[8,128,128]{2,1,0:T(8,128)(2,1)S(1)}, u32[]{:S(2)}, u32[]{:S(2)}) async-start(bf16[8,128,128]{2,1,0:T(8,128)(2,1)} %shard_map.83), calls=%async_computation | async-start | bytes 524288 | tf_op jit(solution)/shard_map/all_to_all | solution.py:320
  17.6 5.2 %collective-permute-start.1 = (bf16[16,256]{1,0:T(8,128)(2,1)S(1)}, bf16[16,256]{1,0:T(8,128)(2,1)S(1)}, u32[]{:S(2)}, u32[]{:S(2)}) collective-permute-start(bf16[16,256]{1,0:T(8,128)(2,1)S(1)} %bitcast.10), channel_id=1, source_target_pairs={{0,1},{1,0},{2,3},{3,2},{4,5},{5,4},{6,7},{7,6},{8,9},{9,8},{10,11... | collective-permute-start | bytes 24584 | tf_op jit(solution)/shard_map/ppermute | solution.py:324
  20.7 9.5 %collective-permute-start.9 = (bf16[512,128]{1,0:T(8,128)(2,1)S(1)}, bf16[512,128]{1,0:T(8,128)(2,1)S(1)}, u32[]{:S(2)}, u32[]{:S(2)}) collective-permute-start(bf16[512,128]{1,0:T(8,128)(2,1)S(1)} %copy-done.2), channel_id=1, source_target_pairs={{0,1},{1,0},{2,3},{3,2},{4,5},{5,4},{6,7},{7,6},{8,9},{9,8},{10,11... | collective-permute-start | bytes 393224 | tf_op jit(solution)/shard_map/ppermute | solution.py:324
  23.8 2.7 %collective-permute-start.2 = (bf16[256,128]{1,0:T(8,128)(2,1)S(1)}, bf16[256,128]{1,0:T(8,128)(2,1)S(1)}, u32[]{:S(2)}, u32[]{:S(2)}) collective-permute-start(bf16[256,128]{1,0:T(8,128)(2,1)S(1)} %get-tuple-element.43), channel_id=1, source_target_pairs={{0,2},{2,0},{32,34},{34,32},{64,66},{66,64},{96,98},{98,96},{1,3},... | collective-permute-start | bytes 196616 | tf_op jit(solution)/shard_map/ppermute | solution.py:328
  23.9 4.5 %collective-permute-start.3 = (bf16[256,128]{1,0:T(8,128)(2,1)S(1)}, bf16[256,128]{1,0:T(8,128)(2,1)S(1)}, u32[]{:S(2)}, u32[]{:S(2)}) collective-permute-start(bf16[256,128]{1,0:T(8,128)(2,1)S(1)} %get-tuple-element.44), channel_id=1, source_target_pairs={{0,32},{2,34},{32,0},{34,2},{64,96},{66,98},{96,64},{98,66},{1,33}... | collective-permute-start | bytes 196616 | tf_op jit(solution)/shard_map/ppermute | solution.py:328
  25.6 5.6 %collective-permute-start.4 = (bf16[256,128]{1,0:T(8,128)(2,1)S(1)}, bf16[256,128]{1,0:T(8,128)(2,1)S(1)}, u32[]{:S(2)}, u32[]{:S(2)}) collective-permute-start(bf16[256,128]{1,0:T(8,128)(2,1)S(1)} %get-tuple-element.45), channel_id=1, source_target_pairs={{0,34},{2,32},{32,2},{34,0},{64,98},{66,96},{96,66},{98,64},{1,35}... | collective-permute-start | bytes 196616 | tf_op jit(solution)/shard_map/ppermute | solution.py:328
  25.9 5.3 %collective-permute-start.5 = (bf16[256,128]{1,0:T(8,128)(2,1)S(1)}, bf16[256,128]{1,0:T(8,128)(2,1)S(1)}, u32[]{:S(2)}, u32[]{:S(2)}) collective-permute-start(bf16[256,128]{1,0:T(8,128)(2,1)S(1)} %get-tuple-element.46), channel_id=1, source_target_pairs={{0,64},{2,66},{32,96},{34,98},{64,0},{66,2},{96,32},{98,34},{1,65}... | collective-permute-start | bytes 196616 | tf_op jit(solution)/shard_map/ppermute | solution.py:328
  26.4 4.8 %collective-permute-start.6 = (bf16[256,128]{1,0:T(8,128)(2,1)S(1)}, bf16[256,128]{1,0:T(8,128)(2,1)S(1)}, u32[]{:S(2)}, u32[]{:S(2)}) collective-permute-start(bf16[256,128]{1,0:T(8,128)(2,1)S(1)} %get-tuple-element.47), channel_id=1, source_target_pairs={{0,66},{2,64},{32,98},{34,96},{64,2},{66,0},{96,34},{98,32},{1,67}... | collective-permute-start | bytes 196616 | tf_op jit(solution)/shard_map/ppermute | solution.py:328
  28.4 5.2 %collective-permute-start.7 = (bf16[256,128]{1,0:T(8,128)(2,1)S(1)}, bf16[256,128]{1,0:T(8,128)(2,1)S(1)}, u32[]{:S(2)}, u32[]{:S(2)}) collective-permute-start(bf16[256,128]{1,0:T(8,128)(2,1)S(1)} %get-tuple-element.48), channel_id=1, source_target_pairs={{0,96},{2,98},{32,64},{34,66},{64,32},{66,34},{96,0},{98,2},{1,97}... | collective-permute-start | bytes 196616 | tf_op jit(solution)/shard_map/ppermute | solution.py:328
  30.3 4.7 %collective-permute-start.8 = (bf16[256,128]{1,0:T(8,128)(2,1)S(1)}, bf16[256,128]{1,0:T(8,128)(2,1)S(1)}, u32[]{:S(2)}, u32[]{:S(2)}) collective-permute-start(bf16[256,128]{1,0:T(8,128)(2,1)S(1)} %get-tuple-element.49), channel_id=1, source_target_pairs={{0,98},{2,96},{32,66},{34,64},{64,34},{66,32},{96,2},{98,0},{1,99}... | collective-permute-start | bytes 196616 | tf_op jit(solution)/shard_map/ppermute | solution.py:328
  40.6 24.4 %copy-start.3 = (bf16[128,128]{1,0:T(8,128)(2,1)S(1)}, bf16[128,128]{1,0:T(8,128)(2,1)}, u32[]{:S(2)}) copy-start(bf16[128,128]{1,0:T(8,128)(2,1)} %rest_8_.1) | copy-start | bytes 98308
  40.6 33.4 %all-to-all-start.1 = ((bf16[128,16,128]{2,1,0:T(8,128)(2,1)}), bf16[128,16,128]{2,1,0:T(8,128)(2,1)S(1)}, u32[]{:S(2)}, u32[]{:S(2)}) async-start(bf16[128,16,128]{2,1,0:T(8,128)(2,1)} %get-tuple-element.62), calls=%async_computation.1 | async-start | bytes 1048576 | tf_op jit(solution)/shard_map/all_to_all | solution.py:320
  55.2 3.7 %collective-permute-start.10 = (bf16[128,128]{1,0:T(8,128)(2,1)S(1)}, bf16[128,128]{1,0:T(8,128)(2,1)S(1)}, u32[]{:S(2)}, u32[]{:S(2)}) collective-permute-start(bf16[128,128]{1,0:T(8,128)(2,1)S(1)} %get-tuple-element.52), channel_id=1, source_target_pairs={{0,2},{2,0},{32,34},{34,32},{64,66},{66,64},{96,98},{98,96},{1,3},... | collective-permute-start | bytes 98312 | tf_op jit(solution)/shard_map/ppermute | solution.py:328
  55.3 5.0 %collective-permute-start.11 = (bf16[128,128]{1,0:T(8,128)(2,1)S(1)}, bf16[128,128]{1,0:T(8,128)(2,1)S(1)}, u32[]{:S(2)}, u32[]{:S(2)}) collective-permute-start(bf16[128,128]{1,0:T(8,128)(2,1)S(1)} %get-tuple-element.53), channel_id=1, source_target_pairs={{0,32},{2,34},{32,0},{34,2},{64,96},{66,98},{96,64},{98,66},{1,33}... | collective-permute-start | bytes 98312 | tf_op jit(solution)/shard_map/ppermute | solution.py:328
  57.0 4.6 %collective-permute-start.12 = (bf16[128,128]{1,0:T(8,128)(2,1)S(1)}, bf16[128,128]{1,0:T(8,128)(2,1)S(1)}, u32[]{:S(2)}, u32[]{:S(2)}) collective-permute-start(bf16[128,128]{1,0:T(8,128)(2,1)S(1)} %get-tuple-element.54), channel_id=1, source_target_pairs={{0,34},{2,32},{32,2},{34,0},{64,98},{66,96},{96,66},{98,64},{1,35}... | collective-permute-start | bytes 98312 | tf_op jit(solution)/shard_map/ppermute | solution.py:328
  57.2 4.7 %collective-permute-start.13 = (bf16[128,128]{1,0:T(8,128)(2,1)S(1)}, bf16[128,128]{1,0:T(8,128)(2,1)S(1)}, u32[]{:S(2)}, u32[]{:S(2)}) collective-permute-start(bf16[128,128]{1,0:T(8,128)(2,1)S(1)} %get-tuple-element.55), channel_id=1, source_target_pairs={{0,64},{2,66},{32,96},{34,98},{64,0},{66,2},{96,32},{98,34},{1,65}... | collective-permute-start | bytes 98312 | tf_op jit(solution)/shard_map/ppermute | solution.py:328
  58.0 4.2 %collective-permute-start.14 = (bf16[128,128]{1,0:T(8,128)(2,1)S(1)}, bf16[128,128]{1,0:T(8,128)(2,1)S(1)}, u32[]{:S(2)}, u32[]{:S(2)}) collective-permute-start(bf16[128,128]{1,0:T(8,128)(2,1)S(1)} %get-tuple-element.56), channel_id=1, source_target_pairs={{0,66},{2,64},{32,98},{34,96},{64,2},{66,0},{96,34},{98,32},{1,67}... | collective-permute-start | bytes 98312 | tf_op jit(solution)/shard_map/ppermute | solution.py:328
  58.9 5.4 %collective-permute-start.15 = (bf16[128,128]{1,0:T(8,128)(2,1)S(1)}, bf16[128,128]{1,0:T(8,128)(2,1)S(1)}, u32[]{:S(2)}, u32[]{:S(2)}) collective-permute-start(bf16[128,128]{1,0:T(8,128)(2,1)S(1)} %get-tuple-element.57), channel_id=1, source_target_pairs={{0,96},{2,98},{32,64},{34,66},{64,32},{66,34},{96,0},{98,2},{1,97}... | collective-permute-start | bytes 98312 | tf_op jit(solution)/shard_map/ppermute | solution.py:328
  60.3 4.7 %collective-permute-start.16 = (bf16[128,128]{1,0:T(8,128)(2,1)S(1)}, bf16[128,128]{1,0:T(8,128)(2,1)S(1)}, u32[]{:S(2)}, u32[]{:S(2)}) collective-permute-start(bf16[128,128]{1,0:T(8,128)(2,1)S(1)} %get-tuple-element.58), channel_id=1, source_target_pairs={{0,98},{2,96},{32,66},{34,64},{64,34},{66,32},{96,2},{98,0},{1,99}... | collective-permute-start | bytes 98312 | tf_op jit(solution)/shard_map/ppermute | solution.py:328
  75.7 1.6 %collective-permute-start.17 = (bf16[128,8,128]{2,1,0:T(8,128)(2,1)S(1)}, bf16[128,8,128]{2,1,0:T(8,128)(2,1)S(1)}, u32[]{:S(2)}, u32[]{:S(2)}) collective-permute-start(bf16[128,8,128]{2,1,0:T(8,128)(2,1)S(1)} %get-tuple-element.64), channel_id=1, source_target_pairs={{0,2},{2,0},{1,3},{3,1},{4,6},{6,4},{5,7},{7,5},{8,10},{10,8},{9,1... | collective-permute-start | bytes 786440 | tf_op jit(solution)/shard_map/ppermute | solution.py:324
  77.4 21.6 %copy-start.4 = (bf16[128,128]{1,0:T(8,128)(2,1)S(1)}, bf16[128,128]{1,0:T(8,128)(2,1)}, u32[]{:S(2)}) copy-start(bf16[128,128]{1,0:T(8,128)(2,1)} %w_ref.1) | copy-start | bytes 98308
  (4 other events, 18.1 us)

commit v4 on v3

--- a/solution.py
+++ b/solution.py
@@ -46,34 +46,18 @@
     for i in range(4):
         normed = standardized(msa_ref[:, i, :].astype(F32), -1).astype(BF16)
         norm_ref[i] = normed
-        right_ref[i * 32 : (i + 1) * 32, :] = dot(second_ref[...], normed, ((1,), (1,))).astype(BF16)
+        right = dot(second_ref[...], normed, ((1,), (1,))).astype(BF16)
+        for z in range(8):
+            right_ref[z, i * 32 : (i + 1) * 32, :] = right
 
 
 def firsts(msa, second_t):
     return on_core(
         first_kernel,
-        (jax.ShapeDtypeStruct((128, 128), BF16), jax.ShapeDtypeStruct((4, 128, 256), BF16)),
+        (jax.ShapeDtypeStruct((8, 128, 128), BF16), jax.ShapeDtypeStruct((4, 128, 256), BF16)),
         2,
         cost=cost(1),
     )(msa, second_t)
-
-
-def spread_kernel(me_ref, own_ref, other_ref, all_ref):
-    @pl.when(me_ref[3] == 1)
-    def _():
-        for z in range(8):
-            all_ref[z] = own_ref[...]
-
-    @pl.when(me_ref[3] == 0)
-    def _():
-        for z in range(8):
-            all_ref[z] = other_ref[...]
-
-
-def spreads(me, own, other):
-    return on_core(
-        spread_kernel, jax.ShapeDtypeStruct((8, 128, 128), BF16), 3, scalars=1, cost=cost(1)
-    )(me, own, other)
 
 
 def pack_kernel(me_ref, norm_ref, own_ref, other_ref, couple_ref, *packed_refs):
@@ -125,14 +109,18 @@
     )(me, own, other)
 
 
-def pair_kernel(me_ref, right_ref, *rest):
+def pair_kernel(me_ref, own_ref, other_ref, *rest):
     packed_refs, by_e_ref, entry_ref = rest[:8], rest[8], rest[9]
     lifted_refs, cols_ref = rest[10:18], rest[18]
     rows_scr, lhs_scr, cols_scr, wide_scr = rest[19:]
     me = me_ref[0]
+    keep = me_ref[3] == 1
     for z in range(8):
         for j in range(4):
-            rows_scr[pl.ds(z * 4 + j, 32, stride=32), :] = right_ref[z, j * 32 : (j + 1) * 32, :].astype(F32)
+            rows = slice(j * 32, (j + 1) * 32)
+            rows_scr[pl.ds(z * 4 + j, 32, stride=32), :] = jnp.where(
+                keep, own_ref[z, rows, :].astype(F32), other_ref[z, rows, :].astype(F32)
+            )
     lefts = jnp.concatenate([packed_refs[m][128:256, :] for m in range(8)], axis=0)
     blank = jnp.zeros((16, 128), BF16)
     for part in range(4):
@@ -174,11 +162,11 @@
         )
 
 
-def pairs(me, right, packed, by_e, entry_t):
+def pairs(me, right, other, packed, by_e, entry_t):
     out = on_core(
         pair_kernel,
         (jax.ShapeDtypeStruct((128, 128), BF16),) * 8 + (jax.ShapeDtypeStruct((128, 16, 128), BF16),),
-        12,
+        13,
         [
             pltpu.VMEM((1024, 128), F32),
             pltpu.VMEM((256, 4096), BF16),
@@ -188,7 +176,7 @@
         scalars=1,
         limit=20,
         cost=cost(5),
-    )(me, right, *packed, by_e, entry_t)
+    )(me, right, other, *packed, by_e, entry_t)
     return out[:8], out[8]
 
 
@@ -335,15 +323,16 @@
         [at["yl"] * 4 + at["xl"] * 2 + at["core"], at["xh"], at["core"], (at["yh"] == at["xh"]).astype(jnp.int32)]
     ).astype(jnp.int32)
     right, normed = firsts(msa, second.T)
-    first_t, w_out, right = lax.optimization_barrier((first.T, w_out, right))
-    right = spreads(me, right, partner(right, "yh"))
+    first_t, w_out, right, normed = lax.optimization_barrier((first.T, w_out, right, normed))
+    right = exchanged(right, "z")
     first_other = partner(first_t, "xh")
     w_other = partner(w_out, "xh")
-    right, normed = lax.optimization_barrier((right, normed))
-    right = exchanged(right, "z")
-    packed = to_peers(packs(me, normed, first_t, first_other, couple))
+    packed = packs(me, normed, first_t, first_other, couple)
+    right, packed = lax.optimization_barrier((right, packed))
+    other = partner(right, "yh")
+    packed = to_peers(packed)
     by_e = weights(me, w_out, w_other)
-    lifted, cols = pairs(me, right, packed, by_e, jnp.swapaxes(entry, 1, 2))
+    lifted, cols = pairs(me, right, other, packed, by_e, jnp.swapaxes(entry, 1, 2))
     cols = exchanged(cols, CHIP)
     gate, base = gates(me, to_peers(lifted), w_gate)
     me, gate, base = lax.optimization_barrier((me, gate, base))

time: 101 us -> 101 us (level)
  waiting for transfers between devices: 21.9 us -> 26 us
  starting transfers between devices: 41.4 us -> 37.6 us
    all_to_all x2, starting transfers between devices: 23.2 us -> 16.4 us  [exchanged(): return lax.all_to_all(x, axes, split_axis=0, concat_axis=0, tiled=True)]
    all_to_all x2, waiting for transfers between devices: 7.96 us -> 13.6 us  [exchanged(): return lax.all_to_all(x, axes, split_axis=0, concat_axis=0, tiled=True)]
    ppermute x4, starting transfers between devices: 6.09 us -> 8.52 us  [partner(): return lax.ppermute(x, axis, [(0, 1), (1, 0)])]
  transfers between devices with their start and end apart: 20 -> 20, of which waited for: 11 -> 12; matrix products, arithmetic and copies ran while one was open for 0% -> 0% of each run, Pallas kernels for 3% -> 3%
where the time goes in v4:
time: 101 us; the launch traced here: 100 us
  starting transfers between devices  37.6 us (37%)
  waiting for transfers between devices  26 us (26%)
  blocking collectives  21.5 us (21%)
  Pallas kernels  13 us (13%)
  local copies, waits for them, and re-layouts  1.82 us (2%)
    all_to_all x1, blocking collectives, exchanged(): return lax.all_to_all(x, axes, split_axis=0, concat_axis=0, tiled=True)  21.5 us
    all_to_all x2, starting transfers between devices, exchanged(): return lax.all_to_all(x, axes, split_axis=0, concat_axis=0, tiled=True)  16.4 us
    all_to_all x2, waiting for transfers between devices, exchanged(): return lax.all_to_all(x, axes, split_axis=0, concat_axis=0, tiled=True)  13.6 us
    ppermute x14, starting transfers between devices, to_peers(): lax.ppermute(pieces[m], PLANE, [(i, i ^ m) for i in range(8)])  12.7 us
    ppermute x4, starting transfers between devices, partner(): return lax.ppermute(x, axis, [(0, 1), (1, 0)])  8.52 us
    ppermute x14, waiting for transfers between devices, to_peers(): lax.ppermute(pieces[m], PLANE, [(i, i ^ m) for i in range(8)])  7.04 us
    pallas_call x1, Pallas kernels, pairs(): on_core(pair_kernel, (jax.ShapeDtypeStruct((128, 128), BF16),) * 8 + (jax...  5.67 us
    ppermute x4, waiting for transfers between devices, partner(): return lax.ppermute(x, axis, [(0, 1), (1, 0)])  5.33 us
  transfers between devices with their start and end apart: 20, of which 12 were waited for; matrix products, arithmetic and copies ran while one was open for 0% of the time, Pallas kernels for 3%

profile of v4, /device:TPU:8, one launch (start us, length us, event | category | flops | bytes accessed | tf_op | source)
XLA Modules:
  0.0 100.3 jit_solution(15856016560319571853)
XLA Ops:
  1.7 1.2 %shard_map.82 = (bf16[8,128,128]{2,1,0:T(8,128)(2,1)}, bf16[4,128,256]{2,1,0:T(8,128)(2,1)S(1)}) custom-call(bf16[128,4,256]{2,1,0:T(4,128)(2,1)S(1)} %copy-done, bf16[32,256]{1,0:T(8,128)(2,1)S(1)} %bitcast.9), custom_call_target="tpu_custom_call" | custom-call | flops 1000000000 | bytes 3000000 | tf_op jit(solution)/shard_map/pallas_call | solution.py:55
  2.9 8.6 %all-to-all-start = ((bf16[8,128,128]{2,1,0:T(8,128)(2,1)}), bf16[8,128,128]{2,1,0:T(8,128)(2,1)S(1)}, u32[]{:S(2)}, u32[]{:S(2)}) async-start(bf16[8,128,128]{2,1,0:T(8,128)(2,1)} %get-tuple-element.46), calls=%async_computation | async-start | bytes 524288 | tf_op jit(solution)/shard_map/all_to_all | solution.py:308
  11.5 3.1 %collective-permute-start = (bf16[16,256]{1,0:T(8,128)(2,1)S(1)}, bf16[16,256]{1,0:T(8,128)(2,1)S(1)}, u32[]{:S(2)}, u32[]{:S(2)}) collective-permute-start(bf16[16,256]{1,0:T(8,128)(2,1)S(1)} %bitcast.10), channel_id=1, source_target_pairs={{0,1},{1,0},{2,3},{3,2},{4,5},{5,4},{6,7},{7,6},{8,9},{9,8},{10,11... | collective-permute-start | bytes 24584 | tf_op jit(solution)/shard_map/ppermute | solution.py:312
  14.7 2.0 %collective-permute-done.other_ref = bf16[16,256]{1,0:T(8,128)(2,1)S(1)} collective-permute-done((bf16[16,256]{1,0:T(8,128)(2,1)S(1)}, bf16[16,256]{1,0:T(8,128)(2,1)S(1)}, u32[]{:S(2)}, u32[]{:S(2)}) %collective-permute-start) | collective-permute-done | bytes 8224 | tf_op jit(solution)/shard_map/ppermute | solution.py:312
  17.6 5.7 %all-to-all-done.own_ref = bf16[8,128,128]{2,1,0:T(8,128)(2,1)S(1)} async-done(((bf16[8,128,128]{2,1,0:T(8,128)(2,1)}), bf16[8,128,128]{2,1,0:T(8,128)(2,1)S(1)}, u32[]{:S(2)}, u32[]{:S(2)}) %all-to-all-start) | async-done | bytes 262176 | tf_op jit(solution)/shard_map/all_to_all | solution.py:308
  23.4 2.3 %collective-permute-start.1 = (bf16[8,128,128]{2,1,0:T(8,128)(2,1)S(1)}, bf16[8,128,128]{2,1,0:T(8,128)(2,1)S(1)}, u32[]{:S(2)}, u32[]{:S(2)}) collective-permute-start(bf16[8,128,128]{2,1,0:T(8,128)(2,1)S(1)} %all-to-all-done.own_ref), channel_id=1, source_target_pairs={{0,128},{128,0},{1,129},{129,1},{2,130},{130,2},{3,131},{131,3},{4... | collective-permute-start | bytes 786440 | tf_op jit(solution)/shard_map/ppermute | solution.py:312
  25.7 3.0 %collective-permute-start.9 = (bf16[512,128]{1,0:T(8,128)(2,1)S(1)}, bf16[512,128]{1,0:T(8,128)(2,1)S(1)}, u32[]{:S(2)}, u32[]{:S(2)}) collective-permute-start(bf16[512,128]{1,0:T(8,128)(2,1)S(1)} %copy-done.2), channel_id=1, source_target_pairs={{0,1},{1,0},{2,3},{3,2},{4,5},{5,4},{6,7},{7,6},{8,9},{9,8},{10,11... | collective-permute-start | bytes 393224 | tf_op jit(solution)/shard_map/ppermute | solution.py:312
  29.3 1.3 %collective-permute-start.4 = (bf16[256,128]{1,0:T(8,128)(2,1)S(1)}, bf16[256,128]{1,0:T(8,128)(2,1)S(1)}, u32[]{:S(2)}, u32[]{:S(2)}) collective-permute-start(bf16[256,128]{1,0:T(8,128)(2,1)S(1)} %get-tuple-element.61), channel_id=1, source_target_pairs={{0,34},{2,32},{32,2},{34,0},{64,98},{66,96},{96,66},{98,64},{1,35}... | collective-permute-start | bytes 196616 | tf_op jit(solution)/shard_map/ppermute | solution.py:316
  30.7 1.8 %collective-permute-done.9.other_ref = bf16[512,128]{1,0:T(8,128)(2,1)S(1)} collective-permute-done((bf16[512,128]{1,0:T(8,128)(2,1)S(1)}, bf16[512,128]{1,0:T(8,128)(2,1)S(1)}, u32[]{:S(2)}, u32[]{:S(2)}) %collective-permute-start.9) | collective-permute-done | bytes 131104 | tf_op jit(solution)/shard_map/ppermute | solution.py:312
  32.5 1.3 %collective-permute-start.5 = (bf16[256,128]{1,0:T(8,128)(2,1)S(1)}, bf16[256,128]{1,0:T(8,128)(2,1)S(1)}, u32[]{:S(2)}, u32[]{:S(2)}) collective-permute-start(bf16[256,128]{1,0:T(8,128)(2,1)S(1)} %get-tuple-element.62), channel_id=1, source_target_pairs={{0,64},{2,66},{32,96},{34,98},{64,0},{66,2},{96,32},{98,34},{1,65}... | collective-permute-start | bytes 196616 | tf_op jit(solution)/shard_map/ppermute | solution.py:316
  34.1 2.5 %collective-permute-start.7 = (bf16[256,128]{1,0:T(8,128)(2,1)S(1)}, bf16[256,128]{1,0:T(8,128)(2,1)S(1)}, u32[]{:S(2)}, u32[]{:S(2)}) collective-permute-start(bf16[256,128]{1,0:T(8,128)(2,1)S(1)} %get-tuple-element.64), channel_id=1, source_target_pairs={{0,96},{2,98},{32,64},{34,66},{64,32},{66,34},{96,0},{98,2},{1,97}... | collective-permute-start | bytes 196616 | tf_op jit(solution)/shard_map/ppermute | solution.py:316
  38.1 1.6 %collective-permute-done.7.rest_6_ = bf16[256,128]{1,0:T(8,128)(2,1)S(1)} collective-permute-done((bf16[256,128]{1,0:T(8,128)(2,1)S(1)}, bf16[256,128]{1,0:T(8,128)(2,1)S(1)}, u32[]{:S(2)}, u32[]{:S(2)}) %collective-permute-start.7) | collective-permute-done | bytes 65568 | tf_op jit(solution)/shard_map/ppermute | solution.py:316
  39.8 1.4 %collective-permute-done.8.rest_7_ = bf16[256,128]{1,0:T(8,128)(2,1)S(1)} collective-permute-done((bf16[256,128]{1,0:T(8,128)(2,1)S(1)}, bf16[256,128]{1,0:T(8,128)(2,1)S(1)}, u32[]{:S(2)}, u32[]{:S(2)}) %collective-permute-start.8) | collective-permute-done | bytes 65568 | tf_op jit(solution)/shard_map/ppermute | solution.py:316
  41.2 5.7 %shard_map.85 = (bf16[128,128]{1,0:T(8,128)(2,1)S(1)}, bf16[128,128]{1,0:T(8,128)(2,1)S(1)}, bf16[128,128]{1,0:T(8,128)(2,1)S(1)}, bf16[128,128]{1,0:T(8,128)(2,...) custom-call(s32[4]{0:T(128)S(1)} %pad_add_fusion.me_ref, ...), custom_call_target="tpu_custom_call" | custom-call | flops 5000000000 | bytes 15000000 | tf_op jit(solution)/shard_map/pallas_call | solution.py:166
  46.8 7.8 %all-to-all-start.1 = ((bf16[128,16,128]{2,1,0:T(8,128)(2,1)}), bf16[128,16,128]{2,1,0:T(8,128)(2,1)S(1)}, u32[]{:S(2)}, u32[]{:S(2)}) async-start(bf16[128,16,128]{2,1,0:T(8,128)(2,1)} %get-tuple-element.78), calls=%async_computation.1 | async-start | bytes 1048576 | tf_op jit(solution)/shard_map/all_to_all | solution.py:308
  54.8 1.7 %collective-permute-start.11 = (bf16[128,128]{1,0:T(8,128)(2,1)S(1)}, bf16[128,128]{1,0:T(8,128)(2,1)S(1)}, u32[]{:S(2)}, u32[]{:S(2)}) collective-permute-start(bf16[128,128]{1,0:T(8,128)(2,1)S(1)} %get-tuple-element.69), channel_id=1, source_target_pairs={{0,32},{2,34},{32,0},{34,2},{64,96},{66,98},{96,64},{98,66},{1,33}... | collective-permute-start | bytes 98312 | tf_op jit(solution)/shard_map/ppermute | solution.py:316
  58.3 1.4 %collective-permute-start.15 = (bf16[128,128]{1,0:T(8,128)(2,1)S(1)}, bf16[128,128]{1,0:T(8,128)(2,1)S(1)}, u32[]{:S(2)}, u32[]{:S(2)}) collective-permute-start(bf16[128,128]{1,0:T(8,128)(2,1)S(1)} %get-tuple-element.73), channel_id=1, source_target_pairs={{0,96},{2,98},{32,64},{34,66},{64,32},{66,34},{96,0},{98,2},{1,97}... | collective-permute-start | bytes 98312 | tf_op jit(solution)/shard_map/ppermute | solution.py:316
  59.7 1.3 %collective-permute-start.16 = (bf16[128,128]{1,0:T(8,128)(2,1)S(1)}, bf16[128,128]{1,0:T(8,128)(2,1)S(1)}, u32[]{:S(2)}, u32[]{:S(2)}) collective-permute-start(bf16[128,128]{1,0:T(8,128)(2,1)S(1)} %get-tuple-element.74), channel_id=1, source_target_pairs={{0,98},{2,96},{32,66},{34,64},{64,34},{66,32},{96,2},{98,0},{1,99}... | collective-permute-start | bytes 98312 | tf_op jit(solution)/shard_map/ppermute | solution.py:316
  61.7 2.2 %collective-permute-done.15.rest_6_ = bf16[128,128]{1,0:T(8,128)(2,1)S(1)} collective-permute-done((bf16[128,128]{1,0:T(8,128)(2,1)S(1)}, bf16[128,128]{1,0:T(8,128)(2,1)S(1)}, u32[]{:S(2)}, u32[]{:S(2)}) %collective-permute-start.15) | collective-permute-done | bytes 32800 | tf_op jit(solution)/shard_map/ppermute | solution.py:316
  65.8 7.9 %all-to-all-done.1.cols_ref = bf16[128,16,128]{2,1,0:T(8,128)(2,1)S(1)} async-done(((bf16[128,16,128]{2,1,0:T(8,128)(2,1)}), bf16[128,16,128]{2,1,0:T(8,128)(2,1)S(1)}, u32[]{:S(2)}, u32[]{:S(2)}) %all-to-all-start.1) | async-done | bytes 524320 | tf_op jit(solution)/shard_map/all_to_all | solution.py:308
  73.7 1.8 %shard_map.87 = (f32[128,8,128]{2,1,0:T(8,128)S(1)}, bf16[128,8,128]{2,1,0:T(8,128)(2,1)S(1)}) custom-call(s32[4]{0:T(128)S(1)} %pad_add_fusion.me_ref, bf16[128,16,128]{2,1,0:T(8,128)(2,1)S(1)} %all-to-all-done.1.cols_ref), custom_call_target="tpu_custom_call" | custom-call | flops 3000000000 | bytes 9000000 | tf_op jit(solution)/shard_map/pallas_call | solution.py:234
  75.6 1.5 %collective-permute-done.17 = bf16[128,8,128]{2,1,0:T(8,128)(2,1)S(1)} collective-permute-done((bf16[128,8,128]{2,1,0:T(8,128)(2,1)S(1)}, bf16[128,8,128]{2,1,0:T(8,128)(2,1)S(1)}, u32[]{:S(2)}, u32[]{:S(2)}) %collective-permute-start.17) | collective-permute-done | bytes 262176 | tf_op jit(solution)/shard_map/ppermute | solution.py:312
  77.2 21.5 %all_to_all.15.mixed_ref = bf16[128,8,128]{2,1,0:T(8,128)(2,1)S(1)} all-to-all(bf16[128,8,128]{2,1,0:T(8,128)(2,1)S(1)} %add_convert_fusion), channel_id=1, replica_groups=mesh['yh'=2,'yl'=2,'xl'=2,'z'=8,'core'=2,'xh'=2] {'yh','yl','xl','z','xh'}, dimensions={0} | all-to-all | bytes 524288 | tf_op jit(solution)/shard_map/all_to_all | solution.py:308
  98.7 1.6 %shard_map.88 = bf16[1024,128]{1,0:T(8,128)(2,1)} custom-call(bf16[128,8,128]{2,1,0:T(8,128)(2,1)S(1)} %all_to_all.15.mixed_ref, f32[1024,128]{1,0:T(8,128)S(1)} %get-tuple-element.81.gate_ref, f32[1024,128]{1,0:T(8,128)S(1)} %get-tuple-element.82.base_ref, bf16[128,128]{1,0:T(8,128)(2,1)S(1)} %copy-done.4), custom_call_target="tpu_custom_call" | custom-call | flops 2000000000 | bytes 6000000 | tf_op jit(solution)/shard_map/pallas_call | solution.py:298
  (43 shorter events, 10.0 us)
Async XLA Ops:
  2.9 13.8 %copy-start.1 = (bf16[4,256,128]{2,1,0:T(8,128)(2,1)S(1)}, bf16[4,256,128]{2,1,0:T(8,128)(2,1)}, u32[]{:S(2)}) copy-start(bf16[4,256,128]{2,1,0:T(8,128)(2,1)} %couple_ref.1) | copy-start | bytes 786436
  2.9 20.5 %all-to-all-start = ((bf16[8,128,128]{2,1,0:T(8,128)(2,1)}), bf16[8,128,128]{2,1,0:T(8,128)(2,1)S(1)}, u32[]{:S(2)}, u32[]{:S(2)}) async-start(bf16[8,128,128]{2,1,0:T(8,128)(2,1)} %get-tuple-element.46), calls=%async_computation | async-start | bytes 524288 | tf_op jit(solution)/shard_map/all_to_all | solution.py:308
  11.5 5.2 %collective-permute-start = (bf16[16,256]{1,0:T(8,128)(2,1)S(1)}, bf16[16,256]{1,0:T(8,128)(2,1)S(1)}, u32[]{:S(2)}, u32[]{:S(2)}) collective-permute-start(bf16[16,256]{1,0:T(8,128)(2,1)S(1)} %bitcast.10), channel_id=1, source_target_pairs={{0,1},{1,0},{2,3},{3,2},{4,5},{5,4},{6,7},{7,6},{8,9},{9,8},{10,11... | collective-permute-start | bytes 24584 | tf_op jit(solution)/shard_map/ppermute | solution.py:312
  14.7 15.9 %copy-start.7 = (bf16[4,128,128]{2,1,0:T(8,128)(2,1)S(1)}, bf16[4,128,128]{2,1,0:T(8,128)(2,1)}, u32[]{:S(2)}) copy-start(bf16[4,128,128]{2,1,0:T(8,128)(2,1)} %param.13) | copy-start | bytes 393220
  23.4 17.8 %collective-permute-start.1 = (bf16[8,128,128]{2,1,0:T(8,128)(2,1)S(1)}, bf16[8,128,128]{2,1,0:T(8,128)(2,1)S(1)}, u32[]{:S(2)}, u32[]{:S(2)}) collective-permute-start(bf16[8,128,128]{2,1,0:T(8,128)(2,1)S(1)} %all-to-all-done.own_ref), channel_id=1, source_target_pairs={{0,128},{128,0},{1,129},{129,1},{2,130},{130,2},{3,131},{131,3},{4... | collective-permute-start | bytes 786440 | tf_op jit(solution)/shard_map/ppermute | solution.py:312
  25.7 6.8 %collective-permute-start.9 = (bf16[512,128]{1,0:T(8,128)(2,1)S(1)}, bf16[512,128]{1,0:T(8,128)(2,1)S(1)}, u32[]{:S(2)}, u32[]{:S(2)}) collective-permute-start(bf16[512,128]{1,0:T(8,128)(2,1)S(1)} %copy-done.2), channel_id=1, source_target_pairs={{0,1},{1,0},{2,3},{3,2},{4,5},{5,4},{6,7},{7,6},{8,9},{9,8},{10,11... | collective-permute-start | bytes 393224 | tf_op jit(solution)/shard_map/ppermute | solution.py:312
  28.7 5.1 %collective-permute-start.2 = (bf16[256,128]{1,0:T(8,128)(2,1)S(1)}, bf16[256,128]{1,0:T(8,128)(2,1)S(1)}, u32[]{:S(2)}, u32[]{:S(2)}) collective-permute-start(bf16[256,128]{1,0:T(8,128)(2,1)S(1)} %get-tuple-element.59), channel_id=1, source_target_pairs={{0,2},{2,0},{32,34},{34,32},{64,66},{66,64},{96,98},{98,96},{1,3},... | collective-permute-start | bytes 196616 | tf_op jit(solution)/shard_map/ppermute | solution.py:316
  28.7 5.4 %collective-permute-start.3 = (bf16[256,128]{1,0:T(8,128)(2,1)S(1)}, bf16[256,128]{1,0:T(8,128)(2,1)S(1)}, u32[]{:S(2)}, u32[]{:S(2)}) collective-permute-start(bf16[256,128]{1,0:T(8,128)(2,1)S(1)} %get-tuple-element.60), channel_id=1, source_target_pairs={{0,32},{2,34},{32,0},{34,2},{64,96},{66,98},{96,64},{98,66},{1,33}... | collective-permute-start | bytes 196616 | tf_op jit(solution)/shard_map/ppermute | solution.py:316
  29.3 7.3 %collective-permute-start.4 = (bf16[256,128]{1,0:T(8,128)(2,1)S(1)}, bf16[256,128]{1,0:T(8,128)(2,1)S(1)}, u32[]{:S(2)}, u32[]{:S(2)}) collective-permute-start(bf16[256,128]{1,0:T(8,128)(2,1)S(1)} %get-tuple-element.61), channel_id=1, source_target_pairs={{0,34},{2,32},{32,2},{34,0},{64,98},{66,96},{96,66},{98,64},{1,35}... | collective-permute-start | bytes 196616 | tf_op jit(solution)/shard_map/ppermute | solution.py:316
  32.5 5.6 %collective-permute-start.5 = (bf16[256,128]{1,0:T(8,128)(2,1)S(1)}, bf16[256,128]{1,0:T(8,128)(2,1)S(1)}, u32[]{:S(2)}, u32[]{:S(2)}) collective-permute-start(bf16[256,128]{1,0:T(8,128)(2,1)S(1)} %get-tuple-element.62), channel_id=1, source_target_pairs={{0,64},{2,66},{32,96},{34,98},{64,0},{66,2},{96,32},{98,34},{1,65}... | collective-permute-start | bytes 196616 | tf_op jit(solution)/shard_map/ppermute | solution.py:316
  33.8 4.3 %collective-permute-start.6 = (bf16[256,128]{1,0:T(8,128)(2,1)S(1)}, bf16[256,128]{1,0:T(8,128)(2,1)S(1)}, u32[]{:S(2)}, u32[]{:S(2)}) collective-permute-start(bf16[256,128]{1,0:T(8,128)(2,1)S(1)} %get-tuple-element.63), channel_id=1, source_target_pairs={{0,66},{2,64},{32,98},{34,96},{64,2},{66,0},{96,34},{98,32},{1,67}... | collective-permute-start | bytes 196616 | tf_op jit(solution)/shard_map/ppermute | solution.py:316
  34.1 5.7 %collective-permute-start.7 = (bf16[256,128]{1,0:T(8,128)(2,1)S(1)}, bf16[256,128]{1,0:T(8,128)(2,1)S(1)}, u32[]{:S(2)}, u32[]{:S(2)}) collective-permute-start(bf16[256,128]{1,0:T(8,128)(2,1)S(1)} %get-tuple-element.64), channel_id=1, source_target_pairs={{0,96},{2,98},{32,64},{34,66},{64,32},{66,34},{96,0},{98,2},{1,97}... | collective-permute-start | bytes 196616 | tf_op jit(solution)/shard_map/ppermute | solution.py:316
  36.6 4.6 %collective-permute-start.8 = (bf16[256,128]{1,0:T(8,128)(2,1)S(1)}, bf16[256,128]{1,0:T(8,128)(2,1)S(1)}, u32[]{:S(2)}, u32[]{:S(2)}) collective-permute-start(bf16[256,128]{1,0:T(8,128)(2,1)S(1)} %get-tuple-element.65), channel_id=1, source_target_pairs={{0,98},{2,96},{32,66},{34,64},{64,34},{66,32},{96,2},{98,0},{1,99}... | collective-permute-start | bytes 196616 | tf_op jit(solution)/shard_map/ppermute | solution.py:316
  46.8 17.9 %copy-start.3 = (bf16[128,128]{1,0:T(8,128)(2,1)S(1)}, bf16[128,128]{1,0:T(8,128)(2,1)}, u32[]{:S(2)}) copy-start(bf16[128,128]{1,0:T(8,128)(2,1)} %rest_8_.1) | copy-start | bytes 98308
  46.8 26.9 %all-to-all-start.1 = ((bf16[128,16,128]{2,1,0:T(8,128)(2,1)}), bf16[128,16,128]{2,1,0:T(8,128)(2,1)S(1)}, u32[]{:S(2)}, u32[]{:S(2)}) async-start(bf16[128,16,128]{2,1,0:T(8,128)(2,1)} %get-tuple-element.78), calls=%async_computation.1 | async-start | bytes 1048576 | tf_op jit(solution)/shard_map/all_to_all | solution.py:308
  54.7 3.7 %collective-permute-start.10 = (bf16[128,128]{1,0:T(8,128)(2,1)S(1)}, bf16[128,128]{1,0:T(8,128)(2,1)S(1)}, u32[]{:S(2)}, u32[]{:S(2)}) collective-permute-start(bf16[128,128]{1,0:T(8,128)(2,1)S(1)} %get-tuple-element.68), channel_id=1, source_target_pairs={{0,2},{2,0},{32,34},{34,32},{64,66},{66,64},{96,98},{98,96},{1,3},... | collective-permute-start | bytes 98312 | tf_op jit(solution)/shard_map/ppermute | solution.py:316
  54.8 5.0 %collective-permute-start.11 = (bf16[128,128]{1,0:T(8,128)(2,1)S(1)}, bf16[128,128]{1,0:T(8,128)(2,1)S(1)}, u32[]{:S(2)}, u32[]{:S(2)}) collective-permute-start(bf16[128,128]{1,0:T(8,128)(2,1)S(1)} %get-tuple-element.69), channel_id=1, source_target_pairs={{0,32},{2,34},{32,0},{34,2},{64,96},{66,98},{96,64},{98,66},{1,33}... | collective-permute-start | bytes 98312 | tf_op jit(solution)/shard_map/ppermute | solution.py:316
  56.4 4.6 %collective-permute-start.12 = (bf16[128,128]{1,0:T(8,128)(2,1)S(1)}, bf16[128,128]{1,0:T(8,128)(2,1)S(1)}, u32[]{:S(2)}, u32[]{:S(2)}) collective-permute-start(bf16[128,128]{1,0:T(8,128)(2,1)S(1)} %get-tuple-element.70), channel_id=1, source_target_pairs={{0,34},{2,32},{32,2},{34,0},{64,98},{66,96},{96,66},{98,64},{1,35}... | collective-permute-start | bytes 98312 | tf_op jit(solution)/shard_map/ppermute | solution.py:316
  56.6 4.7 %collective-permute-start.13 = (bf16[128,128]{1,0:T(8,128)(2,1)S(1)}, bf16[128,128]{1,0:T(8,128)(2,1)S(1)}, u32[]{:S(2)}, u32[]{:S(2)}) collective-permute-start(bf16[128,128]{1,0:T(8,128)(2,1)S(1)} %get-tuple-element.71), channel_id=1, source_target_pairs={{0,64},{2,66},{32,96},{34,98},{64,0},{66,2},{96,32},{98,34},{1,65}... | collective-permute-start | bytes 98312 | tf_op jit(solution)/shard_map/ppermute | solution.py:316
  57.4 4.3 %collective-permute-start.14 = (bf16[128,128]{1,0:T(8,128)(2,1)S(1)}, bf16[128,128]{1,0:T(8,128)(2,1)S(1)}, u32[]{:S(2)}, u32[]{:S(2)}) collective-permute-start(bf16[128,128]{1,0:T(8,128)(2,1)S(1)} %get-tuple-element.72), channel_id=1, source_target_pairs={{0,66},{2,64},{32,98},{34,96},{64,2},{66,0},{96,34},{98,32},{1,67}... | collective-permute-start | bytes 98312 | tf_op jit(solution)/shard_map/ppermute | solution.py:316
  58.3 5.5 %collective-permute-start.15 = (bf16[128,128]{1,0:T(8,128)(2,1)S(1)}, bf16[128,128]{1,0:T(8,128)(2,1)S(1)}, u32[]{:S(2)}, u32[]{:S(2)}) collective-permute-start(bf16[128,128]{1,0:T(8,128)(2,1)S(1)} %get-tuple-element.73), channel_id=1, source_target_pairs={{0,96},{2,98},{32,64},{34,66},{64,32},{66,34},{96,0},{98,2},{1,97}... | collective-permute-start | bytes 98312 | tf_op jit(solution)/shard_map/ppermute | solution.py:316
  59.7 5.0 %collective-permute-start.16 = (bf16[128,128]{1,0:T(8,128)(2,1)S(1)}, bf16[128,128]{1,0:T(8,128)(2,1)S(1)}, u32[]{:S(2)}, u32[]{:S(2)}) collective-permute-start(bf16[128,128]{1,0:T(8,128)(2,1)S(1)} %get-tuple-element.74), channel_id=1, source_target_pairs={{0,98},{2,96},{32,66},{34,64},{64,34},{66,32},{96,2},{98,0},{1,99}... | collective-permute-start | bytes 98312 | tf_op jit(solution)/shard_map/ppermute | solution.py:316
  75.5 1.6 %collective-permute-start.17 = (bf16[128,8,128]{2,1,0:T(8,128)(2,1)S(1)}, bf16[128,8,128]{2,1,0:T(8,128)(2,1)S(1)}, u32[]{:S(2)}, u32[]{:S(2)}) collective-permute-start(bf16[128,8,128]{2,1,0:T(8,128)(2,1)S(1)} %get-tuple-element.80), channel_id=1, source_target_pairs={{0,2},{2,0},{1,3},{3,1},{4,6},{6,4},{5,7},{7,5},{8,10},{10,8},{9,1... | collective-permute-start | bytes 786440 | tf_op jit(solution)/shard_map/ppermute | solution.py:312
  77.2 21.6 %copy-start.4 = (bf16[128,128]{1,0:T(8,128)(2,1)S(1)}, bf16[128,128]{1,0:T(8,128)(2,1)}, u32[]{:S(2)}) copy-start(bf16[128,128]{1,0:T(8,128)(2,1)} %w_ref.1) | copy-start | bytes 98308
  (4 other events, 21.3 us)

commit v5 on v4

--- a/solution.py
+++ b/solution.py
@@ -47,14 +47,14 @@
         normed = standardized(msa_ref[:, i, :].astype(F32), -1).astype(BF16)
         norm_ref[i] = normed
         right = dot(second_ref[...], normed, ((1,), (1,))).astype(BF16)
-        for z in range(8):
+        for z in range(16):
             right_ref[z, i * 32 : (i + 1) * 32, :] = right
 
 
 def firsts(msa, second_t):
     return on_core(
         first_kernel,
-        (jax.ShapeDtypeStruct((8, 128, 128), BF16), jax.ShapeDtypeStruct((4, 128, 256), BF16)),
+        (jax.ShapeDtypeStruct((16, 128, 128), BF16), jax.ShapeDtypeStruct((4, 128, 256), BF16)),
         2,
         cost=cost(1),
     )(msa, second_t)
@@ -67,8 +67,8 @@
         lo = dot(own_ref[...], normed, ((1,), (1,))).astype(BF16)
         hi = dot(other_ref[...], normed, ((1,), (1,))).astype(BF16)
         for m in range(8):
-            packed_refs[m][pl.ds(pl.multiple_of(128 + mex * 64 + i * 16, 16), 16), :] = lo
-            packed_refs[m][pl.ds(pl.multiple_of(192 - mex * 64 + i * 16, 16), 16), :] = hi
+            packed_refs[m][pl.ds(pl.multiple_of(128 + i * 32 + mex * 16, 16), 16), :] = lo
+            packed_refs[m][pl.ds(pl.multiple_of(144 + i * 32 - mex * 16, 16), 16), :] = hi
     row = lax.broadcasted_iota(jnp.int32, (8, 128), 0)
     for m in range(8):
         g = m ^ me
@@ -90,18 +90,23 @@
     )(me, normed, own_t, other_t, couple)
 
 
-def weight_kernel(me_ref, own_ref, other_ref, by_e_ref, w_scr):
+def weight_kernel(me_ref, own_ref, other_ref, wide_ref, w_scr):
     mex = me_ref[1]
     w_scr[pl.ds(pl.multiple_of(mex * 512, 512), 512), :] = own_ref[...].astype(F32)
     w_scr[pl.ds(pl.multiple_of(512 - mex * 512, 512), 512), :] = other_ref[...].astype(F32)
+    blank = jnp.zeros((32, 128), BF16)
     for e in range(32):
-        by_e_ref[e] = w_scr[pl.ds(e, 32, stride=32), :].astype(BF16)
+        w = w_scr[pl.ds(e, 32, stride=32), :].astype(BF16)
+        wide_ref[e * 64 : e * 64 + 32, 0:128] = w
+        wide_ref[e * 64 : e * 64 + 32, 128:256] = blank
+        wide_ref[e * 64 + 32 : e * 64 + 64, 0:128] = blank
+        wide_ref[e * 64 + 32 : e * 64 + 64, 128:256] = w
 
 
 def weights(me, own, other):
     return on_core(
         weight_kernel,
-        jax.ShapeDtypeStruct((32, 32, 128), BF16),
+        jax.ShapeDtypeStruct((2048, 256), BF16),
         3,
         [pltpu.VMEM((1024, 128), F32)],
         scalars=1,
@@ -109,38 +114,34 @@
     )(me, own, other)
 
 
-def pair_kernel(me_ref, own_ref, other_ref, *rest):
-    packed_refs, by_e_ref, entry_ref = rest[:8], rest[8], rest[9]
+def pair_kernel(me_ref, right_ref, *rest):
+    packed_refs, wide_ref, entry_ref = rest[:8], rest[8], rest[9]
     lifted_refs, cols_ref = rest[10:18], rest[18]
-    rows_scr, lhs_scr, cols_scr, wide_scr = rest[19:]
+    rows_scr, lhs_scr, cols_scr = rest[19:]
     me = me_ref[0]
-    keep = me_ref[3] == 1
     for z in range(8):
         for j in range(4):
-            rows = slice(j * 32, (j + 1) * 32)
-            rows_scr[pl.ds(z * 4 + j, 32, stride=32), :] = jnp.where(
-                keep, own_ref[z, rows, :].astype(F32), other_ref[z, rows, :].astype(F32)
-            )
+            rows_scr[pl.ds(z * 4 + j, 32, stride=32), :] = right_ref[
+                me_ref[1] * 8 + z, j * 32 : (j + 1) * 32, :
+            ].astype(F32)
     lefts = jnp.concatenate([packed_refs[m][128:256, :] for m in range(8)], axis=0)
-    blank = jnp.zeros((16, 128), BF16)
+    low = lax.broadcasted_iota(jnp.int32, (32, 128), 1) < 64
     for part in range(4):
-        for e in range(part * 8, part * 8 + 8):
-            for x in range(2):
-                for i in range(4):
-                    for j in range(4):
-                        row = ((e * 2 + x) * 4 + i) * 16
-                        wide_scr[row : row + 16, j * 128 : (j + 1) * 128] = (
-                            by_e_ref[e, x * 16 : (x + 1) * 16, :] if i == j else blank
-                        )
         rows = rows_scr[part * 256 : (part + 1) * 256, :].astype(BF16)
-        outer = (dot(rows, lefts, ((1,), (1,))) * (1.0 / 128)).astype(BF16)
-        for e in range(8):
+        outer = dot(rows, lefts, ((1,), (1,))) * (1.0 / 128)
+        for e in range(4):
             for m in range(8):
-                lhs_scr[m * 32 : (m + 1) * 32, (part * 8 + e) * 128 : (part * 8 + e + 1) * 128] = outer[
-                    e * 32 : (e + 1) * 32, m * 128 : (m + 1) * 128
-                ]
+                lanes = slice(m * 128, (m + 1) * 128)
+                a = outer[e * 64 : e * 64 + 32, lanes]
+                b = outer[e * 64 + 32 : e * 64 + 64, lanes]
+                rows = slice(m * 32, (m + 1) * 32)
+                at = slice((part * 4 + e) * 128, (part * 4 + e + 1) * 128)
+                lhs_scr[0, rows, at] = jnp.where(low, a, pltpu.roll(b, 64, 1)).astype(BF16)
+                lhs_scr[1, rows, at] = jnp.where(low, pltpu.roll(a, 64, 1), b).astype(BF16)
     for half in range(2):
-        update = dot(lhs_scr[half * 128 : (half + 1) * 128, :], wide_scr[...], ((1,), (0,)))
+        update = [
+            dot(lhs_scr[p, half * 128 : (half + 1) * 128, :], wide_ref[...], ((1,), (0,))) for p in range(2)
+        ]
         for mm in range(4):
             m = half * 4 + mm
             normed = []
@@ -148,7 +149,7 @@
                 rows = slice(i * 32, (i + 1) * 32)
                 lifted = (
                     packed_refs[m][rows, :].astype(F32)
-                    + update[mm * 32 : (mm + 1) * 32, i * 128 : (i + 1) * 128]
+                    + update[i // 2][mm * 32 : (mm + 1) * 32, (i % 2) * 128 : (i % 2 + 1) * 128]
                 ).astype(BF16)
                 lifted_refs[m][rows, :] = lifted
                 normed.append(standardized(lifted.astype(F32), -1).astype(BF16))
@@ -162,21 +163,20 @@
         )
 
 
-def pairs(me, right, other, packed, by_e, entry_t):
+def pairs(me, right, packed, by_e, entry_t):
     out = on_core(
         pair_kernel,
         (jax.ShapeDtypeStruct((128, 128), BF16),) * 8 + (jax.ShapeDtypeStruct((128, 16, 128), BF16),),
-        13,
+        12,
         [
             pltpu.VMEM((1024, 128), F32),
-            pltpu.VMEM((256, 4096), BF16),
+            pltpu.VMEM((2, 256, 2048), BF16),
             pltpu.VMEM((2048, 128), F32),
-            pltpu.VMEM((4096, 512), BF16),
         ],
         scalars=1,
-        limit=20,
+        limit=14,
         cost=cost(5),
-    )(me, right, other, *packed, by_e, entry_t)
+    )(me, right, *packed, by_e, entry_t)
     return out[:8], out[8]
 
 
@@ -324,15 +324,12 @@
     ).astype(jnp.int32)
     right, normed = firsts(msa, second.T)
     first_t, w_out, right, normed = lax.optimization_barrier((first.T, w_out, right, normed))
-    right = exchanged(right, "z")
+    right = exchanged(right, ("yh", "z"))
     first_other = partner(first_t, "xh")
     w_other = partner(w_out, "xh")
-    packed = packs(me, normed, first_t, first_other, couple)
-    right, packed = lax.optimization_barrier((right, packed))
-    other = partner(right, "yh")
-    packed = to_peers(packed)
+    packed = to_peers(packs(me, normed, first_t, first_other, couple))
     by_e = weights(me, w_out, w_other)
-    lifted, cols = pairs(me, right, other, packed, by_e, jnp.swapaxes(entry, 1, 2))
+    lifted, cols = pairs(me, right, packed, by_e, jnp.swapaxes(entry, 1, 2))
     cols = exchanged(cols, CHIP)
     gate, base = gates(me, to_peers(lifted), w_gate)
     me, gate, base = lax.optimization_barrier((me, gate, base))

time: 101 us -> 96.7 us (0.957)
  waiting for transfers between devices: 26 us -> 18.7 us
  starting transfers between devices: 37.6 us -> 41.4 us
    all_to_all x2, starting transfers between devices: 16.4 us -> 24.8 us  [exchanged(): return lax.all_to_all(x, axes, split_axis=0, concat_axis=0, tiled=True)]
    all_to_all x2, waiting for transfers between devices: 13.6 us -> 7.28 us  [exchanged(): return lax.all_to_all(x, axes, split_axis=0, concat_axis=0, tiled=True)]
    ppermute x4 -> x3, starting transfers between devices: 8.52 us -> 3.71 us  [partner(): return lax.ppermute(x, axis, [(0, 1), (1, 0)])]
    ppermute x4 -> x3, waiting for transfers between devices: 5.33 us -> 3.07 us  [partner(): return lax.ppermute(x, axis, [(0, 1), (1, 0)])]
    ppermute x14, waiting for transfers between devices: 7.04 us -> 8.36 us  [to_peers(): lax.ppermute(pieces[m], PLANE, [(i, i ^ m) for i in range(8)])]
  transfers between devices with their start and end apart: 20 -> 19, of which waited for: 12 -> 10; matrix products, arithmetic and copies ran while one was open for 0% -> 0% of each run, Pallas kernels for 3% -> 3%
where the time goes in v5:
time: 96.7 us; the launch traced here: 96.2 us
  starting transfers between devices  41.4 us (43%)
  blocking collectives  21.5 us (22%)
  waiting for transfers between devices  18.7 us (19%)
  Pallas kernels  12.5 us (13%)
  local copies, waits for them, and re-layouts  1.82 us (2%)
    all_to_all x2, starting transfers between devices, exchanged(): return lax.all_to_all(x, axes, split_axis=0, concat_axis=0, tiled=True)  24.8 us
    all_to_all x1, blocking collectives, exchanged(): return lax.all_to_all(x, axes, split_axis=0, concat_axis=0, tiled=True)  21.5 us
    ppermute x14, starting transfers between devices, to_peers(): lax.ppermute(pieces[m], PLANE, [(i, i ^ m) for i in range(8)])  12.9 us
    ppermute x14, waiting for transfers between devices, to_peers(): lax.ppermute(pieces[m], PLANE, [(i, i ^ m) for i in range(8)])  8.36 us
    all_to_all x2, waiting for transfers between devices, exchanged(): return lax.all_to_all(x, axes, split_axis=0, concat_axis=0, tiled=True)  7.28 us
    pallas_call x1, Pallas kernels, pairs(): on_core(pair_kernel, (jax.ShapeDtypeStruct((128, 128), BF16),) * 8 + (jax...  4.91 us
    ppermute x3, starting transfers between devices, partner(): return lax.ppermute(x, axis, [(0, 1), (1, 0)])  3.71 us
    ppermute x3, waiting for transfers between devices, partner(): return lax.ppermute(x, axis, [(0, 1), (1, 0)])  3.07 us
  transfers between devices with their start and end apart: 19, of which 10 were waited for; matrix products, arithmetic and copies ran while one was open for 0% of the time, Pallas kernels for 3%

profile of v5, /device:TPU:8, one launch (start us, length us, event | category | flops | bytes accessed | tf_op | source)
XLA Modules:
  0.0 96.2 jit_solution(10628603214188558841)
XLA Ops:
  0.0 0.9 copy-done
  1.7 1.3 %shard_map.82 = (bf16[16,128,128]{2,1,0:T(8,128)(2,1)}, bf16[4,128,256]{2,1,0:T(8,128)(2,1)S(1)}) custom-call(bf16[128,4,256]{2,1,0:T(4,128)(2,1)S(1)} %copy-done, bf16[32,256]{1,0:T(8,128)(2,1)S(1)} %bitcast.9), custom_call_target="tpu_custom_call" | custom-call | flops 1000000000 | bytes 3000000 | tf_op jit(solution)/shard_map/pallas_call | solution.py:55
  3.0 10.4 %all-to-all-start = ((bf16[16,128,128]{2,1,0:T(8,128)(2,1)}), bf16[16,128,128]{2,1,0:T(8,128)(2,1)S(1)}, u32[]{:S(2)}, u32[]{:S(2)}) async-start(bf16[16,128,128]{2,1,0:T(8,128)(2,1)} %get-tuple-element.37), calls=%async_computation | async-start | bytes 1048576 | tf_op jit(solution)/shard_map/all_to_all | solution.py:308
  13.5 3.1 %collective-permute-start = (bf16[16,256]{1,0:T(8,128)(2,1)S(1)}, bf16[16,256]{1,0:T(8,128)(2,1)S(1)}, u32[]{:S(2)}, u32[]{:S(2)}) collective-permute-start(bf16[16,256]{1,0:T(8,128)(2,1)S(1)} %bitcast.10), channel_id=1, source_target_pairs={{0,1},{1,0},{2,3},{3,2},{4,5},{5,4},{6,7},{7,6},{8,9},{9,8},{10,11... | collective-permute-start | bytes 24584 | tf_op jit(solution)/shard_map/ppermute | solution.py:312
  17.2 1.5 %collective-permute-done.other_ref = bf16[16,256]{1,0:T(8,128)(2,1)S(1)} collective-permute-done((bf16[16,256]{1,0:T(8,128)(2,1)S(1)}, bf16[16,256]{1,0:T(8,128)(2,1)S(1)}, u32[]{:S(2)}, u32[]{:S(2)}) %collective-permute-start) | collective-permute-done | bytes 8224 | tf_op jit(solution)/shard_map/ppermute | solution.py:312
  19.7 1.6 %collective-permute-start.2 = (bf16[256,128]{1,0:T(8,128)(2,1)S(1)}, bf16[256,128]{1,0:T(8,128)(2,1)S(1)}, u32[]{:S(2)}, u32[]{:S(2)}) collective-permute-start(bf16[256,128]{1,0:T(8,128)(2,1)S(1)} %get-tuple-element.42), channel_id=1, source_target_pairs={{0,32},{2,34},{32,0},{34,2},{64,96},{66,98},{96,64},{98,66},{1,33}... | collective-permute-start | bytes 196616 | tf_op jit(solution)/shard_map/ppermute | solution.py:316
  21.8 1.4 %collective-permute-start.4 = (bf16[256,128]{1,0:T(8,128)(2,1)S(1)}, bf16[256,128]{1,0:T(8,128)(2,1)S(1)}, u32[]{:S(2)}, u32[]{:S(2)}) collective-permute-start(bf16[256,128]{1,0:T(8,128)(2,1)S(1)} %get-tuple-element.44), channel_id=1, source_target_pairs={{0,64},{2,66},{32,96},{34,98},{64,0},{66,2},{96,32},{98,34},{1,65}... | collective-permute-start | bytes 196616 | tf_op jit(solution)/shard_map/ppermute | solution.py:316
  24.2 2.7 %collective-permute-start.6 = (bf16[256,128]{1,0:T(8,128)(2,1)S(1)}, bf16[256,128]{1,0:T(8,128)(2,1)S(1)}, u32[]{:S(2)}, u32[]{:S(2)}) collective-permute-start(bf16[256,128]{1,0:T(8,128)(2,1)S(1)} %get-tuple-element.46), channel_id=1, source_target_pairs={{0,96},{2,98},{32,64},{34,66},{64,32},{66,34},{96,0},{98,2},{1,97}... | collective-permute-start | bytes 196616 | tf_op jit(solution)/shard_map/ppermute | solution.py:316
  27.0 1.0 %shard_map.84.rest_8_ = bf16[2048,256]{1,0:T(8,128)(2,1)S(1)} custom-call(s32[4]{0:T(128)S(1)} %pad_add_fusion.me_ref, bf16[512,128]{1,0:T(8,128)(2,1)S(1)} %copy-done.2, bf16[512,128]{1,0:T(8,128)(2,1)S(1)} %collective-permute-done.8.other_ref), custom_call_target="tpu_custom_call" | custom-call | flops 1000000000 | bytes 3000000 | tf_op jit(solution)/shard_map/pallas_call | solution.py:107
  28.6 3.0 %collective-permute-done.5.rest_5_ = bf16[256,128]{1,0:T(8,128)(2,1)S(1)} collective-permute-done((bf16[256,128]{1,0:T(8,128)(2,1)S(1)}, bf16[256,128]{1,0:T(8,128)(2,1)S(1)}, u32[]{:S(2)}, u32[]{:S(2)}) %collective-permute-start.5) | collective-permute-done | bytes 65568 | tf_op jit(solution)/shard_map/ppermute | solution.py:316
  31.6 4.9 %shard_map.85 = (bf16[128,128]{1,0:T(8,128)(2,1)S(1)}, bf16[128,128]{1,0:T(8,128)(2,1)S(1)}, bf16[128,128]{1,0:T(8,128)(2,1)S(1)}, bf16[128,128]{1,0:T(8,128)(2,...) custom-call(s32[4]{0:T(128)S(1)} %pad_add_fusion.me_ref, ...), custom_call_target="tpu_custom_call" | custom-call | flops 5000000000 | bytes 15000000 | tf_op jit(solution)/shard_map/pallas_call | solution.py:167
  36.6 14.4 %all-to-all-start.1 = ((bf16[128,16,128]{2,1,0:T(8,128)(2,1)}), bf16[128,16,128]{2,1,0:T(8,128)(2,1)S(1)}, u32[]{:S(2)}, u32[]{:S(2)}) async-start(bf16[128,16,128]{2,1,0:T(8,128)(2,1)} %get-tuple-element.60), calls=%async_computation.1 | async-start | bytes 1048576 | tf_op jit(solution)/shard_map/all_to_all | solution.py:308
  51.0 1.8 %collective-permute-start.10 = (bf16[128,128]{1,0:T(8,128)(2,1)S(1)}, bf16[128,128]{1,0:T(8,128)(2,1)S(1)}, u32[]{:S(2)}, u32[]{:S(2)}) collective-permute-start(bf16[128,128]{1,0:T(8,128)(2,1)S(1)} %get-tuple-element.51), channel_id=1, source_target_pairs={{0,32},{2,34},{32,0},{34,2},{64,96},{66,98},{96,64},{98,66},{1,33}... | collective-permute-start | bytes 98312 | tf_op jit(solution)/shard_map/ppermute | solution.py:316
  53.7 1.1 %collective-permute-start.13 = (bf16[128,128]{1,0:T(8,128)(2,1)S(1)}, bf16[128,128]{1,0:T(8,128)(2,1)S(1)}, u32[]{:S(2)}, u32[]{:S(2)}) collective-permute-start(bf16[128,128]{1,0:T(8,128)(2,1)S(1)} %get-tuple-element.54), channel_id=1, source_target_pairs={{0,66},{2,64},{32,98},{34,96},{64,2},{66,0},{96,34},{98,32},{1,67}... | collective-permute-start | bytes 98312 | tf_op jit(solution)/shard_map/ppermute | solution.py:316
  54.8 1.4 %collective-permute-start.14 = (bf16[128,128]{1,0:T(8,128)(2,1)S(1)}, bf16[128,128]{1,0:T(8,128)(2,1)S(1)}, u32[]{:S(2)}, u32[]{:S(2)}) collective-permute-start(bf16[128,128]{1,0:T(8,128)(2,1)S(1)} %get-tuple-element.55), channel_id=1, source_target_pairs={{0,96},{2,98},{32,64},{34,66},{64,32},{66,34},{96,0},{98,2},{1,97}... | collective-permute-start | bytes 98312 | tf_op jit(solution)/shard_map/ppermute | solution.py:316
  56.2 1.1 %collective-permute-start.15 = (bf16[128,128]{1,0:T(8,128)(2,1)S(1)}, bf16[128,128]{1,0:T(8,128)(2,1)S(1)}, u32[]{:S(2)}, u32[]{:S(2)}) collective-permute-start(bf16[128,128]{1,0:T(8,128)(2,1)S(1)} %get-tuple-element.56), channel_id=1, source_target_pairs={{0,98},{2,96},{32,66},{34,64},{64,34},{66,32},{96,2},{98,0},{1,99}... | collective-permute-start | bytes 98312 | tf_op jit(solution)/shard_map/ppermute | solution.py:316
  57.9 2.1 %collective-permute-done.14.rest_6_ = bf16[128,128]{1,0:T(8,128)(2,1)S(1)} collective-permute-done((bf16[128,128]{1,0:T(8,128)(2,1)S(1)}, bf16[128,128]{1,0:T(8,128)(2,1)S(1)}, u32[]{:S(2)}, u32[]{:S(2)}) %collective-permute-start.14) | collective-permute-done | bytes 32800 | tf_op jit(solution)/shard_map/ppermute | solution.py:316
  60.0 1.3 %collective-permute-done.15.rest_7_ = bf16[128,128]{1,0:T(8,128)(2,1)S(1)} collective-permute-done((bf16[128,128]{1,0:T(8,128)(2,1)S(1)}, bf16[128,128]{1,0:T(8,128)(2,1)S(1)}, u32[]{:S(2)}, u32[]{:S(2)}) %collective-permute-start.15) | collective-permute-done | bytes 32800 | tf_op jit(solution)/shard_map/ppermute | solution.py:316
  61.3 1.1 %shard_map.86 = (f32[1024,128]{1,0:T(8,128)S(1)}, f32[1024,128]{1,0:T(8,128)S(1)}) custom-call(s32[4]{0:T(128)S(1)} %pad_add_fusion.me_ref, bf16[128,128]{1,0:T(8,128)(2,1)S(1)} %get-tuple-element.49.rest_0_, bf16[128,128]{1,0:T(8,128)(2,1)S(1)} %collective-permute-done.9.rest_1_, bf16[128,128]{1,0:T(8,128)(2,1)S(1)} %collective-permute-done.10.rest_2_, ...), custom_call_target="tpu_custom_call" | custom-call | flops 2000000000 | bytes 6000000 | tf_op jit(solution)/shard_map/pallas_call | solution.py:271
  62.3 7.3 %all-to-all-done.1.cols_ref = bf16[128,16,128]{2,1,0:T(8,128)(2,1)S(1)} async-done(((bf16[128,16,128]{2,1,0:T(8,128)(2,1)}), bf16[128,16,128]{2,1,0:T(8,128)(2,1)S(1)}, u32[]{:S(2)}, u32[]{:S(2)}) %all-to-all-start.1) | async-done | bytes 524320 | tf_op jit(solution)/shard_map/all_to_all | solution.py:308
  69.6 1.8 %shard_map.87 = (f32[128,8,128]{2,1,0:T(8,128)S(1)}, bf16[128,8,128]{2,1,0:T(8,128)(2,1)S(1)}) custom-call(s32[4]{0:T(128)S(1)} %pad_add_fusion.me_ref, bf16[128,16,128]{2,1,0:T(8,128)(2,1)S(1)} %all-to-all-done.1.cols_ref), custom_call_target="tpu_custom_call" | custom-call | flops 3000000000 | bytes 9000000 | tf_op jit(solution)/shard_map/pallas_call | solution.py:234
  71.5 1.5 %collective-permute-done.16 = bf16[128,8,128]{2,1,0:T(8,128)(2,1)S(1)} collective-permute-done((bf16[128,8,128]{2,1,0:T(8,128)(2,1)S(1)}, bf16[128,8,128]{2,1,0:T(8,128)(2,1)S(1)}, u32[]{:S(2)}, u32[]{:S(2)}) %collective-permute-start.16) | collective-permute-done | bytes 262176 | tf_op jit(solution)/shard_map/ppermute | solution.py:312
  73.1 21.5 %all_to_all.15.mixed_ref = bf16[128,8,128]{2,1,0:T(8,128)(2,1)S(1)} all-to-all(bf16[128,8,128]{2,1,0:T(8,128)(2,1)S(1)} %add_convert_fusion), channel_id=1, replica_groups=mesh['yh'=2,'yl'=2,'xl'=2,'z'=8,'core'=2,'xh'=2] {'yh','yl','xl','z','xh'}, dimensions={0} | all-to-all | bytes 524288 | tf_op jit(solution)/shard_map/all_to_all | solution.py:308
  94.6 1.6 %shard_map.88 = bf16[1024,128]{1,0:T(8,128)(2,1)} custom-call(bf16[128,8,128]{2,1,0:T(8,128)(2,1)S(1)} %all_to_all.15.mixed_ref, f32[1024,128]{1,0:T(8,128)S(1)} %get-tuple-element.63.gate_ref, f32[1024,128]{1,0:T(8,128)S(1)} %get-tuple-element.64.base_ref, bf16[128,128]{1,0:T(8,128)(2,1)S(1)} %copy-done.4), custom_call_target="tpu_custom_call" | custom-call | flops 2000000000 | bytes 6000000 | tf_op jit(solution)/shard_map/pallas_call | solution.py:298
  (41 shorter events, 6.1 us)
Async XLA Ops:
  3.0 10.4 %copy-start.6 = (bf16[256,16]{0,1:T(8,128)(2,1)S(1)}, bf16[256,16]{0,1:T(8,128)(2,1)}, u32[]{:S(2)}) copy-start(bf16[256,16]{0,1:T(8,128)(2,1)} %param.10) | copy-start | bytes 24580
  3.0 13.6 %copy-start.2 = (bf16[512,128]{1,0:T(8,128)(2,1)S(1)}, bf16[512,128]{1,0:T(8,128)(2,1)}, u32[]{:S(2)}) copy-start(bf16[512,128]{1,0:T(8,128)(2,1)} %own_ref) | copy-start | bytes 393220
  3.0 15.7 %copy-start.1 = (bf16[4,256,128]{2,1,0:T(8,128)(2,1)S(1)}, bf16[4,256,128]{2,1,0:T(8,128)(2,1)}, u32[]{:S(2)}) copy-start(bf16[4,256,128]{2,1,0:T(8,128)(2,1)} %couple_ref.1) | copy-start | bytes 786436
  3.0 28.6 %all-to-all-start = ((bf16[16,128,128]{2,1,0:T(8,128)(2,1)}), bf16[16,128,128]{2,1,0:T(8,128)(2,1)S(1)}, u32[]{:S(2)}, u32[]{:S(2)}) async-start(bf16[16,128,128]{2,1,0:T(8,128)(2,1)} %get-tuple-element.37), calls=%async_computation | async-start | bytes 1048576 | tf_op jit(solution)/shard_map/all_to_all | solution.py:308
  13.5 5.2 %collective-permute-start = (bf16[16,256]{1,0:T(8,128)(2,1)S(1)}, bf16[16,256]{1,0:T(8,128)(2,1)S(1)}, u32[]{:S(2)}, u32[]{:S(2)}) collective-permute-start(bf16[16,256]{1,0:T(8,128)(2,1)S(1)} %bitcast.10), channel_id=1, source_target_pairs={{0,1},{1,0},{2,3},{3,2},{4,5},{5,4},{6,7},{7,6},{8,9},{9,8},{10,11... | collective-permute-start | bytes 24584 | tf_op jit(solution)/shard_map/ppermute | solution.py:312
  16.6 10.4 %collective-permute-start.8 = (bf16[512,128]{1,0:T(8,128)(2,1)S(1)}, bf16[512,128]{1,0:T(8,128)(2,1)S(1)}, u32[]{:S(2)}, u32[]{:S(2)}) collective-permute-start(bf16[512,128]{1,0:T(8,128)(2,1)S(1)} %copy-done.2), channel_id=1, source_target_pairs={{0,1},{1,0},{2,3},{3,2},{4,5},{5,4},{6,7},{7,6},{8,9},{9,8},{10,11... | collective-permute-start | bytes 393224 | tf_op jit(solution)/shard_map/ppermute | solution.py:312
  19.6 3.6 %collective-permute-start.1 = (bf16[256,128]{1,0:T(8,128)(2,1)S(1)}, bf16[256,128]{1,0:T(8,128)(2,1)S(1)}, u32[]{:S(2)}, u32[]{:S(2)}) collective-permute-start(bf16[256,128]{1,0:T(8,128)(2,1)S(1)} %get-tuple-element.41), channel_id=1, source_target_pairs={{0,2},{2,0},{32,34},{34,32},{64,66},{66,64},{96,98},{98,96},{1,3},... | collective-permute-start | bytes 196616 | tf_op jit(solution)/shard_map/ppermute | solution.py:316
  19.7 4.5 %collective-permute-start.2 = (bf16[256,128]{1,0:T(8,128)(2,1)S(1)}, bf16[256,128]{1,0:T(8,128)(2,1)S(1)}, u32[]{:S(2)}, u32[]{:S(2)}) collective-permute-start(bf16[256,128]{1,0:T(8,128)(2,1)S(1)} %get-tuple-element.42), channel_id=1, source_target_pairs={{0,32},{2,34},{32,0},{34,2},{64,96},{66,98},{96,64},{98,66},{1,33}... | collective-permute-start | bytes 196616 | tf_op jit(solution)/shard_map/ppermute | solution.py:316
  21.4 6.5 %collective-permute-start.3 = (bf16[256,128]{1,0:T(8,128)(2,1)S(1)}, bf16[256,128]{1,0:T(8,128)(2,1)S(1)}, u32[]{:S(2)}, u32[]{:S(2)}) collective-permute-start(bf16[256,128]{1,0:T(8,128)(2,1)S(1)} %get-tuple-element.43), channel_id=1, source_target_pairs={{0,34},{2,32},{32,2},{34,0},{64,98},{66,96},{96,66},{98,64},{1,35}... | collective-permute-start | bytes 196616 | tf_op jit(solution)/shard_map/ppermute | solution.py:316
  21.8 6.8 %collective-permute-start.4 = (bf16[256,128]{1,0:T(8,128)(2,1)S(1)}, bf16[256,128]{1,0:T(8,128)(2,1)S(1)}, u32[]{:S(2)}, u32[]{:S(2)}) collective-permute-start(bf16[256,128]{1,0:T(8,128)(2,1)S(1)} %get-tuple-element.44), channel_id=1, source_target_pairs={{0,64},{2,66},{32,96},{34,98},{64,0},{66,2},{96,32},{98,34},{1,65}... | collective-permute-start | bytes 196616 | tf_op jit(solution)/shard_map/ppermute | solution.py:316
  23.2 8.5 %collective-permute-start.5 = (bf16[256,128]{1,0:T(8,128)(2,1)S(1)}, bf16[256,128]{1,0:T(8,128)(2,1)S(1)}, u32[]{:S(2)}, u32[]{:S(2)}) collective-permute-start(bf16[256,128]{1,0:T(8,128)(2,1)S(1)} %get-tuple-element.45), channel_id=1, source_target_pairs={{0,66},{2,64},{32,98},{34,96},{64,2},{66,0},{96,34},{98,32},{1,67}... | collective-permute-start | bytes 196616 | tf_op jit(solution)/shard_map/ppermute | solution.py:316
  24.2 7.4 %collective-permute-start.6 = (bf16[256,128]{1,0:T(8,128)(2,1)S(1)}, bf16[256,128]{1,0:T(8,128)(2,1)S(1)}, u32[]{:S(2)}, u32[]{:S(2)}) collective-permute-start(bf16[256,128]{1,0:T(8,128)(2,1)S(1)} %get-tuple-element.46), channel_id=1, source_target_pairs={{0,96},{2,98},{32,64},{34,66},{64,32},{66,34},{96,0},{98,2},{1,97}... | collective-permute-start | bytes 196616 | tf_op jit(solution)/shard_map/ppermute | solution.py:316
  27.0 4.7 %collective-permute-start.7 = (bf16[256,128]{1,0:T(8,128)(2,1)S(1)}, bf16[256,128]{1,0:T(8,128)(2,1)S(1)}, u32[]{:S(2)}, u32[]{:S(2)}) collective-permute-start(bf16[256,128]{1,0:T(8,128)(2,1)S(1)} %get-tuple-element.47), channel_id=1, source_target_pairs={{0,98},{2,96},{32,66},{34,64},{64,34},{66,32},{96,2},{98,0},{1,99}... | collective-permute-start | bytes 196616 | tf_op jit(solution)/shard_map/ppermute | solution.py:316
  36.6 24.7 %copy-start.3 = (bf16[128,128]{1,0:T(8,128)(2,1)S(1)}, bf16[128,128]{1,0:T(8,128)(2,1)}, u32[]{:S(2)}) copy-start(bf16[128,128]{1,0:T(8,128)(2,1)} %rest_8_.1) | copy-start | bytes 98308
  36.6 33.1 %all-to-all-start.1 = ((bf16[128,16,128]{2,1,0:T(8,128)(2,1)}), bf16[128,16,128]{2,1,0:T(8,128)(2,1)S(1)}, u32[]{:S(2)}, u32[]{:S(2)}) async-start(bf16[128,16,128]{2,1,0:T(8,128)(2,1)} %get-tuple-element.60), calls=%async_computation.1 | async-start | bytes 1048576 | tf_op jit(solution)/shard_map/all_to_all | solution.py:308
  50.9 3.9 %collective-permute-start.9 = (bf16[128,128]{1,0:T(8,128)(2,1)S(1)}, bf16[128,128]{1,0:T(8,128)(2,1)S(1)}, u32[]{:S(2)}, u32[]{:S(2)}) collective-permute-start(bf16[128,128]{1,0:T(8,128)(2,1)S(1)} %get-tuple-element.50), channel_id=1, source_target_pairs={{0,2},{2,0},{32,34},{34,32},{64,66},{66,64},{96,98},{98,96},{1,3},... | collective-permute-start | bytes 98312 | tf_op jit(solution)/shard_map/ppermute | solution.py:316
  51.0 5.1 %collective-permute-start.10 = (bf16[128,128]{1,0:T(8,128)(2,1)S(1)}, bf16[128,128]{1,0:T(8,128)(2,1)S(1)}, u32[]{:S(2)}, u32[]{:S(2)}) collective-permute-start(bf16[128,128]{1,0:T(8,128)(2,1)S(1)} %get-tuple-element.51), channel_id=1, source_target_pairs={{0,32},{2,34},{32,0},{34,2},{64,96},{66,98},{96,64},{98,66},{1,33}... | collective-permute-start | bytes 98312 | tf_op jit(solution)/shard_map/ppermute | solution.py:316
  52.9 4.4 %collective-permute-start.11 = (bf16[128,128]{1,0:T(8,128)(2,1)S(1)}, bf16[128,128]{1,0:T(8,128)(2,1)S(1)}, u32[]{:S(2)}, u32[]{:S(2)}) collective-permute-start(bf16[128,128]{1,0:T(8,128)(2,1)S(1)} %get-tuple-element.52), channel_id=1, source_target_pairs={{0,34},{2,32},{32,2},{34,0},{64,98},{66,96},{96,66},{98,64},{1,35}... | collective-permute-start | bytes 98312 | tf_op jit(solution)/shard_map/ppermute | solution.py:316
  52.9 4.6 %collective-permute-start.12 = (bf16[128,128]{1,0:T(8,128)(2,1)S(1)}, bf16[128,128]{1,0:T(8,128)(2,1)S(1)}, u32[]{:S(2)}, u32[]{:S(2)}) collective-permute-start(bf16[128,128]{1,0:T(8,128)(2,1)S(1)} %get-tuple-element.53), channel_id=1, source_target_pairs={{0,64},{2,66},{32,96},{34,98},{64,0},{66,2},{96,32},{98,34},{1,65}... | collective-permute-start | bytes 98312 | tf_op jit(solution)/shard_map/ppermute | solution.py:316
  53.7 4.2 %collective-permute-start.13 = (bf16[128,128]{1,0:T(8,128)(2,1)S(1)}, bf16[128,128]{1,0:T(8,128)(2,1)S(1)}, u32[]{:S(2)}, u32[]{:S(2)}) collective-permute-start(bf16[128,128]{1,0:T(8,128)(2,1)S(1)} %get-tuple-element.54), channel_id=1, source_target_pairs={{0,66},{2,64},{32,98},{34,96},{64,2},{66,0},{96,34},{98,32},{1,67}... | collective-permute-start | bytes 98312 | tf_op jit(solution)/shard_map/ppermute | solution.py:316
  54.8 5.2 %collective-permute-start.14 = (bf16[128,128]{1,0:T(8,128)(2,1)S(1)}, bf16[128,128]{1,0:T(8,128)(2,1)S(1)}, u32[]{:S(2)}, u32[]{:S(2)}) collective-permute-start(bf16[128,128]{1,0:T(8,128)(2,1)S(1)} %get-tuple-element.55), channel_id=1, source_target_pairs={{0,96},{2,98},{32,64},{34,66},{64,32},{66,34},{96,0},{98,2},{1,97}... | collective-permute-start | bytes 98312 | tf_op jit(solution)/shard_map/ppermute | solution.py:316
  56.2 5.1 %collective-permute-start.15 = (bf16[128,128]{1,0:T(8,128)(2,1)S(1)}, bf16[128,128]{1,0:T(8,128)(2,1)S(1)}, u32[]{:S(2)}, u32[]{:S(2)}) collective-permute-start(bf16[128,128]{1,0:T(8,128)(2,1)S(1)} %get-tuple-element.56), channel_id=1, source_target_pairs={{0,98},{2,96},{32,66},{34,64},{64,34},{66,32},{96,2},{98,0},{1,99}... | collective-permute-start | bytes 98312 | tf_op jit(solution)/shard_map/ppermute | solution.py:316
  71.4 1.6 %collective-permute-start.16 = (bf16[128,8,128]{2,1,0:T(8,128)(2,1)S(1)}, bf16[128,8,128]{2,1,0:T(8,128)(2,1)S(1)}, u32[]{:S(2)}, u32[]{:S(2)}) collective-permute-start(bf16[128,8,128]{2,1,0:T(8,128)(2,1)S(1)} %get-tuple-element.62), channel_id=1, source_target_pairs={{0,2},{2,0},{1,3},{3,1},{4,6},{6,4},{5,7},{7,5},{8,10},{10,8},{9,1... | collective-permute-start | bytes 786440 | tf_op jit(solution)/shard_map/ppermute | solution.py:312
  73.1 21.6 %copy-start.4 = (bf16[128,128]{1,0:T(8,128)(2,1)S(1)}, bf16[128,128]{1,0:T(8,128)(2,1)}, u32[]{:S(2)}) copy-start(bf16[128,128]{1,0:T(8,128)(2,1)} %w_ref.1) | copy-start | bytes 98308
  (3 other events, 5.8 us)

commit v6 on v5

--- a/solution.py
+++ b/solution.py
@@ -42,7 +42,15 @@
     return pl.CostEstimate(flops=int(us * 1e9), bytes_accessed=int(us * 3e6), transcendentals=0)
 
 
-def first_kernel(msa_ref, second_ref, right_ref, norm_ref):
+def first_kernel(msa_hbm, second_hbm, right_ref, norm_ref, msa_ref, second_ref, sems):
+    fetches = [
+        pltpu.make_async_copy(msa_hbm, msa_ref, sems.at[0]),
+        pltpu.make_async_copy(second_hbm, second_ref, sems.at[1]),
+    ]
+    for fetch in fetches:
+        fetch.start()
+    for fetch in fetches:
+        fetch.wait()
     for i in range(4):
         normed = standardized(msa_ref[:, i, :].astype(F32), -1).astype(BF16)
         norm_ref[i] = normed
@@ -52,11 +60,18 @@
 
 
 def firsts(msa, second_t):
-    return on_core(
+    return pl.pallas_call(
         first_kernel,
-        (jax.ShapeDtypeStruct((16, 128, 128), BF16), jax.ShapeDtypeStruct((4, 128, 256), BF16)),
-        2,
-        cost=cost(1),
+        out_shape=(jax.ShapeDtypeStruct((16, 128, 128), BF16), jax.ShapeDtypeStruct((4, 128, 256), BF16)),
+        in_specs=[pl.BlockSpec(memory_space=pl.ANY)] * 2,
+        out_specs=(VMEM, VMEM),
+        scratch_shapes=[
+            pltpu.VMEM((128, 4, 256), BF16),
+            pltpu.VMEM((32, 256), BF16),
+            pltpu.SemaphoreType.DMA((2,)),
+        ],
+        compiler_params=pltpu.CompilerParams(vmem_limit_bytes=60 << 20),
+        cost_estimate=cost(1),
     )(msa, second_t)
 
 
@@ -128,7 +143,7 @@
     low = lax.broadcasted_iota(jnp.int32, (32, 128), 1) < 64
     for part in range(4):
         rows = rows_scr[part * 256 : (part + 1) * 256, :].astype(BF16)
-        outer = dot(rows, lefts, ((1,), (1,))) * (1.0 / 128)
+        outer = dot(rows, lefts, ((1,), (1,)))
         for e in range(4):
             for m in range(8):
                 lanes = slice(m * 128, (m + 1) * 128)
@@ -149,7 +164,7 @@
                 rows = slice(i * 32, (i + 1) * 32)
                 lifted = (
                     packed_refs[m][rows, :].astype(F32)
-                    + update[i // 2][mm * 32 : (mm + 1) * 32, (i % 2) * 128 : (i % 2 + 1) * 128]
+                    + update[i // 2][mm * 32 : (mm + 1) * 32, (i % 2) * 128 : (i % 2 + 1) * 128] * (1.0 / 128)
                 ).astype(BF16)
                 lifted_refs[m][rows, :] = lifted
                 normed.append(standardized(lifted.astype(F32), -1).astype(BF16))

time: 96.7 us -> 95.8 us (level)
  local copies, waits for them, and re-layouts: 1.82 us -> 0.17 us
    unnamed x17 -> x15, local copies, waits for them, and re-layouts: 1.82 us -> 0.17 us
    pallas_call x1, Pallas kernels: 1.34 us -> 2.31 us  [firsts(): pl.pallas_call(first_kernel, out_shape=(jax.ShapeDtypeStruct((16, 128, 12...]
where the time goes in v6:
time: 95.8 us; the launch traced here: 95.4 us
  starting transfers between devices  41.4 us (43%)
  blocking collectives  21.5 us (22%)
  waiting for transfers between devices  18.7 us (20%)
  Pallas kernels  13.3 us (14%)
    all_to_all x2, starting transfers between devices, exchanged(): return lax.all_to_all(x, axes, split_axis=0, concat_axis=0, tiled=True)  24.8 us
    all_to_all x1, blocking collectives, exchanged(): return lax.all_to_all(x, axes, split_axis=0, concat_axis=0, tiled=True)  21.5 us
    ppermute x14, starting transfers between devices, to_peers(): lax.ppermute(pieces[m], PLANE, [(i, i ^ m) for i in range(8)])  12.9 us
    ppermute x14, waiting for transfers between devices, to_peers(): lax.ppermute(pieces[m], PLANE, [(i, i ^ m) for i in range(8)])  8.36 us
    all_to_all x2, waiting for transfers between devices, exchanged(): return lax.all_to_all(x, axes, split_axis=0, concat_axis=0, tiled=True)  7.28 us
    pallas_call x1, Pallas kernels, pairs(): on_core(pair_kernel, (jax.ShapeDtypeStruct((128, 128), BF16),) * 8 + (jax...  4.71 us
    ppermute x3, starting transfers between devices, partner(): return lax.ppermute(x, axis, [(0, 1), (1, 0)])  3.71 us
    ppermute x3, waiting for transfers between devices, partner(): return lax.ppermute(x, axis, [(0, 1), (1, 0)])  3.07 us
  transfers between devices with their start and end apart: 19, of which 10 were waited for; matrix products, arithmetic and copies ran while one was open for 0% of the time, Pallas kernels for 3%

profile of v6, /device:TPU:8, one launch (start us, length us, event | category | flops | bytes accessed | tf_op | source)
XLA Modules:
  0.0 95.4 jit_solution(17515222887835707211)
XLA Ops:
  0.0 2.3 %shard_map.82 = (bf16[16,128,128]{2,1,0:T(8,128)(2,1)}, bf16[4,128,256]{2,1,0:T(8,128)(2,1)}) custom-call(bf16[128,4,256]{2,1,0:T(4,128)(2,1)} %msa_hbm.1, bf16[32,256]{1,0:T(8,128)(2,1)} %bitcast.11), custom_call_target="tpu_custom_call" | custom-call | flops 1000000000 | bytes 3000000 | tf_op jit(solution)/shard_map/pallas_call | solution.py:63
  2.4 10.4 %all-to-all-start = ((bf16[16,128,128]{2,1,0:T(8,128)(2,1)}), bf16[16,128,128]{2,1,0:T(8,128)(2,1)S(1)}, u32[]{:S(2)}, u32[]{:S(2)}) async-start(bf16[16,128,128]{2,1,0:T(8,128)(2,1)} %get-tuple-element.37), calls=%async_computation | async-start | bytes 1048576 | tf_op jit(solution)/shard_map/all_to_all | solution.py:323
  12.8 3.1 %collective-permute-start = (bf16[16,256]{1,0:T(8,128)(2,1)S(1)}, bf16[16,256]{1,0:T(8,128)(2,1)S(1)}, u32[]{:S(2)}, u32[]{:S(2)}) collective-permute-start(bf16[16,256]{1,0:T(8,128)(2,1)S(1)} %bitcast.9), channel_id=1, source_target_pairs={{0,1},{1,0},{2,3},{3,2},{4,5},{5,4},{6,7},{7,6},{8,9},{9,8},{10,11... | collective-permute-start | bytes 24584 | tf_op jit(solution)/shard_map/ppermute | solution.py:327
  16.5 1.5 %collective-permute-done.other_ref = bf16[16,256]{1,0:T(8,128)(2,1)S(1)} collective-permute-done((bf16[16,256]{1,0:T(8,128)(2,1)S(1)}, bf16[16,256]{1,0:T(8,128)(2,1)S(1)}, u32[]{:S(2)}, u32[]{:S(2)}) %collective-permute-start) | collective-permute-done | bytes 8224 | tf_op jit(solution)/shard_map/ppermute | solution.py:327
  18.1 0.9 shard_map.83
  19.1 1.6 %collective-permute-start.2 = (bf16[256,128]{1,0:T(8,128)(2,1)S(1)}, bf16[256,128]{1,0:T(8,128)(2,1)S(1)}, u32[]{:S(2)}, u32[]{:S(2)}) collective-permute-start(bf16[256,128]{1,0:T(8,128)(2,1)S(1)} %get-tuple-element.42), channel_id=1, source_target_pairs={{0,32},{2,34},{32,0},{34,2},{64,96},{66,98},{96,64},{98,66},{1,33}... | collective-permute-start | bytes 196616 | tf_op jit(solution)/shard_map/ppermute | solution.py:331
  21.2 1.4 %collective-permute-start.4 = (bf16[256,128]{1,0:T(8,128)(2,1)S(1)}, bf16[256,128]{1,0:T(8,128)(2,1)S(1)}, u32[]{:S(2)}, u32[]{:S(2)}) collective-permute-start(bf16[256,128]{1,0:T(8,128)(2,1)S(1)} %get-tuple-element.44), channel_id=1, source_target_pairs={{0,64},{2,66},{32,96},{34,98},{64,0},{66,2},{96,32},{98,34},{1,65}... | collective-permute-start | bytes 196616 | tf_op jit(solution)/shard_map/ppermute | solution.py:331
  23.6 2.7 %collective-permute-start.6 = (bf16[256,128]{1,0:T(8,128)(2,1)S(1)}, bf16[256,128]{1,0:T(8,128)(2,1)S(1)}, u32[]{:S(2)}, u32[]{:S(2)}) collective-permute-start(bf16[256,128]{1,0:T(8,128)(2,1)S(1)} %get-tuple-element.46), channel_id=1, source_target_pairs={{0,96},{2,98},{32,64},{34,66},{64,32},{66,34},{96,0},{98,2},{1,97}... | collective-permute-start | bytes 196616 | tf_op jit(solution)/shard_map/ppermute | solution.py:331
  26.3 1.0 %shard_map.84.rest_8_ = bf16[2048,256]{1,0:T(8,128)(2,1)S(1)} custom-call(s32[4]{0:T(128)S(1)} %pad_add_fusion.me_ref, bf16[512,128]{1,0:T(8,128)(2,1)S(1)} %copy-done.1, bf16[512,128]{1,0:T(8,128)(2,1)S(1)} %collective-permute-done.8.other_ref), custom_call_target="tpu_custom_call" | custom-call | flops 1000000000 | bytes 3000000 | tf_op jit(solution)/shard_map/pallas_call | solution.py:122
  28.0 3.0 %collective-permute-done.5.rest_5_ = bf16[256,128]{1,0:T(8,128)(2,1)S(1)} collective-permute-done((bf16[256,128]{1,0:T(8,128)(2,1)S(1)}, bf16[256,128]{1,0:T(8,128)(2,1)S(1)}, u32[]{:S(2)}, u32[]{:S(2)}) %collective-permute-start.5) | collective-permute-done | bytes 65568 | tf_op jit(solution)/shard_map/ppermute | solution.py:331
  31.0 4.7 %shard_map.85 = (bf16[128,128]{1,0:T(8,128)(2,1)S(1)}, bf16[128,128]{1,0:T(8,128)(2,1)S(1)}, bf16[128,128]{1,0:T(8,128)(2,1)S(1)}, bf16[128,128]{1,0:T(8,128)(2,...) custom-call(s32[4]{0:T(128)S(1)} %pad_add_fusion.me_ref, ...), custom_call_target="tpu_custom_call" | custom-call | flops 5000000000 | bytes 15000000 | tf_op jit(solution)/shard_map/pallas_call | solution.py:182
  35.7 14.4 %all-to-all-start.1 = ((bf16[128,16,128]{2,1,0:T(8,128)(2,1)}), bf16[128,16,128]{2,1,0:T(8,128)(2,1)S(1)}, u32[]{:S(2)}, u32[]{:S(2)}) async-start(bf16[128,16,128]{2,1,0:T(8,128)(2,1)} %get-tuple-element.60), calls=%async_computation.1 | async-start | bytes 1048576 | tf_op jit(solution)/shard_map/all_to_all | solution.py:323
  50.2 1.8 %collective-permute-start.10 = (bf16[128,128]{1,0:T(8,128)(2,1)S(1)}, bf16[128,128]{1,0:T(8,128)(2,1)S(1)}, u32[]{:S(2)}, u32[]{:S(2)}) collective-permute-start(bf16[128,128]{1,0:T(8,128)(2,1)S(1)} %get-tuple-element.51), channel_id=1, source_target_pairs={{0,32},{2,34},{32,0},{34,2},{64,96},{66,98},{96,64},{98,66},{1,33}... | collective-permute-start | bytes 98312 | tf_op jit(solution)/shard_map/ppermute | solution.py:331
  52.8 1.1 %collective-permute-start.13 = (bf16[128,128]{1,0:T(8,128)(2,1)S(1)}, bf16[128,128]{1,0:T(8,128)(2,1)S(1)}, u32[]{:S(2)}, u32[]{:S(2)}) collective-permute-start(bf16[128,128]{1,0:T(8,128)(2,1)S(1)} %get-tuple-element.54), channel_id=1, source_target_pairs={{0,66},{2,64},{32,98},{34,96},{64,2},{66,0},{96,34},{98,32},{1,67}... | collective-permute-start | bytes 98312 | tf_op jit(solution)/shard_map/ppermute | solution.py:331
  54.0 1.4 %collective-permute-start.14 = (bf16[128,128]{1,0:T(8,128)(2,1)S(1)}, bf16[128,128]{1,0:T(8,128)(2,1)S(1)}, u32[]{:S(2)}, u32[]{:S(2)}) collective-permute-start(bf16[128,128]{1,0:T(8,128)(2,1)S(1)} %get-tuple-element.55), channel_id=1, source_target_pairs={{0,96},{2,98},{32,64},{34,66},{64,32},{66,34},{96,0},{98,2},{1,97}... | collective-permute-start | bytes 98312 | tf_op jit(solution)/shard_map/ppermute | solution.py:331
  55.3 1.1 %collective-permute-start.15 = (bf16[128,128]{1,0:T(8,128)(2,1)S(1)}, bf16[128,128]{1,0:T(8,128)(2,1)S(1)}, u32[]{:S(2)}, u32[]{:S(2)}) collective-permute-start(bf16[128,128]{1,0:T(8,128)(2,1)S(1)} %get-tuple-element.56), channel_id=1, source_target_pairs={{0,98},{2,96},{32,66},{34,64},{64,34},{66,32},{96,2},{98,0},{1,99}... | collective-permute-start | bytes 98312 | tf_op jit(solution)/shard_map/ppermute | solution.py:331
  57.0 2.1 %collective-permute-done.14.rest_6_ = bf16[128,128]{1,0:T(8,128)(2,1)S(1)} collective-permute-done((bf16[128,128]{1,0:T(8,128)(2,1)S(1)}, bf16[128,128]{1,0:T(8,128)(2,1)S(1)}, u32[]{:S(2)}, u32[]{:S(2)}) %collective-permute-start.14) | collective-permute-done | bytes 32800 | tf_op jit(solution)/shard_map/ppermute | solution.py:331
  59.1 1.3 %collective-permute-done.15.rest_7_ = bf16[128,128]{1,0:T(8,128)(2,1)S(1)} collective-permute-done((bf16[128,128]{1,0:T(8,128)(2,1)S(1)}, bf16[128,128]{1,0:T(8,128)(2,1)S(1)}, u32[]{:S(2)}, u32[]{:S(2)}) %collective-permute-start.15) | collective-permute-done | bytes 32800 | tf_op jit(solution)/shard_map/ppermute | solution.py:331
  60.4 1.1 %shard_map.86 = (f32[1024,128]{1,0:T(8,128)S(1)}, f32[1024,128]{1,0:T(8,128)S(1)}) custom-call(s32[4]{0:T(128)S(1)} %pad_add_fusion.me_ref, bf16[128,128]{1,0:T(8,128)(2,1)S(1)} %get-tuple-element.49.rest_0_, bf16[128,128]{1,0:T(8,128)(2,1)S(1)} %collective-permute-done.9.rest_1_, bf16[128,128]{1,0:T(8,128)(2,1)S(1)} %collective-permute-done.10.rest_2_, ...), custom_call_target="tpu_custom_call" | custom-call | flops 2000000000 | bytes 6000000 | tf_op jit(solution)/shard_map/pallas_call | solution.py:286
  61.5 7.3 %all-to-all-done.1.cols_ref = bf16[128,16,128]{2,1,0:T(8,128)(2,1)S(1)} async-done(((bf16[128,16,128]{2,1,0:T(8,128)(2,1)}), bf16[128,16,128]{2,1,0:T(8,128)(2,1)S(1)}, u32[]{:S(2)}, u32[]{:S(2)}) %all-to-all-start.1) | async-done | bytes 524320 | tf_op jit(solution)/shard_map/all_to_all | solution.py:323
  68.8 1.8 %shard_map.87 = (f32[128,8,128]{2,1,0:T(8,128)S(1)}, bf16[128,8,128]{2,1,0:T(8,128)(2,1)S(1)}) custom-call(s32[4]{0:T(128)S(1)} %pad_add_fusion.me_ref, bf16[128,16,128]{2,1,0:T(8,128)(2,1)S(1)} %all-to-all-done.1.cols_ref), custom_call_target="tpu_custom_call" | custom-call | flops 3000000000 | bytes 9000000 | tf_op jit(solution)/shard_map/pallas_call | solution.py:249
  70.7 1.5 %collective-permute-done.16 = bf16[128,8,128]{2,1,0:T(8,128)(2,1)S(1)} collective-permute-done((bf16[128,8,128]{2,1,0:T(8,128)(2,1)S(1)}, bf16[128,8,128]{2,1,0:T(8,128)(2,1)S(1)}, u32[]{:S(2)}, u32[]{:S(2)}) %collective-permute-start.16) | collective-permute-done | bytes 262176 | tf_op jit(solution)/shard_map/ppermute | solution.py:327
  72.2 21.5 %all_to_all.15.mixed_ref = bf16[128,8,128]{2,1,0:T(8,128)(2,1)S(1)} all-to-all(bf16[128,8,128]{2,1,0:T(8,128)(2,1)S(1)} %add_convert_fusion), channel_id=1, replica_groups=mesh['yh'=2,'yl'=2,'xl'=2,'z'=8,'core'=2,'xh'=2] {'yh','yl','xl','z','xh'}, dimensions={0} | all-to-all | bytes 524288 | tf_op jit(solution)/shard_map/all_to_all | solution.py:323
  93.8 1.6 %shard_map.88 = bf16[1024,128]{1,0:T(8,128)(2,1)} custom-call(bf16[128,8,128]{2,1,0:T(8,128)(2,1)S(1)} %all_to_all.15.mixed_ref, f32[1024,128]{1,0:T(8,128)S(1)} %get-tuple-element.63.gate_ref, f32[1024,128]{1,0:T(8,128)S(1)} %get-tuple-element.64.base_ref, bf16[128,128]{1,0:T(8,128)(2,1)S(1)} %copy-done.3), custom_call_target="tpu_custom_call" | custom-call | flops 2000000000 | bytes 6000000 | tf_op jit(solution)/shard_map/pallas_call | solution.py:313
  (39 shorter events, 4.6 us)
Async XLA Ops:
  2.3 13.6 %copy-start.1 = (bf16[512,128]{1,0:T(8,128)(2,1)S(1)}, bf16[512,128]{1,0:T(8,128)(2,1)}, u32[]{:S(2)}) copy-start(bf16[512,128]{1,0:T(8,128)(2,1)} %own_ref) | copy-start | bytes 393220
  2.3 15.7 %copy-start = (bf16[4,256,128]{2,1,0:T(8,128)(2,1)S(1)}, bf16[4,256,128]{2,1,0:T(8,128)(2,1)}, u32[]{:S(2)}) copy-start(bf16[4,256,128]{2,1,0:T(8,128)(2,1)} %couple_ref.1) | copy-start | bytes 786436
  2.4 15.7 %copy-start.5 = (bf16[4,128,256]{2,1,0:T(8,128)(2,1)S(1)}, bf16[4,128,256]{2,1,0:T(8,128)(2,1)}, u32[]{:S(2)}) copy-start(bf16[4,128,256]{2,1,0:T(8,128)(2,1)} %get-tuple-element.38.norm_ref) | copy-start | bytes 786436
  2.4 28.7 %all-to-all-start = ((bf16[16,128,128]{2,1,0:T(8,128)(2,1)}), bf16[16,128,128]{2,1,0:T(8,128)(2,1)S(1)}, u32[]{:S(2)}, u32[]{:S(2)}) async-start(bf16[16,128,128]{2,1,0:T(8,128)(2,1)} %get-tuple-element.37), calls=%async_computation | async-start | bytes 1048576 | tf_op jit(solution)/shard_map/all_to_all | solution.py:323
  12.8 5.2 %collective-permute-start = (bf16[16,256]{1,0:T(8,128)(2,1)S(1)}, bf16[16,256]{1,0:T(8,128)(2,1)S(1)}, u32[]{:S(2)}, u32[]{:S(2)}) collective-permute-start(bf16[16,256]{1,0:T(8,128)(2,1)S(1)} %bitcast.9), channel_id=1, source_target_pairs={{0,1},{1,0},{2,3},{3,2},{4,5},{5,4},{6,7},{7,6},{8,9},{9,8},{10,11... | collective-permute-start | bytes 24584 | tf_op jit(solution)/shard_map/ppermute | solution.py:327
  15.9 10.4 %collective-permute-start.8 = (bf16[512,128]{1,0:T(8,128)(2,1)S(1)}, bf16[512,128]{1,0:T(8,128)(2,1)S(1)}, u32[]{:S(2)}, u32[]{:S(2)}) collective-permute-start(bf16[512,128]{1,0:T(8,128)(2,1)S(1)} %copy-done.1), channel_id=1, source_target_pairs={{0,1},{1,0},{2,3},{3,2},{4,5},{5,4},{6,7},{7,6},{8,9},{9,8},{10,11... | collective-permute-start | bytes 393224 | tf_op jit(solution)/shard_map/ppermute | solution.py:327
  19.0 3.6 %collective-permute-start.1 = (bf16[256,128]{1,0:T(8,128)(2,1)S(1)}, bf16[256,128]{1,0:T(8,128)(2,1)S(1)}, u32[]{:S(2)}, u32[]{:S(2)}) collective-permute-start(bf16[256,128]{1,0:T(8,128)(2,1)S(1)} %get-tuple-element.41), channel_id=1, source_target_pairs={{0,2},{2,0},{32,34},{34,32},{64,66},{66,64},{96,98},{98,96},{1,3},... | collective-permute-start | bytes 196616 | tf_op jit(solution)/shard_map/ppermute | solution.py:331
  19.1 4.5 %collective-permute-start.2 = (bf16[256,128]{1,0:T(8,128)(2,1)S(1)}, bf16[256,128]{1,0:T(8,128)(2,1)S(1)}, u32[]{:S(2)}, u32[]{:S(2)}) collective-permute-start(bf16[256,128]{1,0:T(8,128)(2,1)S(1)} %get-tuple-element.42), channel_id=1, source_target_pairs={{0,32},{2,34},{32,0},{34,2},{64,96},{66,98},{96,64},{98,66},{1,33}... | collective-permute-start | bytes 196616 | tf_op jit(solution)/shard_map/ppermute | solution.py:331
  20.8 6.5 %collective-permute-start.3 = (bf16[256,128]{1,0:T(8,128)(2,1)S(1)}, bf16[256,128]{1,0:T(8,128)(2,1)S(1)}, u32[]{:S(2)}, u32[]{:S(2)}) collective-permute-start(bf16[256,128]{1,0:T(8,128)(2,1)S(1)} %get-tuple-element.43), channel_id=1, source_target_pairs={{0,34},{2,32},{32,2},{34,0},{64,98},{66,96},{96,66},{98,64},{1,35}... | collective-permute-start | bytes 196616 | tf_op jit(solution)/shard_map/ppermute | solution.py:331
  21.2 6.8 %collective-permute-start.4 = (bf16[256,128]{1,0:T(8,128)(2,1)S(1)}, bf16[256,128]{1,0:T(8,128)(2,1)S(1)}, u32[]{:S(2)}, u32[]{:S(2)}) collective-permute-start(bf16[256,128]{1,0:T(8,128)(2,1)S(1)} %get-tuple-element.44), channel_id=1, source_target_pairs={{0,64},{2,66},{32,96},{34,98},{64,0},{66,2},{96,32},{98,34},{1,65}... | collective-permute-start | bytes 196616 | tf_op jit(solution)/shard_map/ppermute | solution.py:331
  22.5 8.5 %collective-permute-start.5 = (bf16[256,128]{1,0:T(8,128)(2,1)S(1)}, bf16[256,128]{1,0:T(8,128)(2,1)S(1)}, u32[]{:S(2)}, u32[]{:S(2)}) collective-permute-start(bf16[256,128]{1,0:T(8,128)(2,1)S(1)} %get-tuple-element.45), channel_id=1, source_target_pairs={{0,66},{2,64},{32,98},{34,96},{64,2},{66,0},{96,34},{98,32},{1,67}... | collective-permute-start | bytes 196616 | tf_op jit(solution)/shard_map/ppermute | solution.py:331
  23.6 7.4 %collective-permute-start.6 = (bf16[256,128]{1,0:T(8,128)(2,1)S(1)}, bf16[256,128]{1,0:T(8,128)(2,1)S(1)}, u32[]{:S(2)}, u32[]{:S(2)}) collective-permute-start(bf16[256,128]{1,0:T(8,128)(2,1)S(1)} %get-tuple-element.46), channel_id=1, source_target_pairs={{0,96},{2,98},{32,64},{34,66},{64,32},{66,34},{96,0},{98,2},{1,97}... | collective-permute-start | bytes 196616 | tf_op jit(solution)/shard_map/ppermute | solution.py:331
  26.3 4.7 %collective-permute-start.7 = (bf16[256,128]{1,0:T(8,128)(2,1)S(1)}, bf16[256,128]{1,0:T(8,128)(2,1)S(1)}, u32[]{:S(2)}, u32[]{:S(2)}) collective-permute-start(bf16[256,128]{1,0:T(8,128)(2,1)S(1)} %get-tuple-element.47), channel_id=1, source_target_pairs={{0,98},{2,96},{32,66},{34,64},{64,34},{66,32},{96,2},{98,0},{1,99}... | collective-permute-start | bytes 196616 | tf_op jit(solution)/shard_map/ppermute | solution.py:331
  35.7 24.7 %copy-start.2 = (bf16[128,128]{1,0:T(8,128)(2,1)S(1)}, bf16[128,128]{1,0:T(8,128)(2,1)}, u32[]{:S(2)}) copy-start(bf16[128,128]{1,0:T(8,128)(2,1)} %rest_8_.1) | copy-start | bytes 98308
  35.7 33.1 %all-to-all-start.1 = ((bf16[128,16,128]{2,1,0:T(8,128)(2,1)}), bf16[128,16,128]{2,1,0:T(8,128)(2,1)S(1)}, u32[]{:S(2)}, u32[]{:S(2)}) async-start(bf16[128,16,128]{2,1,0:T(8,128)(2,1)} %get-tuple-element.60), calls=%async_computation.1 | async-start | bytes 1048576 | tf_op jit(solution)/shard_map/all_to_all | solution.py:323
  50.1 3.9 %collective-permute-start.9 = (bf16[128,128]{1,0:T(8,128)(2,1)S(1)}, bf16[128,128]{1,0:T(8,128)(2,1)S(1)}, u32[]{:S(2)}, u32[]{:S(2)}) collective-permute-start(bf16[128,128]{1,0:T(8,128)(2,1)S(1)} %get-tuple-element.50), channel_id=1, source_target_pairs={{0,2},{2,0},{32,34},{34,32},{64,66},{66,64},{96,98},{98,96},{1,3},... | collective-permute-start | bytes 98312 | tf_op jit(solution)/shard_map/ppermute | solution.py:331
  50.2 5.1 %collective-permute-start.10 = (bf16[128,128]{1,0:T(8,128)(2,1)S(1)}, bf16[128,128]{1,0:T(8,128)(2,1)S(1)}, u32[]{:S(2)}, u32[]{:S(2)}) collective-permute-start(bf16[128,128]{1,0:T(8,128)(2,1)S(1)} %get-tuple-element.51), channel_id=1, source_target_pairs={{0,32},{2,34},{32,0},{34,2},{64,96},{66,98},{96,64},{98,66},{1,33}... | collective-permute-start | bytes 98312 | tf_op jit(solution)/shard_map/ppermute | solution.py:331
  52.0 4.4 %collective-permute-start.11 = (bf16[128,128]{1,0:T(8,128)(2,1)S(1)}, bf16[128,128]{1,0:T(8,128)(2,1)S(1)}, u32[]{:S(2)}, u32[]{:S(2)}) collective-permute-start(bf16[128,128]{1,0:T(8,128)(2,1)S(1)} %get-tuple-element.52), channel_id=1, source_target_pairs={{0,34},{2,32},{32,2},{34,0},{64,98},{66,96},{96,66},{98,64},{1,35}... | collective-permute-start | bytes 98312 | tf_op jit(solution)/shard_map/ppermute | solution.py:331
  52.1 4.6 %collective-permute-start.12 = (bf16[128,128]{1,0:T(8,128)(2,1)S(1)}, bf16[128,128]{1,0:T(8,128)(2,1)S(1)}, u32[]{:S(2)}, u32[]{:S(2)}) collective-permute-start(bf16[128,128]{1,0:T(8,128)(2,1)S(1)} %get-tuple-element.53), channel_id=1, source_target_pairs={{0,64},{2,66},{32,96},{34,98},{64,0},{66,2},{96,32},{98,34},{1,65}... | collective-permute-start | bytes 98312 | tf_op jit(solution)/shard_map/ppermute | solution.py:331
  52.8 4.2 %collective-permute-start.13 = (bf16[128,128]{1,0:T(8,128)(2,1)S(1)}, bf16[128,128]{1,0:T(8,128)(2,1)S(1)}, u32[]{:S(2)}, u32[]{:S(2)}) collective-permute-start(bf16[128,128]{1,0:T(8,128)(2,1)S(1)} %get-tuple-element.54), channel_id=1, source_target_pairs={{0,66},{2,64},{32,98},{34,96},{64,2},{66,0},{96,34},{98,32},{1,67}... | collective-permute-start | bytes 98312 | tf_op jit(solution)/shard_map/ppermute | solution.py:331
  54.0 5.2 %collective-permute-start.14 = (bf16[128,128]{1,0:T(8,128)(2,1)S(1)}, bf16[128,128]{1,0:T(8,128)(2,1)S(1)}, u32[]{:S(2)}, u32[]{:S(2)}) collective-permute-start(bf16[128,128]{1,0:T(8,128)(2,1)S(1)} %get-tuple-element.55), channel_id=1, source_target_pairs={{0,96},{2,98},{32,64},{34,66},{64,32},{66,34},{96,0},{98,2},{1,97}... | collective-permute-start | bytes 98312 | tf_op jit(solution)/shard_map/ppermute | solution.py:331
  55.3 5.1 %collective-permute-start.15 = (bf16[128,128]{1,0:T(8,128)(2,1)S(1)}, bf16[128,128]{1,0:T(8,128)(2,1)S(1)}, u32[]{:S(2)}, u32[]{:S(2)}) collective-permute-start(bf16[128,128]{1,0:T(8,128)(2,1)S(1)} %get-tuple-element.56), channel_id=1, source_target_pairs={{0,98},{2,96},{32,66},{34,64},{64,34},{66,32},{96,2},{98,0},{1,99}... | collective-permute-start | bytes 98312 | tf_op jit(solution)/shard_map/ppermute | solution.py:331
  70.6 1.6 %collective-permute-start.16 = (bf16[128,8,128]{2,1,0:T(8,128)(2,1)S(1)}, bf16[128,8,128]{2,1,0:T(8,128)(2,1)S(1)}, u32[]{:S(2)}, u32[]{:S(2)}) collective-permute-start(bf16[128,8,128]{2,1,0:T(8,128)(2,1)S(1)} %get-tuple-element.62), channel_id=1, source_target_pairs={{0,2},{2,0},{1,3},{3,1},{4,6},{6,4},{5,7},{7,5},{8,10},{10,8},{9,1... | collective-permute-start | bytes 786440 | tf_op jit(solution)/shard_map/ppermute | solution.py:327
  72.2 21.6 %copy-start.3 = (bf16[128,128]{1,0:T(8,128)(2,1)S(1)}, bf16[128,128]{1,0:T(8,128)(2,1)}, u32[]{:S(2)}) copy-start(bf16[128,128]{1,0:T(8,128)(2,1)} %w_ref.1) | copy-start | bytes 98308
  (2 other events, 14.6 us)

commit v7 on v6

--- a/solution.py
+++ b/solution.py
@@ -101,7 +101,7 @@
 
 def packs(me, normed, own_t, other_t, couple):
     return on_core(
-        pack_kernel, (jax.ShapeDtypeStruct((256, 128), BF16),) * 8, 5, scalars=1, cost=cost(1)
+        pack_kernel, (jax.ShapeDtypeStruct((256, 128), BF16),) * 8, 5, scalars=1, cost=cost(5)
     )(me, normed, own_t, other_t, couple)
 
 
@@ -125,7 +125,7 @@
         3,
         [pltpu.VMEM((1024, 128), F32)],
         scalars=1,
-        cost=cost(1),
+        cost=cost(5),
     )(me, own, other)
 
 
@@ -328,8 +328,8 @@
 
 
 def to_peers(pieces):
-    sent = [lax.ppermute(pieces[m], PLANE, [(i, i ^ m) for i in range(8)]) for m in range(1, 8)]
-    return [pieces[0], *sent]
+    sent = {m: lax.ppermute(pieces[m], PLANE, [(i, i ^ m) for i in range(8)]) for m in (7, 6, 5, 3, 4, 2, 1)}
+    return [pieces[0], *(sent[m] for m in range(1, 8))]
 
 
 def per_device(msa, couple, first, second, w_out, entry, w_gate, w_final):
@@ -338,7 +338,8 @@
         [at["yl"] * 4 + at["xl"] * 2 + at["core"], at["xh"], at["core"], (at["yh"] == at["xh"]).astype(jnp.int32)]
     ).astype(jnp.int32)
     right, normed = firsts(msa, second.T)
-    first_t, w_out, right, normed = lax.optimization_barrier((first.T, w_out, right, normed))
+    first_t = first.T
+    w_out, right = lax.optimization_barrier((w_out, right))
     right = exchanged(right, ("yh", "z"))
     first_other = partner(first_t, "xh")
     w_other = partner(w_out, "xh")

time: 95.8 us -> 95.8 us (level)
  starting transfers between devices: 41.4 us -> 39.3 us
  waiting for transfers between devices: 18.7 us -> 20.1 us
    all_to_all x2, starting transfers between devices: 24.8 us -> 22.7 us  [exchanged(): return lax.all_to_all(x, axes, split_axis=0, concat_axis=0, tiled=True)]
    ppermute x3, waiting for transfers between devices: 3.07 us -> 1.53 us  [partner(): return lax.ppermute(x, axis, [(0, 1), (1, 0)])]
    ppermute x14, waiting for transfers between devices: 8.36 us -> 9.86 us  [to_peers(): lax.ppermute(pieces[m], PLANE, [(i, i ^ m) for i in range(8)])]
    all_to_all x2, waiting for transfers between devices: 7.28 us -> 8.69 us  [exchanged(): return lax.all_to_all(x, axes, split_axis=0, concat_axis=0, tiled=True)]
  transfers between devices with their start and end apart: 19 -> 19, of which waited for: 10 -> 10; matrix products, arithmetic and copies ran while one was open for 0% -> 0% of each run, Pallas kernels for 3% -> 5%
where the time goes in v7:
time: 95.8 us; the launch traced here: 95.3 us
  starting transfers between devices  39.3 us (41%)
  blocking collectives  21.6 us (23%)
  waiting for transfers between devices  20.1 us (21%)
  Pallas kernels  13.3 us (14%)
    all_to_all x2, starting transfers between devices, exchanged(): return lax.all_to_all(x, axes, split_axis=0, concat_axis=0, tiled=True)  22.7 us
    all_to_all x1, blocking collectives, exchanged(): return lax.all_to_all(x, axes, split_axis=0, concat_axis=0, tiled=True)  21.6 us
    ppermute x14, starting transfers between devices, to_peers(): lax.ppermute(pieces[m], PLANE, [(i, i ^ m) for i in range(8)])  12.9 us
    ppermute x14, waiting for transfers between devices, to_peers(): lax.ppermute(pieces[m], PLANE, [(i, i ^ m) for i in range(8)])  9.86 us
    all_to_all x2, waiting for transfers between devices, exchanged(): return lax.all_to_all(x, axes, split_axis=0, concat_axis=0, tiled=True)  8.69 us
    pallas_call x1, Pallas kernels, pairs(): on_core(pair_kernel, (jax.ShapeDtypeStruct((128, 128), BF16),) * 8 + (jax...  4.7 us
    ppermute x3, starting transfers between devices, partner(): return lax.ppermute(x, axis, [(0, 1), (1, 0)])  3.71 us
    pallas_call x1, Pallas kernels, firsts(): pl.pallas_call(first_kernel, out_shape=(jax.ShapeDtypeStruct((16, 128, 12...  2.31 us
  transfers between devices with their start and end apart: 19, of which 10 were waited for; matrix products, arithmetic and copies ran while one was open for 0% of the time, Pallas kernels for 5%

profile of v7, /device:TPU:8, one launch (start us, length us, event | category | flops | bytes accessed | tf_op | source)
XLA Modules:
  0.0 95.3 jit_solution(14694458676657752872)
XLA Ops:
  0.0 3.0 %collective-permute-start = (bf16[16,256]{1,0:T(8,128)(2,1)}, bf16[16,256]{1,0:T(8,128)(2,1)S(1)}, u32[]{:S(2)}, u32[]{:S(2)}) collective-permute-start(bf16[16,256]{1,0:T(8,128)(2,1)} %bitcast.9), channel_id=1, source_target_pairs={{0,1},{1,0},{2,3},{3,2},{4,5},{5,4},{6,7},{7,6},{8,9},{9,8},{10,11... | collective-permute-start | bytes 24584 | tf_op jit(solution)/shard_map/ppermute | solution.py:327
  3.0 2.3 %shard_map.82 = (bf16[16,128,128]{2,1,0:T(8,128)(2,1)}, bf16[4,128,256]{2,1,0:T(8,128)(2,1)}) custom-call(bf16[128,4,256]{2,1,0:T(4,128)(2,1)} %msa_hbm.1, bf16[32,256]{1,0:T(8,128)(2,1)} %bitcast.11), custom_call_target="tpu_custom_call" | custom-call | flops 1000000000 | bytes 3000000 | tf_op jit(solution)/shard_map/pallas_call | solution.py:63
  5.4 10.4 %all-to-all-start = ((bf16[16,128,128]{2,1,0:T(8,128)(2,1)}), bf16[16,128,128]{2,1,0:T(8,128)(2,1)S(1)}, u32[]{:S(2)}, u32[]{:S(2)}) async-start(bf16[16,128,128]{2,1,0:T(8,128)(2,1)} %get-tuple-element.34), calls=%async_computation | async-start | bytes 1048576 | tf_op jit(solution)/shard_map/all_to_all | solution.py:323
  17.1 0.9 shard_map.83
  18.1 1.6 %collective-permute-start.2 = (bf16[256,128]{1,0:T(8,128)(2,1)S(1)}, bf16[256,128]{1,0:T(8,128)(2,1)S(1)}, u32[]{:S(2)}, u32[]{:S(2)}) collective-permute-start(bf16[256,128]{1,0:T(8,128)(2,1)S(1)} %get-tuple-element.38), channel_id=1, source_target_pairs={{0,32},{2,34},{32,0},{34,2},{64,96},{66,98},{96,64},{98,66},{1,33}... | collective-permute-start | bytes 196616 | tf_op jit(solution)/shard_map/ppermute | solution.py:331
  20.2 1.4 %collective-permute-start.4 = (bf16[256,128]{1,0:T(8,128)(2,1)S(1)}, bf16[256,128]{1,0:T(8,128)(2,1)S(1)}, u32[]{:S(2)}, u32[]{:S(2)}) collective-permute-start(bf16[256,128]{1,0:T(8,128)(2,1)S(1)} %get-tuple-element.40), channel_id=1, source_target_pairs={{0,64},{2,66},{32,96},{34,98},{64,0},{66,2},{96,32},{98,34},{1,65}... | collective-permute-start | bytes 196616 | tf_op jit(solution)/shard_map/ppermute | solution.py:331
  22.6 2.7 %collective-permute-start.6 = (bf16[256,128]{1,0:T(8,128)(2,1)S(1)}, bf16[256,128]{1,0:T(8,128)(2,1)S(1)}, u32[]{:S(2)}, u32[]{:S(2)}) collective-permute-start(bf16[256,128]{1,0:T(8,128)(2,1)S(1)} %get-tuple-element.42), channel_id=1, source_target_pairs={{0,96},{2,98},{32,64},{34,66},{64,32},{66,34},{96,0},{98,2},{1,97}... | collective-permute-start | bytes 196616 | tf_op jit(solution)/shard_map/ppermute | solution.py:331
  25.4 1.0 %shard_map.84.rest_8_ = bf16[2048,256]{1,0:T(8,128)(2,1)S(1)} custom-call(s32[4]{0:T(128)S(1)} %pad_add_fusion.me_ref, bf16[512,128]{1,0:T(8,128)(2,1)S(1)} %copy-done.1, bf16[512,128]{1,0:T(8,128)(2,1)S(1)} %collective-permute-done.8.other_ref), custom_call_target="tpu_custom_call" | custom-call | flops 5000000000 | bytes 15000000 | tf_op jit(solution)/shard_map/pallas_call | solution.py:122
  27.2 4.4 %collective-permute-done.5.rest_5_ = bf16[256,128]{1,0:T(8,128)(2,1)S(1)} collective-permute-done((bf16[256,128]{1,0:T(8,128)(2,1)S(1)}, bf16[256,128]{1,0:T(8,128)(2,1)S(1)}, u32[]{:S(2)}, u32[]{:S(2)}) %collective-permute-start.5) | collective-permute-done | bytes 65568 | tf_op jit(solution)/shard_map/ppermute | solution.py:331
  31.6 1.0 %all-to-all-done.right_ref = bf16[16,128,128]{2,1,0:T(8,128)(2,1)S(1)} async-done(((bf16[16,128,128]{2,1,0:T(8,128)(2,1)}), bf16[16,128,128]{2,1,0:T(8,128)(2,1)S(1)}, u32[]{:S(2)}, u32[]{:S(2)}) %all-to-all-start) | async-done | bytes 524320 | tf_op jit(solution)/shard_map/all_to_all | solution.py:323
  32.6 4.7 %shard_map.85 = (bf16[128,128]{1,0:T(8,128)(2,1)S(1)}, bf16[128,128]{1,0:T(8,128)(2,1)S(1)}, bf16[128,128]{1,0:T(8,128)(2,1)S(1)}, bf16[128,128]{1,0:T(8,128)(2,...) custom-call(s32[4]{0:T(128)S(1)} %pad_add_fusion.me_ref, ...), custom_call_target="tpu_custom_call" | custom-call | flops 5000000000 | bytes 15000000 | tf_op jit(solution)/shard_map/pallas_call | solution.py:182
  37.3 12.3 %all-to-all-start.1 = ((bf16[128,16,128]{2,1,0:T(8,128)(2,1)}), bf16[128,16,128]{2,1,0:T(8,128)(2,1)S(1)}, u32[]{:S(2)}, u32[]{:S(2)}) async-start(bf16[128,16,128]{2,1,0:T(8,128)(2,1)} %get-tuple-element.56), calls=%async_computation.1 | async-start | bytes 1048576 | tf_op jit(solution)/shard_map/all_to_all | solution.py:323
  49.7 1.8 %collective-permute-start.10 = (bf16[128,128]{1,0:T(8,128)(2,1)S(1)}, bf16[128,128]{1,0:T(8,128)(2,1)S(1)}, u32[]{:S(2)}, u32[]{:S(2)}) collective-permute-start(bf16[128,128]{1,0:T(8,128)(2,1)S(1)} %get-tuple-element.47), channel_id=1, source_target_pairs={{0,32},{2,34},{32,0},{34,2},{64,96},{66,98},{96,64},{98,66},{1,33}... | collective-permute-start | bytes 98312 | tf_op jit(solution)/shard_map/ppermute | solution.py:331
  52.4 1.1 %collective-permute-start.13 = (bf16[128,128]{1,0:T(8,128)(2,1)S(1)}, bf16[128,128]{1,0:T(8,128)(2,1)S(1)}, u32[]{:S(2)}, u32[]{:S(2)}) collective-permute-start(bf16[128,128]{1,0:T(8,128)(2,1)S(1)} %get-tuple-element.50), channel_id=1, source_target_pairs={{0,66},{2,64},{32,98},{34,96},{64,2},{66,0},{96,34},{98,32},{1,67}... | collective-permute-start | bytes 98312 | tf_op jit(solution)/shard_map/ppermute | solution.py:331
  53.5 1.4 %collective-permute-start.14 = (bf16[128,128]{1,0:T(8,128)(2,1)S(1)}, bf16[128,128]{1,0:T(8,128)(2,1)S(1)}, u32[]{:S(2)}, u32[]{:S(2)}) collective-permute-start(bf16[128,128]{1,0:T(8,128)(2,1)S(1)} %get-tuple-element.51), channel_id=1, source_target_pairs={{0,96},{2,98},{32,64},{34,66},{64,32},{66,34},{96,0},{98,2},{1,97}... | collective-permute-start | bytes 98312 | tf_op jit(solution)/shard_map/ppermute | solution.py:331
  54.9 1.1 %collective-permute-start.15 = (bf16[128,128]{1,0:T(8,128)(2,1)S(1)}, bf16[128,128]{1,0:T(8,128)(2,1)S(1)}, u32[]{:S(2)}, u32[]{:S(2)}) collective-permute-start(bf16[128,128]{1,0:T(8,128)(2,1)S(1)} %get-tuple-element.52), channel_id=1, source_target_pairs={{0,98},{2,96},{32,66},{34,64},{64,34},{66,32},{96,2},{98,0},{1,99}... | collective-permute-start | bytes 98312 | tf_op jit(solution)/shard_map/ppermute | solution.py:331
  56.8 2.0 %collective-permute-done.14.rest_6_ = bf16[128,128]{1,0:T(8,128)(2,1)S(1)} collective-permute-done((bf16[128,128]{1,0:T(8,128)(2,1)S(1)}, bf16[128,128]{1,0:T(8,128)(2,1)S(1)}, u32[]{:S(2)}, u32[]{:S(2)}) %collective-permute-start.14) | collective-permute-done | bytes 32800 | tf_op jit(solution)/shard_map/ppermute | solution.py:331
  58.8 1.1 %collective-permute-done.15.rest_7_ = bf16[128,128]{1,0:T(8,128)(2,1)S(1)} collective-permute-done((bf16[128,128]{1,0:T(8,128)(2,1)S(1)}, bf16[128,128]{1,0:T(8,128)(2,1)S(1)}, u32[]{:S(2)}, u32[]{:S(2)}) %collective-permute-start.15) | collective-permute-done | bytes 32800 | tf_op jit(solution)/shard_map/ppermute | solution.py:331
  59.9 1.1 %shard_map.86 = (f32[1024,128]{1,0:T(8,128)S(1)}, f32[1024,128]{1,0:T(8,128)S(1)}) custom-call(s32[4]{0:T(128)S(1)} %pad_add_fusion.me_ref, bf16[128,128]{1,0:T(8,128)(2,1)S(1)} %get-tuple-element.45.rest_0_, bf16[128,128]{1,0:T(8,128)(2,1)S(1)} %collective-permute-done.9.rest_1_, bf16[128,128]{1,0:T(8,128)(2,1)S(1)} %collective-permute-done.10.rest_2_, ...), custom_call_target="tpu_custom_call" | custom-call | flops 2000000000 | bytes 6000000 | tf_op jit(solution)/shard_map/pallas_call | solution.py:286
  61.0 7.7 %all-to-all-done.1.cols_ref = bf16[128,16,128]{2,1,0:T(8,128)(2,1)S(1)} async-done(((bf16[128,16,128]{2,1,0:T(8,128)(2,1)}), bf16[128,16,128]{2,1,0:T(8,128)(2,1)S(1)}, u32[]{:S(2)}, u32[]{:S(2)}) %all-to-all-start.1) | async-done | bytes 524320 | tf_op jit(solution)/shard_map/all_to_all | solution.py:323
  68.7 1.8 %shard_map.87 = (f32[128,8,128]{2,1,0:T(8,128)S(1)}, bf16[128,8,128]{2,1,0:T(8,128)(2,1)S(1)}) custom-call(s32[4]{0:T(128)S(1)} %pad_add_fusion.me_ref, bf16[128,16,128]{2,1,0:T(8,128)(2,1)S(1)} %all-to-all-done.1.cols_ref), custom_call_target="tpu_custom_call" | custom-call | flops 3000000000 | bytes 9000000 | tf_op jit(solution)/shard_map/pallas_call | solution.py:249
  70.6 1.5 %collective-permute-done.16 = bf16[128,8,128]{2,1,0:T(8,128)(2,1)S(1)} collective-permute-done((bf16[128,8,128]{2,1,0:T(8,128)(2,1)S(1)}, bf16[128,8,128]{2,1,0:T(8,128)(2,1)S(1)}, u32[]{:S(2)}, u32[]{:S(2)}) %collective-permute-start.16) | collective-permute-done | bytes 262176 | tf_op jit(solution)/shard_map/ppermute | solution.py:327
  72.1 21.6 %all_to_all.15.mixed_ref = bf16[128,8,128]{2,1,0:T(8,128)(2,1)S(1)} all-to-all(bf16[128,8,128]{2,1,0:T(8,128)(2,1)S(1)} %add_convert_fusion), channel_id=1, replica_groups=mesh['yh'=2,'yl'=2,'xl'=2,'z'=8,'core'=2,'xh'=2] {'yh','yl','xl','z','xh'}, dimensions={0} | all-to-all | bytes 524288 | tf_op jit(solution)/shard_map/all_to_all | solution.py:323
  93.7 1.6 %shard_map.88 = bf16[1024,128]{1,0:T(8,128)(2,1)} custom-call(bf16[128,8,128]{2,1,0:T(8,128)(2,1)S(1)} %all_to_all.15.mixed_ref, f32[1024,128]{1,0:T(8,128)S(1)} %get-tuple-element.59.gate_ref, f32[1024,128]{1,0:T(8,128)S(1)} %get-tuple-element.60.base_ref, bf16[128,128]{1,0:T(8,128)(2,1)S(1)} %copy-done.3), custom_call_target="tpu_custom_call" | custom-call | flops 2000000000 | bytes 6000000 | tf_op jit(solution)/shard_map/pallas_call | solution.py:313
  (39 shorter events, 5.7 us)
Async XLA Ops:
  0.0 16.5 %collective-permute-start = (bf16[16,256]{1,0:T(8,128)(2,1)}, bf16[16,256]{1,0:T(8,128)(2,1)S(1)}, u32[]{:S(2)}, u32[]{:S(2)}) collective-permute-start(bf16[16,256]{1,0:T(8,128)(2,1)} %bitcast.9), channel_id=1, source_target_pairs={{0,1},{1,0},{2,3},{3,2},{4,5},{5,4},{6,7},{7,6},{8,9},{9,8},{10,11... | collective-permute-start | bytes 24584 | tf_op jit(solution)/shard_map/ppermute | solution.py:327
  5.3 10.5 %copy-start.1 = (bf16[512,128]{1,0:T(8,128)(2,1)S(1)}, bf16[512,128]{1,0:T(8,128)(2,1)}, u32[]{:S(2)}) copy-start(bf16[512,128]{1,0:T(8,128)(2,1)} %own_ref) | copy-start | bytes 393220
  5.4 11.2 %copy-start = (bf16[4,256,128]{2,1,0:T(8,128)(2,1)S(1)}, bf16[4,256,128]{2,1,0:T(8,128)(2,1)}, u32[]{:S(2)}) copy-start(bf16[4,256,128]{2,1,0:T(8,128)(2,1)} %couple_ref.1) | copy-start | bytes 786436
  5.4 11.2 %copy-start.5 = (bf16[4,128,256]{2,1,0:T(8,128)(2,1)S(1)}, bf16[4,128,256]{2,1,0:T(8,128)(2,1)}, u32[]{:S(2)}) copy-start(bf16[4,128,256]{2,1,0:T(8,128)(2,1)} %get-tuple-element.35.norm_ref) | copy-start | bytes 786436
  5.4 27.2 %all-to-all-start = ((bf16[16,128,128]{2,1,0:T(8,128)(2,1)}), bf16[16,128,128]{2,1,0:T(8,128)(2,1)S(1)}, u32[]{:S(2)}, u32[]{:S(2)}) async-start(bf16[16,128,128]{2,1,0:T(8,128)(2,1)} %get-tuple-element.34), calls=%async_computation | async-start | bytes 1048576 | tf_op jit(solution)/shard_map/all_to_all | solution.py:323
  15.8 9.5 %collective-permute-start.8 = (bf16[512,128]{1,0:T(8,128)(2,1)S(1)}, bf16[512,128]{1,0:T(8,128)(2,1)S(1)}, u32[]{:S(2)}, u32[]{:S(2)}) collective-permute-start(bf16[512,128]{1,0:T(8,128)(2,1)S(1)} %copy-done.1), channel_id=1, source_target_pairs={{0,1},{1,0},{2,3},{3,2},{4,5},{5,4},{6,7},{7,6},{8,9},{9,8},{10,11... | collective-permute-start | bytes 393224 | tf_op jit(solution)/shard_map/ppermute | solution.py:327
  18.0 3.6 %collective-permute-start.1 = (bf16[256,128]{1,0:T(8,128)(2,1)S(1)}, bf16[256,128]{1,0:T(8,128)(2,1)S(1)}, u32[]{:S(2)}, u32[]{:S(2)}) collective-permute-start(bf16[256,128]{1,0:T(8,128)(2,1)S(1)} %get-tuple-element.37), channel_id=1, source_target_pairs={{0,2},{2,0},{32,34},{34,32},{64,66},{66,64},{96,98},{98,96},{1,3},... | collective-permute-start | bytes 196616 | tf_op jit(solution)/shard_map/ppermute | solution.py:331
  18.1 4.5 %collective-permute-start.2 = (bf16[256,128]{1,0:T(8,128)(2,1)S(1)}, bf16[256,128]{1,0:T(8,128)(2,1)S(1)}, u32[]{:S(2)}, u32[]{:S(2)}) collective-permute-start(bf16[256,128]{1,0:T(8,128)(2,1)S(1)} %get-tuple-element.38), channel_id=1, source_target_pairs={{0,32},{2,34},{32,0},{34,2},{64,96},{66,98},{96,64},{98,66},{1,33}... | collective-permute-start | bytes 196616 | tf_op jit(solution)/shard_map/ppermute | solution.py:331
  19.8 6.5 %collective-permute-start.3 = (bf16[256,128]{1,0:T(8,128)(2,1)S(1)}, bf16[256,128]{1,0:T(8,128)(2,1)S(1)}, u32[]{:S(2)}, u32[]{:S(2)}) collective-permute-start(bf16[256,128]{1,0:T(8,128)(2,1)S(1)} %get-tuple-element.39), channel_id=1, source_target_pairs={{0,34},{2,32},{32,2},{34,0},{64,98},{66,96},{96,66},{98,64},{1,35}... | collective-permute-start | bytes 196616 | tf_op jit(solution)/shard_map/ppermute | solution.py:331
  20.2 7.0 %collective-permute-start.4 = (bf16[256,128]{1,0:T(8,128)(2,1)S(1)}, bf16[256,128]{1,0:T(8,128)(2,1)S(1)}, u32[]{:S(2)}, u32[]{:S(2)}) collective-permute-start(bf16[256,128]{1,0:T(8,128)(2,1)S(1)} %get-tuple-element.40), channel_id=1, source_target_pairs={{0,64},{2,66},{32,96},{34,98},{64,0},{66,2},{96,32},{98,34},{1,65}... | collective-permute-start | bytes 196616 | tf_op jit(solution)/shard_map/ppermute | solution.py:331
  21.6 10.0 %collective-permute-start.5 = (bf16[256,128]{1,0:T(8,128)(2,1)S(1)}, bf16[256,128]{1,0:T(8,128)(2,1)S(1)}, u32[]{:S(2)}, u32[]{:S(2)}) collective-permute-start(bf16[256,128]{1,0:T(8,128)(2,1)S(1)} %get-tuple-element.41), channel_id=1, source_target_pairs={{0,66},{2,64},{32,98},{34,96},{64,2},{66,0},{96,34},{98,32},{1,67}... | collective-permute-start | bytes 196616 | tf_op jit(solution)/shard_map/ppermute | solution.py:331
  22.6 9.0 %collective-permute-start.6 = (bf16[256,128]{1,0:T(8,128)(2,1)S(1)}, bf16[256,128]{1,0:T(8,128)(2,1)S(1)}, u32[]{:S(2)}, u32[]{:S(2)}) collective-permute-start(bf16[256,128]{1,0:T(8,128)(2,1)S(1)} %get-tuple-element.42), channel_id=1, source_target_pairs={{0,96},{2,98},{32,64},{34,66},{64,32},{66,34},{96,0},{98,2},{1,97}... | collective-permute-start | bytes 196616 | tf_op jit(solution)/shard_map/ppermute | solution.py:331
  25.4 6.2 %collective-permute-start.7 = (bf16[256,128]{1,0:T(8,128)(2,1)S(1)}, bf16[256,128]{1,0:T(8,128)(2,1)S(1)}, u32[]{:S(2)}, u32[]{:S(2)}) collective-permute-start(bf16[256,128]{1,0:T(8,128)(2,1)S(1)} %get-tuple-element.43), channel_id=1, source_target_pairs={{0,98},{2,96},{32,66},{34,64},{64,34},{66,32},{96,2},{98,0},{1,99}... | collective-permute-start | bytes 196616 | tf_op jit(solution)/shard_map/ppermute | solution.py:331
  37.3 22.6 %copy-start.2 = (bf16[128,128]{1,0:T(8,128)(2,1)S(1)}, bf16[128,128]{1,0:T(8,128)(2,1)}, u32[]{:S(2)}) copy-start(bf16[128,128]{1,0:T(8,128)(2,1)} %rest_8_.1) | copy-start | bytes 98308
  37.3 31.4 %all-to-all-start.1 = ((bf16[128,16,128]{2,1,0:T(8,128)(2,1)}), bf16[128,16,128]{2,1,0:T(8,128)(2,1)S(1)}, u32[]{:S(2)}, u32[]{:S(2)}) async-start(bf16[128,16,128]{2,1,0:T(8,128)(2,1)} %get-tuple-element.56), calls=%async_computation.1 | async-start | bytes 1048576 | tf_op jit(solution)/shard_map/all_to_all | solution.py:323
  49.6 3.9 %collective-permute-start.9 = (bf16[128,128]{1,0:T(8,128)(2,1)S(1)}, bf16[128,128]{1,0:T(8,128)(2,1)S(1)}, u32[]{:S(2)}, u32[]{:S(2)}) collective-permute-start(bf16[128,128]{1,0:T(8,128)(2,1)S(1)} %get-tuple-element.46), channel_id=1, source_target_pairs={{0,2},{2,0},{32,34},{34,32},{64,66},{66,64},{96,98},{98,96},{1,3},... | collective-permute-start | bytes 98312 | tf_op jit(solution)/shard_map/ppermute | solution.py:331
  49.7 5.1 %collective-permute-start.10 = (bf16[128,128]{1,0:T(8,128)(2,1)S(1)}, bf16[128,128]{1,0:T(8,128)(2,1)S(1)}, u32[]{:S(2)}, u32[]{:S(2)}) collective-permute-start(bf16[128,128]{1,0:T(8,128)(2,1)S(1)} %get-tuple-element.47), channel_id=1, source_target_pairs={{0,32},{2,34},{32,0},{34,2},{64,96},{66,98},{96,64},{98,66},{1,33}... | collective-permute-start | bytes 98312 | tf_op jit(solution)/shard_map/ppermute | solution.py:331
  51.6 4.4 %collective-permute-start.11 = (bf16[128,128]{1,0:T(8,128)(2,1)S(1)}, bf16[128,128]{1,0:T(8,128)(2,1)S(1)}, u32[]{:S(2)}, u32[]{:S(2)}) collective-permute-start(bf16[128,128]{1,0:T(8,128)(2,1)S(1)} %get-tuple-element.48), channel_id=1, source_target_pairs={{0,34},{2,32},{32,2},{34,0},{64,98},{66,96},{96,66},{98,64},{1,35}... | collective-permute-start | bytes 98312 | tf_op jit(solution)/shard_map/ppermute | solution.py:331
  51.6 4.7 %collective-permute-start.12 = (bf16[128,128]{1,0:T(8,128)(2,1)S(1)}, bf16[128,128]{1,0:T(8,128)(2,1)S(1)}, u32[]{:S(2)}, u32[]{:S(2)}) collective-permute-start(bf16[128,128]{1,0:T(8,128)(2,1)S(1)} %get-tuple-element.49), channel_id=1, source_target_pairs={{0,64},{2,66},{32,96},{34,98},{64,0},{66,2},{96,32},{98,34},{1,65}... | collective-permute-start | bytes 98312 | tf_op jit(solution)/shard_map/ppermute | solution.py:331
  52.4 4.4 %collective-permute-start.13 = (bf16[128,128]{1,0:T(8,128)(2,1)S(1)}, bf16[128,128]{1,0:T(8,128)(2,1)S(1)}, u32[]{:S(2)}, u32[]{:S(2)}) collective-permute-start(bf16[128,128]{1,0:T(8,128)(2,1)S(1)} %get-tuple-element.50), channel_id=1, source_target_pairs={{0,66},{2,64},{32,98},{34,96},{64,2},{66,0},{96,34},{98,32},{1,67}... | collective-permute-start | bytes 98312 | tf_op jit(solution)/shard_map/ppermute | solution.py:331
  53.5 5.3 %collective-permute-start.14 = (bf16[128,128]{1,0:T(8,128)(2,1)S(1)}, bf16[128,128]{1,0:T(8,128)(2,1)S(1)}, u32[]{:S(2)}, u32[]{:S(2)}) collective-permute-start(bf16[128,128]{1,0:T(8,128)(2,1)S(1)} %get-tuple-element.51), channel_id=1, source_target_pairs={{0,96},{2,98},{32,64},{34,66},{64,32},{66,34},{96,0},{98,2},{1,97}... | collective-permute-start | bytes 98312 | tf_op jit(solution)/shard_map/ppermute | solution.py:331
  54.9 5.0 %collective-permute-start.15 = (bf16[128,128]{1,0:T(8,128)(2,1)S(1)}, bf16[128,128]{1,0:T(8,128)(2,1)S(1)}, u32[]{:S(2)}, u32[]{:S(2)}) collective-permute-start(bf16[128,128]{1,0:T(8,128)(2,1)S(1)} %get-tuple-element.52), channel_id=1, source_target_pairs={{0,98},{2,96},{32,66},{34,64},{64,34},{66,32},{96,2},{98,0},{1,99}... | collective-permute-start | bytes 98312 | tf_op jit(solution)/shard_map/ppermute | solution.py:331
  70.5 1.6 %collective-permute-start.16 = (bf16[128,8,128]{2,1,0:T(8,128)(2,1)S(1)}, bf16[128,8,128]{2,1,0:T(8,128)(2,1)S(1)}, u32[]{:S(2)}, u32[]{:S(2)}) collective-permute-start(bf16[128,8,128]{2,1,0:T(8,128)(2,1)S(1)} %get-tuple-element.58), channel_id=1, source_target_pairs={{0,2},{2,0},{1,3},{3,1},{4,6},{6,4},{5,7},{7,5},{8,10},{10,8},{9,1... | collective-permute-start | bytes 786440 | tf_op jit(solution)/shard_map/ppermute | solution.py:327
  72.1 21.6 %copy-start.3 = (bf16[128,128]{1,0:T(8,128)(2,1)S(1)}, bf16[128,128]{1,0:T(8,128)(2,1)}, u32[]{:S(2)}) copy-start(bf16[128,128]{1,0:T(8,128)(2,1)} %w_ref.1) | copy-start | bytes 98308
  (2 other events, 3.3 us)

commit v8 on v7

--- a/solution.py
+++ b/solution.py
@@ -141,16 +141,16 @@
             ].astype(F32)
     lefts = jnp.concatenate([packed_refs[m][128:256, :] for m in range(8)], axis=0)
     low = lax.broadcasted_iota(jnp.int32, (32, 128), 1) < 64
-    for part in range(4):
-        rows = rows_scr[part * 256 : (part + 1) * 256, :].astype(BF16)
+    for part in range(2):
+        rows = rows_scr[part * 512 : (part + 1) * 512, :].astype(BF16)
         outer = dot(rows, lefts, ((1,), (1,)))
-        for e in range(4):
+        for e in range(8):
             for m in range(8):
                 lanes = slice(m * 128, (m + 1) * 128)
                 a = outer[e * 64 : e * 64 + 32, lanes]
                 b = outer[e * 64 + 32 : e * 64 + 64, lanes]
                 rows = slice(m * 32, (m + 1) * 32)
-                at = slice((part * 4 + e) * 128, (part * 4 + e + 1) * 128)
+                at = slice((part * 8 + e) * 128, (part * 8 + e + 1) * 128)
                 lhs_scr[0, rows, at] = jnp.where(low, a, pltpu.roll(b, 64, 1)).astype(BF16)
                 lhs_scr[1, rows, at] = jnp.where(low, pltpu.roll(a, 64, 1), b).astype(BF16)
     for half in range(2):

time: 95.8 us -> 95.8 us (level)
  no operation moved by 1% of the time
where the time goes in v8:
time: 95.8 us; the launch traced here: 95.4 us
  starting transfers between devices  39.3 us (41%)
  blocking collectives  21.6 us (23%)
  waiting for transfers between devices  20.1 us (21%)
  Pallas kernels  13.3 us (14%)
    all_to_all x2, starting transfers between devices, exchanged(): return lax.all_to_all(x, axes, split_axis=0, concat_axis=0, tiled=True)  22.7 us
    all_to_all x1, blocking collectives, exchanged(): return lax.all_to_all(x, axes, split_axis=0, concat_axis=0, tiled=True)  21.6 us
    ppermute x14, starting transfers between devices, to_peers(): lax.ppermute(pieces[m], PLANE, [(i, i ^ m) for i in range(8)])  12.9 us
    ppermute x14, waiting for transfers between devices, to_peers(): lax.ppermute(pieces[m], PLANE, [(i, i ^ m) for i in range(8)])  9.87 us
    all_to_all x2, waiting for transfers between devices, exchanged(): return lax.all_to_all(x, axes, split_axis=0, concat_axis=0, tiled=True)  8.68 us
    pallas_call x1, Pallas kernels, pairs(): on_core(pair_kernel, (jax.ShapeDtypeStruct((128, 128), BF16),) * 8 + (jax...  4.76 us
    ppermute x3, starting transfers between devices, partner(): return lax.ppermute(x, axis, [(0, 1), (1, 0)])  3.71 us
    pallas_call x1, Pallas kernels, firsts(): pl.pallas_call(first_kernel, out_shape=(jax.ShapeDtypeStruct((16, 128, 12...  2.31 us
  transfers between devices with their start and end apart: 19, of which 10 were waited for; matrix products, arithmetic and copies ran while one was open for 0% of the time, Pallas kernels for 5%

profile of v8, /device:TPU:8, one launch (start us, length us, event | category | flops | bytes accessed | tf_op | source)
XLA Modules:
  0.0 95.4 jit_solution(4955852972309090341)
XLA Ops:
  0.0 3.0 %collective-permute-start = (bf16[16,256]{1,0:T(8,128)(2,1)}, bf16[16,256]{1,0:T(8,128)(2,1)S(1)}, u32[]{:S(2)}, u32[]{:S(2)}) collective-permute-start(bf16[16,256]{1,0:T(8,128)(2,1)} %bitcast.9), channel_id=1, source_target_pairs={{0,1},{1,0},{2,3},{3,2},{4,5},{5,4},{6,7},{7,6},{8,9},{9,8},{10,11... | collective-permute-start | bytes 24584 | tf_op jit(solution)/shard_map/ppermute | solution.py:327
  3.0 2.3 %shard_map.82 = (bf16[16,128,128]{2,1,0:T(8,128)(2,1)}, bf16[4,128,256]{2,1,0:T(8,128)(2,1)}) custom-call(bf16[128,4,256]{2,1,0:T(4,128)(2,1)} %msa_hbm.1, bf16[32,256]{1,0:T(8,128)(2,1)} %bitcast.11), custom_call_target="tpu_custom_call" | custom-call | flops 1000000000 | bytes 3000000 | tf_op jit(solution)/shard_map/pallas_call | solution.py:63
  5.4 10.4 %all-to-all-start = ((bf16[16,128,128]{2,1,0:T(8,128)(2,1)}), bf16[16,128,128]{2,1,0:T(8,128)(2,1)S(1)}, u32[]{:S(2)}, u32[]{:S(2)}) async-start(bf16[16,128,128]{2,1,0:T(8,128)(2,1)} %get-tuple-element.34), calls=%async_computation | async-start | bytes 1048576 | tf_op jit(solution)/shard_map/all_to_all | solution.py:323
  17.1 0.9 shard_map.83
  18.1 1.6 %collective-permute-start.2 = (bf16[256,128]{1,0:T(8,128)(2,1)S(1)}, bf16[256,128]{1,0:T(8,128)(2,1)S(1)}, u32[]{:S(2)}, u32[]{:S(2)}) collective-permute-start(bf16[256,128]{1,0:T(8,128)(2,1)S(1)} %get-tuple-element.38), channel_id=1, source_target_pairs={{0,32},{2,34},{32,0},{34,2},{64,96},{66,98},{96,64},{98,66},{1,33}... | collective-permute-start | bytes 196616 | tf_op jit(solution)/shard_map/ppermute | solution.py:331
  20.2 1.4 %collective-permute-start.4 = (bf16[256,128]{1,0:T(8,128)(2,1)S(1)}, bf16[256,128]{1,0:T(8,128)(2,1)S(1)}, u32[]{:S(2)}, u32[]{:S(2)}) collective-permute-start(bf16[256,128]{1,0:T(8,128)(2,1)S(1)} %get-tuple-element.40), channel_id=1, source_target_pairs={{0,64},{2,66},{32,96},{34,98},{64,0},{66,2},{96,32},{98,34},{1,65}... | collective-permute-start | bytes 196616 | tf_op jit(solution)/shard_map/ppermute | solution.py:331
  22.6 2.7 %collective-permute-start.6 = (bf16[256,128]{1,0:T(8,128)(2,1)S(1)}, bf16[256,128]{1,0:T(8,128)(2,1)S(1)}, u32[]{:S(2)}, u32[]{:S(2)}) collective-permute-start(bf16[256,128]{1,0:T(8,128)(2,1)S(1)} %get-tuple-element.42), channel_id=1, source_target_pairs={{0,96},{2,98},{32,64},{34,66},{64,32},{66,34},{96,0},{98,2},{1,97}... | collective-permute-start | bytes 196616 | tf_op jit(solution)/shard_map/ppermute | solution.py:331
  25.4 1.0 %shard_map.84.rest_8_ = bf16[2048,256]{1,0:T(8,128)(2,1)S(1)} custom-call(s32[4]{0:T(128)S(1)} %pad_add_fusion.me_ref, bf16[512,128]{1,0:T(8,128)(2,1)S(1)} %copy-done.1, bf16[512,128]{1,0:T(8,128)(2,1)S(1)} %collective-permute-done.8.other_ref), custom_call_target="tpu_custom_call" | custom-call | flops 5000000000 | bytes 15000000 | tf_op jit(solution)/shard_map/pallas_call | solution.py:122
  27.2 4.4 %collective-permute-done.5.rest_5_ = bf16[256,128]{1,0:T(8,128)(2,1)S(1)} collective-permute-done((bf16[256,128]{1,0:T(8,128)(2,1)S(1)}, bf16[256,128]{1,0:T(8,128)(2,1)S(1)}, u32[]{:S(2)}, u32[]{:S(2)}) %collective-permute-start.5) | collective-permute-done | bytes 65568 | tf_op jit(solution)/shard_map/ppermute | solution.py:331
  31.6 1.0 %all-to-all-done.right_ref = bf16[16,128,128]{2,1,0:T(8,128)(2,1)S(1)} async-done(((bf16[16,128,128]{2,1,0:T(8,128)(2,1)}), bf16[16,128,128]{2,1,0:T(8,128)(2,1)S(1)}, u32[]{:S(2)}, u32[]{:S(2)}) %all-to-all-start) | async-done | bytes 524320 | tf_op jit(solution)/shard_map/all_to_all | solution.py:323
  32.6 4.8 %shard_map.85 = (bf16[128,128]{1,0:T(8,128)(2,1)S(1)}, bf16[128,128]{1,0:T(8,128)(2,1)S(1)}, bf16[128,128]{1,0:T(8,128)(2,1)S(1)}, bf16[128,128]{1,0:T(8,128)(2,...) custom-call(s32[4]{0:T(128)S(1)} %pad_add_fusion.me_ref, ...), custom_call_target="tpu_custom_call" | custom-call | flops 5000000000 | bytes 15000000 | tf_op jit(solution)/shard_map/pallas_call | solution.py:182
  37.4 12.3 %all-to-all-start.1 = ((bf16[128,16,128]{2,1,0:T(8,128)(2,1)}), bf16[128,16,128]{2,1,0:T(8,128)(2,1)S(1)}, u32[]{:S(2)}, u32[]{:S(2)}) async-start(bf16[128,16,128]{2,1,0:T(8,128)(2,1)} %get-tuple-element.56), calls=%async_computation.1 | async-start | bytes 1048576 | tf_op jit(solution)/shard_map/all_to_all | solution.py:323
  49.8 1.8 %collective-permute-start.10 = (bf16[128,128]{1,0:T(8,128)(2,1)S(1)}, bf16[128,128]{1,0:T(8,128)(2,1)S(1)}, u32[]{:S(2)}, u32[]{:S(2)}) collective-permute-start(bf16[128,128]{1,0:T(8,128)(2,1)S(1)} %get-tuple-element.47), channel_id=1, source_target_pairs={{0,32},{2,34},{32,0},{34,2},{64,96},{66,98},{96,64},{98,66},{1,33}... | collective-permute-start | bytes 98312 | tf_op jit(solution)/shard_map/ppermute | solution.py:331
  52.4 1.1 %collective-permute-start.13 = (bf16[128,128]{1,0:T(8,128)(2,1)S(1)}, bf16[128,128]{1,0:T(8,128)(2,1)S(1)}, u32[]{:S(2)}, u32[]{:S(2)}) collective-permute-start(bf16[128,128]{1,0:T(8,128)(2,1)S(1)} %get-tuple-element.50), channel_id=1, source_target_pairs={{0,66},{2,64},{32,98},{34,96},{64,2},{66,0},{96,34},{98,32},{1,67}... | collective-permute-start | bytes 98312 | tf_op jit(solution)/shard_map/ppermute | solution.py:331
  53.5 1.4 %collective-permute-start.14 = (bf16[128,128]{1,0:T(8,128)(2,1)S(1)}, bf16[128,128]{1,0:T(8,128)(2,1)S(1)}, u32[]{:S(2)}, u32[]{:S(2)}) collective-permute-start(bf16[128,128]{1,0:T(8,128)(2,1)S(1)} %get-tuple-element.51), channel_id=1, source_target_pairs={{0,96},{2,98},{32,64},{34,66},{64,32},{66,34},{96,0},{98,2},{1,97}... | collective-permute-start | bytes 98312 | tf_op jit(solution)/shard_map/ppermute | solution.py:331
  54.9 1.1 %collective-permute-start.15 = (bf16[128,128]{1,0:T(8,128)(2,1)S(1)}, bf16[128,128]{1,0:T(8,128)(2,1)S(1)}, u32[]{:S(2)}, u32[]{:S(2)}) collective-permute-start(bf16[128,128]{1,0:T(8,128)(2,1)S(1)} %get-tuple-element.52), channel_id=1, source_target_pairs={{0,98},{2,96},{32,66},{34,64},{64,34},{66,32},{96,2},{98,0},{1,99}... | collective-permute-start | bytes 98312 | tf_op jit(solution)/shard_map/ppermute | solution.py:331
  56.9 2.0 %collective-permute-done.14.rest_6_ = bf16[128,128]{1,0:T(8,128)(2,1)S(1)} collective-permute-done((bf16[128,128]{1,0:T(8,128)(2,1)S(1)}, bf16[128,128]{1,0:T(8,128)(2,1)S(1)}, u32[]{:S(2)}, u32[]{:S(2)}) %collective-permute-start.14) | collective-permute-done | bytes 32800 | tf_op jit(solution)/shard_map/ppermute | solution.py:331
  58.9 1.1 %collective-permute-done.15.rest_7_ = bf16[128,128]{1,0:T(8,128)(2,1)S(1)} collective-permute-done((bf16[128,128]{1,0:T(8,128)(2,1)S(1)}, bf16[128,128]{1,0:T(8,128)(2,1)S(1)}, u32[]{:S(2)}, u32[]{:S(2)}) %collective-permute-start.15) | collective-permute-done | bytes 32800 | tf_op jit(solution)/shard_map/ppermute | solution.py:331
  60.0 1.1 %shard_map.86 = (f32[1024,128]{1,0:T(8,128)S(1)}, f32[1024,128]{1,0:T(8,128)S(1)}) custom-call(s32[4]{0:T(128)S(1)} %pad_add_fusion.me_ref, bf16[128,128]{1,0:T(8,128)(2,1)S(1)} %get-tuple-element.45.rest_0_, bf16[128,128]{1,0:T(8,128)(2,1)S(1)} %collective-permute-done.9.rest_1_, bf16[128,128]{1,0:T(8,128)(2,1)S(1)} %collective-permute-done.10.rest_2_, ...), custom_call_target="tpu_custom_call" | custom-call | flops 2000000000 | bytes 6000000 | tf_op jit(solution)/shard_map/pallas_call | solution.py:286
  61.0 7.7 %all-to-all-done.1.cols_ref = bf16[128,16,128]{2,1,0:T(8,128)(2,1)S(1)} async-done(((bf16[128,16,128]{2,1,0:T(8,128)(2,1)}), bf16[128,16,128]{2,1,0:T(8,128)(2,1)S(1)}, u32[]{:S(2)}, u32[]{:S(2)}) %all-to-all-start.1) | async-done | bytes 524320 | tf_op jit(solution)/shard_map/all_to_all | solution.py:323
  68.7 1.8 %shard_map.87 = (f32[128,8,128]{2,1,0:T(8,128)S(1)}, bf16[128,8,128]{2,1,0:T(8,128)(2,1)S(1)}) custom-call(s32[4]{0:T(128)S(1)} %pad_add_fusion.me_ref, bf16[128,16,128]{2,1,0:T(8,128)(2,1)S(1)} %all-to-all-done.1.cols_ref), custom_call_target="tpu_custom_call" | custom-call | flops 3000000000 | bytes 9000000 | tf_op jit(solution)/shard_map/pallas_call | solution.py:249
  70.6 1.5 %collective-permute-done.16 = bf16[128,8,128]{2,1,0:T(8,128)(2,1)S(1)} collective-permute-done((bf16[128,8,128]{2,1,0:T(8,128)(2,1)S(1)}, bf16[128,8,128]{2,1,0:T(8,128)(2,1)S(1)}, u32[]{:S(2)}, u32[]{:S(2)}) %collective-permute-start.16) | collective-permute-done | bytes 262176 | tf_op jit(solution)/shard_map/ppermute | solution.py:327
  72.2 21.6 %all_to_all.15.mixed_ref = bf16[128,8,128]{2,1,0:T(8,128)(2,1)S(1)} all-to-all(bf16[128,8,128]{2,1,0:T(8,128)(2,1)S(1)} %add_convert_fusion), channel_id=1, replica_groups=mesh['yh'=2,'yl'=2,'xl'=2,'z'=8,'core'=2,'xh'=2] {'yh','yl','xl','z','xh'}, dimensions={0} | all-to-all | bytes 524288 | tf_op jit(solution)/shard_map/all_to_all | solution.py:323
  93.8 1.6 %shard_map.88 = bf16[1024,128]{1,0:T(8,128)(2,1)} custom-call(bf16[128,8,128]{2,1,0:T(8,128)(2,1)S(1)} %all_to_all.15.mixed_ref, f32[1024,128]{1,0:T(8,128)S(1)} %get-tuple-element.59.gate_ref, f32[1024,128]{1,0:T(8,128)S(1)} %get-tuple-element.60.base_ref, bf16[128,128]{1,0:T(8,128)(2,1)S(1)} %copy-done.3), custom_call_target="tpu_custom_call" | custom-call | flops 2000000000 | bytes 6000000 | tf_op jit(solution)/shard_map/pallas_call | solution.py:313
  (39 shorter events, 5.7 us)
Async XLA Ops:
  0.0 16.5 %collective-permute-start = (bf16[16,256]{1,0:T(8,128)(2,1)}, bf16[16,256]{1,0:T(8,128)(2,1)S(1)}, u32[]{:S(2)}, u32[]{:S(2)}) collective-permute-start(bf16[16,256]{1,0:T(8,128)(2,1)} %bitcast.9), channel_id=1, source_target_pairs={{0,1},{1,0},{2,3},{3,2},{4,5},{5,4},{6,7},{7,6},{8,9},{9,8},{10,11... | collective-permute-start | bytes 24584 | tf_op jit(solution)/shard_map/ppermute | solution.py:327
  5.3 10.5 %copy-start.1 = (bf16[512,128]{1,0:T(8,128)(2,1)S(1)}, bf16[512,128]{1,0:T(8,128)(2,1)}, u32[]{:S(2)}) copy-start(bf16[512,128]{1,0:T(8,128)(2,1)} %own_ref) | copy-start | bytes 393220
  5.4 11.2 %copy-start = (bf16[4,256,128]{2,1,0:T(8,128)(2,1)S(1)}, bf16[4,256,128]{2,1,0:T(8,128)(2,1)}, u32[]{:S(2)}) copy-start(bf16[4,256,128]{2,1,0:T(8,128)(2,1)} %couple_ref.1) | copy-start | bytes 786436
  5.4 11.2 %copy-start.5 = (bf16[4,128,256]{2,1,0:T(8,128)(2,1)S(1)}, bf16[4,128,256]{2,1,0:T(8,128)(2,1)}, u32[]{:S(2)}) copy-start(bf16[4,128,256]{2,1,0:T(8,128)(2,1)} %get-tuple-element.35.norm_ref) | copy-start | bytes 786436
  5.4 27.2 %all-to-all-start = ((bf16[16,128,128]{2,1,0:T(8,128)(2,1)}), bf16[16,128,128]{2,1,0:T(8,128)(2,1)S(1)}, u32[]{:S(2)}, u32[]{:S(2)}) async-start(bf16[16,128,128]{2,1,0:T(8,128)(2,1)} %get-tuple-element.34), calls=%async_computation | async-start | bytes 1048576 | tf_op jit(solution)/shard_map/all_to_all | solution.py:323
  15.8 9.5 %collective-permute-start.8 = (bf16[512,128]{1,0:T(8,128)(2,1)S(1)}, bf16[512,128]{1,0:T(8,128)(2,1)S(1)}, u32[]{:S(2)}, u32[]{:S(2)}) collective-permute-start(bf16[512,128]{1,0:T(8,128)(2,1)S(1)} %copy-done.1), channel_id=1, source_target_pairs={{0,1},{1,0},{2,3},{3,2},{4,5},{5,4},{6,7},{7,6},{8,9},{9,8},{10,11... | collective-permute-start | bytes 393224 | tf_op jit(solution)/shard_map/ppermute | solution.py:327
  18.0 3.6 %collective-permute-start.1 = (bf16[256,128]{1,0:T(8,128)(2,1)S(1)}, bf16[256,128]{1,0:T(8,128)(2,1)S(1)}, u32[]{:S(2)}, u32[]{:S(2)}) collective-permute-start(bf16[256,128]{1,0:T(8,128)(2,1)S(1)} %get-tuple-element.37), channel_id=1, source_target_pairs={{0,2},{2,0},{32,34},{34,32},{64,66},{66,64},{96,98},{98,96},{1,3},... | collective-permute-start | bytes 196616 | tf_op jit(solution)/shard_map/ppermute | solution.py:331
  18.1 4.5 %collective-permute-start.2 = (bf16[256,128]{1,0:T(8,128)(2,1)S(1)}, bf16[256,128]{1,0:T(8,128)(2,1)S(1)}, u32[]{:S(2)}, u32[]{:S(2)}) collective-permute-start(bf16[256,128]{1,0:T(8,128)(2,1)S(1)} %get-tuple-element.38), channel_id=1, source_target_pairs={{0,32},{2,34},{32,0},{34,2},{64,96},{66,98},{96,64},{98,66},{1,33}... | collective-permute-start | bytes 196616 | tf_op jit(solution)/shard_map/ppermute | solution.py:331
  19.8 6.5 %collective-permute-start.3 = (bf16[256,128]{1,0:T(8,128)(2,1)S(1)}, bf16[256,128]{1,0:T(8,128)(2,1)S(1)}, u32[]{:S(2)}, u32[]{:S(2)}) collective-permute-start(bf16[256,128]{1,0:T(8,128)(2,1)S(1)} %get-tuple-element.39), channel_id=1, source_target_pairs={{0,34},{2,32},{32,2},{34,0},{64,98},{66,96},{96,66},{98,64},{1,35}... | collective-permute-start | bytes 196616 | tf_op jit(solution)/shard_map/ppermute | solution.py:331
  20.2 7.0 %collective-permute-start.4 = (bf16[256,128]{1,0:T(8,128)(2,1)S(1)}, bf16[256,128]{1,0:T(8,128)(2,1)S(1)}, u32[]{:S(2)}, u32[]{:S(2)}) collective-permute-start(bf16[256,128]{1,0:T(8,128)(2,1)S(1)} %get-tuple-element.40), channel_id=1, source_target_pairs={{0,64},{2,66},{32,96},{34,98},{64,0},{66,2},{96,32},{98,34},{1,65}... | collective-permute-start | bytes 196616 | tf_op jit(solution)/shard_map/ppermute | solution.py:331
  21.6 10.0 %collective-permute-start.5 = (bf16[256,128]{1,0:T(8,128)(2,1)S(1)}, bf16[256,128]{1,0:T(8,128)(2,1)S(1)}, u32[]{:S(2)}, u32[]{:S(2)}) collective-permute-start(bf16[256,128]{1,0:T(8,128)(2,1)S(1)} %get-tuple-element.41), channel_id=1, source_target_pairs={{0,66},{2,64},{32,98},{34,96},{64,2},{66,0},{96,34},{98,32},{1,67}... | collective-permute-start | bytes 196616 | tf_op jit(solution)/shard_map/ppermute | solution.py:331
  22.6 9.0 %collective-permute-start.6 = (bf16[256,128]{1,0:T(8,128)(2,1)S(1)}, bf16[256,128]{1,0:T(8,128)(2,1)S(1)}, u32[]{:S(2)}, u32[]{:S(2)}) collective-permute-start(bf16[256,128]{1,0:T(8,128)(2,1)S(1)} %get-tuple-element.42), channel_id=1, source_target_pairs={{0,96},{2,98},{32,64},{34,66},{64,32},{66,34},{96,0},{98,2},{1,97}... | collective-permute-start | bytes 196616 | tf_op jit(solution)/shard_map/ppermute | solution.py:331
  25.4 6.2 %collective-permute-start.7 = (bf16[256,128]{1,0:T(8,128)(2,1)S(1)}, bf16[256,128]{1,0:T(8,128)(2,1)S(1)}, u32[]{:S(2)}, u32[]{:S(2)}) collective-permute-start(bf16[256,128]{1,0:T(8,128)(2,1)S(1)} %get-tuple-element.43), channel_id=1, source_target_pairs={{0,98},{2,96},{32,66},{34,64},{64,34},{66,32},{96,2},{98,0},{1,99}... | collective-permute-start | bytes 196616 | tf_op jit(solution)/shard_map/ppermute | solution.py:331
  37.4 22.6 %copy-start.2 = (bf16[128,128]{1,0:T(8,128)(2,1)S(1)}, bf16[128,128]{1,0:T(8,128)(2,1)}, u32[]{:S(2)}) copy-start(bf16[128,128]{1,0:T(8,128)(2,1)} %rest_8_.1) | copy-start | bytes 98308
  37.4 31.4 %all-to-all-start.1 = ((bf16[128,16,128]{2,1,0:T(8,128)(2,1)}), bf16[128,16,128]{2,1,0:T(8,128)(2,1)S(1)}, u32[]{:S(2)}, u32[]{:S(2)}) async-start(bf16[128,16,128]{2,1,0:T(8,128)(2,1)} %get-tuple-element.56), calls=%async_computation.1 | async-start | bytes 1048576 | tf_op jit(solution)/shard_map/all_to_all | solution.py:323
  49.7 3.9 %collective-permute-start.9 = (bf16[128,128]{1,0:T(8,128)(2,1)S(1)}, bf16[128,128]{1,0:T(8,128)(2,1)S(1)}, u32[]{:S(2)}, u32[]{:S(2)}) collective-permute-start(bf16[128,128]{1,0:T(8,128)(2,1)S(1)} %get-tuple-element.46), channel_id=1, source_target_pairs={{0,2},{2,0},{32,34},{34,32},{64,66},{66,64},{96,98},{98,96},{1,3},... | collective-permute-start | bytes 98312 | tf_op jit(solution)/shard_map/ppermute | solution.py:331
  49.8 5.1 %collective-permute-start.10 = (bf16[128,128]{1,0:T(8,128)(2,1)S(1)}, bf16[128,128]{1,0:T(8,128)(2,1)S(1)}, u32[]{:S(2)}, u32[]{:S(2)}) collective-permute-start(bf16[128,128]{1,0:T(8,128)(2,1)S(1)} %get-tuple-element.47), channel_id=1, source_target_pairs={{0,32},{2,34},{32,0},{34,2},{64,96},{66,98},{96,64},{98,66},{1,33}... | collective-permute-start | bytes 98312 | tf_op jit(solution)/shard_map/ppermute | solution.py:331
  51.6 4.4 %collective-permute-start.11 = (bf16[128,128]{1,0:T(8,128)(2,1)S(1)}, bf16[128,128]{1,0:T(8,128)(2,1)S(1)}, u32[]{:S(2)}, u32[]{:S(2)}) collective-permute-start(bf16[128,128]{1,0:T(8,128)(2,1)S(1)} %get-tuple-element.48), channel_id=1, source_target_pairs={{0,34},{2,32},{32,2},{34,0},{64,98},{66,96},{96,66},{98,64},{1,35}... | collective-permute-start | bytes 98312 | tf_op jit(solution)/shard_map/ppermute | solution.py:331
  51.7 4.7 %collective-permute-start.12 = (bf16[128,128]{1,0:T(8,128)(2,1)S(1)}, bf16[128,128]{1,0:T(8,128)(2,1)S(1)}, u32[]{:S(2)}, u32[]{:S(2)}) collective-permute-start(bf16[128,128]{1,0:T(8,128)(2,1)S(1)} %get-tuple-element.49), channel_id=1, source_target_pairs={{0,64},{2,66},{32,96},{34,98},{64,0},{66,2},{96,32},{98,34},{1,65}... | collective-permute-start | bytes 98312 | tf_op jit(solution)/shard_map/ppermute | solution.py:331
  52.4 4.4 %collective-permute-start.13 = (bf16[128,128]{1,0:T(8,128)(2,1)S(1)}, bf16[128,128]{1,0:T(8,128)(2,1)S(1)}, u32[]{:S(2)}, u32[]{:S(2)}) collective-permute-start(bf16[128,128]{1,0:T(8,128)(2,1)S(1)} %get-tuple-element.50), channel_id=1, source_target_pairs={{0,66},{2,64},{32,98},{34,96},{64,2},{66,0},{96,34},{98,32},{1,67}... | collective-permute-start | bytes 98312 | tf_op jit(solution)/shard_map/ppermute | solution.py:331
  53.5 5.3 %collective-permute-start.14 = (bf16[128,128]{1,0:T(8,128)(2,1)S(1)}, bf16[128,128]{1,0:T(8,128)(2,1)S(1)}, u32[]{:S(2)}, u32[]{:S(2)}) collective-permute-start(bf16[128,128]{1,0:T(8,128)(2,1)S(1)} %get-tuple-element.51), channel_id=1, source_target_pairs={{0,96},{2,98},{32,64},{34,66},{64,32},{66,34},{96,0},{98,2},{1,97}... | collective-permute-start | bytes 98312 | tf_op jit(solution)/shard_map/ppermute | solution.py:331
  54.9 5.1 %collective-permute-start.15 = (bf16[128,128]{1,0:T(8,128)(2,1)S(1)}, bf16[128,128]{1,0:T(8,128)(2,1)S(1)}, u32[]{:S(2)}, u32[]{:S(2)}) collective-permute-start(bf16[128,128]{1,0:T(8,128)(2,1)S(1)} %get-tuple-element.52), channel_id=1, source_target_pairs={{0,98},{2,96},{32,66},{34,64},{64,34},{66,32},{96,2},{98,0},{1,99}... | collective-permute-start | bytes 98312 | tf_op jit(solution)/shard_map/ppermute | solution.py:331
  70.5 1.6 %collective-permute-start.16 = (bf16[128,8,128]{2,1,0:T(8,128)(2,1)S(1)}, bf16[128,8,128]{2,1,0:T(8,128)(2,1)S(1)}, u32[]{:S(2)}, u32[]{:S(2)}) collective-permute-start(bf16[128,8,128]{2,1,0:T(8,128)(2,1)S(1)} %get-tuple-element.58), channel_id=1, source_target_pairs={{0,2},{2,0},{1,3},{3,1},{4,6},{6,4},{5,7},{7,5},{8,10},{10,8},{9,1... | collective-permute-start | bytes 786440 | tf_op jit(solution)/shard_map/ppermute | solution.py:327
  72.2 21.6 %copy-start.3 = (bf16[128,128]{1,0:T(8,128)(2,1)S(1)}, bf16[128,128]{1,0:T(8,128)(2,1)}, u32[]{:S(2)}) copy-start(bf16[128,128]{1,0:T(8,128)(2,1)} %w_ref.1) | copy-start | bytes 98308
  (2 other events, 3.3 us)
